TPU v7x, 32 devices: a whole 2x2x4 slice. The times are simulated.
32 devices in a mesh: rep: 4 (over x, core), stripe: 8 (over z, y).
Axes of the slice: x: 2, y: 2, z: 4, core: 2. Of those that a mesh axis runs over, the one named last changes fastest.
Arguments:
- activations: bfloat16 [1024, 1024], P('rep'), may hold values from -6 to 6
- out_grads: bfloat16 [1024, 4096], P('rep', 'stripe'), may hold values from -4 to 4
- statistics: float32 [4, 8, 512, 512], P('rep', 'stripe'), may hold values from -48 to 4608, as said below
- owner_blocks: int32 [8, 2], P('stripe'), may hold values from 0 to 1, each once within a row
Outputs:
- preconditioned: float32 [1024, 4096], P(None, 'stripe')
- new_stats: float32 [4, 8, 512, 512], P('rep', 'stripe')
Inputs may be any that keep to these rules, and one draw needn't show every extreme that they name: statistics[p, s] is symmetric positive definite for every p and s. `owner_blocks`: each row lists every row block 0 to 1 exactly once.
All inputs are finite; a program needn't handle non-finite values.
Results may differ from a plain program's by a relative error of at most 0.0003.
Values sent between devices are 32-bit elements; how exact they have to be, the bound alone decides.
No kernel may reach another device: no remote copies, remote signals or barrier semaphores. Data moves between devices by JAX's collectives and lax.ppermute only.
A program may use at most 128 MiB of HBM per device.

v0:
```python
import functools
import math

import jax
import jax.numpy as jnp
from jax import lax
from jax.experimental import pallas as pl
from jax.experimental.pallas import tpu as pltpu
from jax.sharding import PartitionSpec as P


BLOCK = 512
HALF = BLOCK // 2
PACKED = HALF + 8
CHUNK = 64
MOST = HALF - 64

decay_rate = 0.95
damping = 0.25
epsilon = 1e-06
AXES = ("rep", "stripe")
f32 = jnp.float32
bf16 = jnp.bfloat16

ROOT_COEFFS = (
    25 / 16,
    -5 / 16 - 3125 / 4096,
    3125 / 4096,
    -1250 / 4096,
    250 / 4096,
    -25 / 4096,
    1 / 4096,
)
SMALL_CUBIC = (-1 / 32, 9 / 16, -3 / 2, 1.0)


def quotient(poly, divisor):
    rest, out = list(poly), []
    for i in range(len(poly) - len(divisor), -1, -1):
        out.insert(0, rest[i + len(divisor) - 1])
        for n, d in enumerate(divisor):
            rest[i + n] -= out[0] * d
    return out, rest[: len(divisor) - 1]


ROOT_FACTOR, ROOT_REST = quotient(ROOT_COEFFS, SMALL_CUBIC)

VMEM = pl.BlockSpec(memory_space=pltpu.VMEM)
SMEM = pl.BlockSpec(memory_space=pltpu.SMEM)
HBM = pl.BlockSpec(memory_space=pltpu.HBM)
LOW = pl.ds(0, HALF)
TOP = pl.ds(HALF, HALF)


def call(body, out_shapes, in_specs, scratch=(), limit=16, flops=0, out_specs=None, **kwargs):
    return pl.pallas_call(
        body,
        out_shape=[jax.ShapeDtypeStruct(s, f32) if isinstance(s, tuple) else s for s in out_shapes],
        in_specs=in_specs,
        out_specs=out_specs or [VMEM] * len(out_shapes),
        scratch_shapes=list(scratch),
        compiler_params=pltpu.CompilerParams(vmem_limit_bytes=limit << 20),
        cost_estimate=pl.CostEstimate(flops=flops, bytes_accessed=1 << 20, transcendentals=0),
        **kwargs,
    )


def flip(x, mask):
    return lax.ppermute(x, "rep", [(i, i ^ mask) for i in range(lax.axis_size("rep"))])


def in_hbm(x):
    return pltpu.with_memory_space_constraint(x, pltpu.HBM)


def chip_core():
    me = lax.axis_index("rep")
    return lax.shift_right_logical(me, 1), lax.bitwise_and(me, 1)


def split(x):
    hi = x.astype(bf16)
    return hi, (x - hi.astype(f32)).astype(bf16)


def mm(a, b):
    return jnp.dot(a, b, preferred_element_type=f32)


def dot3(a, b):
    return mm(a[0], b[0]) + (mm(a[0], b[1]) + mm(a[1], b[0]))


def triangle():
    i = lax.broadcasted_iota(jnp.int32, (HALF, HALF), 0)
    j = lax.broadcasted_iota(jnp.int32, (HALF, HALF), 1)
    return i, j


def lanes(x):
    rows = jnp.sum(x, axis=0, keepdims=True)
    return sum(rows[:, k : k + 128] for k in range(0, x.shape[1], 128))


def pack_into(out, a, b, c):
    i, j = triangle()
    out[LOW, LOW] = jnp.where(i <= j, a, c)
    out[LOW, TOP] = b
    out[HALF:, LOW] = jnp.broadcast_to(jnp.sum(jnp.where(i == j, c, 0.0), axis=0, keepdims=True), (8, HALF))


def unpack(u, diag):
    i, j = triangle()
    ut = u.T
    return jnp.where(i <= j, u, ut), jnp.where(i > j, u, jnp.where(i < j, ut, diag))


def pack_stat(pairs, stat, owners, out, trace, rows):
    chip, core = chip_core()
    for n in range(2 * pairs):
        half = core if n < pairs else 1 - core
        row = owners[0, lax.bitwise_xor(chip, jnp.int32(n % pairs))] * BLOCK + half * HALF
        rows[n : n + 1, :] = jnp.full((1, 128), row.astype(f32))
    i, j = triangle()
    a, c = stat[LOW, LOW], stat[TOP, TOP]
    pack_into(out, a, stat[LOW, TOP], c)
    trace[...] = lanes(jnp.where(i == j, a + c, 0.0))


def grad_terms(plan, acts, grads, owners, *refs):
    outs, (av, gv, ov, sems) = refs[: len(plan)], refs[len(plan) :]
    chip, core = chip_core()
    parts = [(owners, ov)]
    for src, dst in ((grads, gv), (acts, av)):
        parts += [(src.at[pl.ds(r, CHUNK)], dst.at[pl.ds(r, CHUNK)]) for r in range(0, src.shape[0], CHUNK)]
    copies = [pltpu.make_async_copy(src, dst, sems.at[k]) for k, (src, dst) in enumerate(parts)]
    for copy in copies:
        copy.start()
    for copy in copies:
        copy.wait()
    cotangent = gv[...]
    for out, (chips, swapped) in zip(outs, plan):
        half = 1 - core if swapped else core
        for n, j in enumerate(chips):
            start = ov[0, chip ^ j] * BLOCK + half * HALF
            cols = av[:, pl.ds(pl.multiple_of(start, HALF), HALF)]
            out[n] = lax.dot_general(cols, cotangent, (((0,), (0,)), ((), ())), preferred_element_type=f32)


def finish_half(devices, keep, got, rest, trace, half, sums):
    value = keep[0] + got[0] + rest[...]
    half[LOW] = value
    half[HALF:] = jnp.zeros((PACKED - HALF, BLOCK), f32)
    both = jnp.concatenate([lanes(value * value), trace[...]], axis=0)
    sums[...] = jnp.broadcast_to(both[None], (devices, 2, 128))


def spread(top, corner, out):
    out[0, LOW], out[1, LOW] = split(top)
    out[0, TOP, TOP], out[1, TOP, TOP] = split(corner)
    for k in range(2):
        out[k, TOP, LOW] = out[k, LOW, TOP].T


def upper_product(a, b):
    top = dot3((a[0, LOW], a[1, LOW]), (b[0], b[1]))
    return top, dot3((a[0, TOP], a[1, TOP]), (b[0, :, TOP], b[1, :, TOP]))


def total(x):
    return jnp.sum(jnp.sum(x, axis=0, keepdims=True), axis=1, keepdims=True)


def load_gradient(core, half, other, g):
    mine = pl.ds(pl.multiple_of(core * HALF, HALF), HALF)
    theirs = pl.ds(pl.multiple_of(HALF - core * HALF, HALF), HALF)
    for rows, src in ((mine, half), (theirs, other)):
        g[0, rows], g[1, rows] = split(src[LOW])


def unpack_upper(packed):
    s00, s11 = unpack(packed[LOW, LOW], packed[HALF : HALF + 1, LOW])
    return jnp.concatenate([s00, packed[LOW, TOP]], axis=1), s11


def update_stat(half, other, old, facts, square_out, cube_out, out, g_out, g, s1, s2, sem):
    _, core = chip_core()
    load_gradient(core, half, other, g.at[0])
    copy = pltpu.make_async_copy(g.at[0], g_out, sem)
    copy.start()
    for k in range(2):
        g[1, k] = g[0, k].T
    top, corner = upper_product(g.at[1 - core], g.at[core])
    was_top, was_corner = unpack_upper(old)
    top = decay_rate * was_top + top
    corner = decay_rate * was_corner + corner
    s00, s01 = top[:, :HALF], top[:, HALF:]
    pack_into(out, s00, s01, corner)
    i, j = triangle()
    trace = total(jnp.where(i == j, s00 + corner, 0.0))
    norm_sq = total(s00 * s00 + corner * corner + 2.0 * (s01 * s01))
    inv = 1.0 / jnp.sqrt(norm_sq + epsilon)
    spread(top * inv, corner * inv, s1)
    top, corner = upper_product(s1, s1)
    pack_into(square_out, top[:, :HALF], top[:, HALF:], corner)
    spread(top, corner, s2)
    top, corner = upper_product(s1, s2)
    pack_into(cube_out, top[:, :HALF], top[:, HALF:], corner)
    facts[...] = jnp.concatenate([jnp.broadcast_to(x, (1, 128)) for x in (norm_sq, trace)], axis=0)
    copy.wait()


def coefficients(devices, facts, sums):
    both = jnp.sum(jnp.sum(sums[...], axis=0), axis=1, keepdims=True)
    grad_sq, trace_all = both[0:1], both[1:2]
    shift = (decay_rate * trace_all + 2.0 * grad_sq) * (damping / (devices * BLOCK))
    shift = jnp.broadcast_to(shift, (1, 128))
    norm_sq, trace = facts[0:1, :], facts[1:2, :]
    frob = jnp.sqrt(norm_sq + 2.0 * shift * trace + BLOCK * shift * shift + epsilon)
    a = jnp.sqrt(norm_sq + epsilon) / frob
    e = shift / frob

    def taken(poly, outer):
        out = []
        for i in range(len(poly)):
            value = jnp.full_like(e, poly[-1] * math.comb(len(poly) - 1, i))
            for j in range(len(poly) - 2, i - 1, -1):
                value = value * e + math.comb(j, i) * poly[j]
            out.append((outer * value)[:, 0:1])
            outer = outer * a
        return out

    outer = 1.0 / jnp.sqrt(jnp.sqrt(frob))
    return taken(SMALL_CUBIC, jnp.ones_like(e)), taken(ROOT_FACTOR, outer), taken(ROOT_REST, outer), grad_sq


def root(devices, stat, g_in, square, cubed, facts, sums, out, totals, g, left, right, sem):
    fetch = pltpu.make_async_copy(g_in, g, sem)
    fetch.start()
    small, factor, rest, grad_sq = coefficients(devices, facts, sums)
    inv = 1.0 / jnp.sqrt(facts[0:1, 0:1] + epsilon)
    i, j = triangle()
    on_diagonal = i == j

    def polynomial(k, powers, part):
        value = sum(k[n] * powers[n - 1][part] for n in range(1, len(k)))
        if part == 1:
            return value + jnp.where(on_diagonal, k[0], 0.0)
        return jnp.concatenate([value[:, :HALF] + jnp.where(on_diagonal, k[0], 0.0), value[:, HALF:]], axis=1)

    powers = [[x * inv for x in unpack_upper(stat)], unpack_upper(square), unpack_upper(cubed)]
    for dst, k in ((left, small), (right, factor)):
        dst[LOW] = polynomial(k, powers, 0).astype(bf16)
        dst[TOP, TOP] = polynomial(k, powers, 1).astype(bf16)
        dst[TOP, LOW] = dst[LOW, TOP].T
    out[LOW] = mm(left[LOW], right[...]) + polynomial(rest, powers, 0)
    corner = mm(left[TOP], right[:, TOP]) + polynomial(rest, powers, 1)
    out[HALF:, LOW] = corner[: HALF // 2]
    out[HALF:, TOP] = corner[HALF // 2 :]
    totals[...] = jnp.broadcast_to(grad_sq, (1, 128))
    fetch.wait()


def root_corner(packed):
    return jnp.concatenate([packed[HALF:, LOW], packed[HALF:, TOP]], axis=0)


def half_way(g, packed, out, x):
    _, core = chip_core()
    spread(packed[LOW], root_corner(packed), x)

    @pl.when(core == 1)
    def _():
        y = dot3((x[0, TOP], x[1, TOP]), (g[0], g[1]))
        out[0, LOW], out[1, LOW] = split(y)

    @pl.when(core == 0)
    def _():
        out[0], out[1] = split(dot3((g[0], g[1]), (x[0], x[1])))


def last_product(middle, packed, mine, most, rest, sums, x):
    _, core = chip_core()

    @pl.when(core == 1)
    def _():
        spread(packed[LOW], root_corner(packed), x)
        mine[...] = dot3((middle[0, LOW], middle[1, LOW]), (x[0], x[1]))

    @pl.when(core == 0)
    def _():
        mine[...] = dot3(split(packed[LOW]), (middle[0], middle[1]))

    most[...], rest[...] = mine[:MOST], mine[MOST:]
    sums[...] = jnp.broadcast_to(lanes(mine[...] * mine[...])[None], sums.shape)


def unpack_stat(packed, out):
    sa, sc = unpack(packed[LOW, LOW], packed[HALF : HALF + 1, LOW])
    off = packed[LOW, TOP]
    out[LOW, LOW] = sa
    out[LOW, TOP] = off
    out[TOP, LOW] = off.T
    out[TOP, TOP] = sc


def write_pieces(pieces, scale, out, scaled, sems):
    copies, base = [], 0
    for first, src in pieces:
        for r in range(0, src.shape[0], CHUNK):
            here = pl.ds(base + r, CHUNK)
            scaled[here] = src[pl.ds(r, CHUNK)] * scale
            start = pl.multiple_of(first + r, CHUNK)
            copies.append(pltpu.make_async_copy(scaled.at[here], out.at[pl.ds(start, CHUNK)], sems.at[len(copies)]))
            copies[-1].start()
        base += src.shape[0]
    for copy in copies:
        copy.wait()


def first_row(rows, n):
    return jnp.max(rows[n : n + 1, :]).astype(jnp.int32)


def place_first(plan, *refs):
    found, (sums, totals, rows, out, scale, scaled, sems) = refs[: len(plan)], refs[len(plan) :]
    prec_sq = jnp.sum(jnp.sum(sums[...], axis=0), axis=1, keepdims=True)
    factor = jnp.sqrt(totals[0:1, 0:1] / (prec_sq + epsilon))
    scale[...] = jnp.broadcast_to(factor, (1, 128))
    write_pieces([(first_row(rows, n) + r, x) for (n, r), x in zip(plan, found)], factor, out, scaled, sems)


def place_next(plan, *refs):
    found, (scale, rows, _, out, scaled, sems) = refs[: len(plan)], refs[len(plan) :]
    write_pieces(
        [(first_row(rows, n) + r, x) for (n, r), x in zip(plan, found)], scale[0:1, 0:1], out, scaled, sems
    )


def per_device(activations, out_grads, statistics, owner_blocks):
    rep_count = lax.axis_size("rep")
    pairs = rep_count // 2
    devices = rep_count * lax.axis_size("stripe")
    stripes = lax.axis_size("stripe")
    tokens = activations.shape[0]
    piece, square = (HALF, BLOCK), (BLOCK, BLOCK)
    unit = 6 * BLOCK**3

    whole = jax.ShapeDtypeStruct((2,) + square, bf16)
    split_square = pltpu.VMEM((2,) + square, bf16)
    m = pairs // 2

    def terms(*plan):
        return call(
            functools.partial(grad_terms, plan),
            [(len(chips),) + piece for chips, _ in plan],
            [HBM] * 3,
            [
                pltpu.VMEM(activations.shape, bf16),
                pltpu.VMEM(out_grads.shape, bf16),
                pltpu.SMEM(owner_blocks.shape, jnp.int32),
                pltpu.SemaphoreType.DMA((1 + 2 * (tokens // CHUNK),)),
            ],
            flops=2 * tokens * HALF * BLOCK * sum(len(chips) for chips, _ in plan),
        )(*(in_hbm(x) for x in (activations, out_grads, owner_blocks)))

    above, below = range(m, pairs), range(m)
    (send_far,) = terms((above, True))
    got_far = flip(send_far, 1)
    keep_far, send_near, keep_near = terms((above, False), (below, True), (below, False))
    got_near = flip(send_near, 1)
    arrived = [flip(keep_far[j] + got_far[j], 2 * m) for j in range(m)]
    while m > 1:
        m //= 2
        held = [keep_near[j] + got_near[j] + arrived[j] for j in range(m, 2 * m)]
        arrived = [x + flip(y, 2 * m) for x, y in zip(arrived, held)]
    shuffle = [(s * pairs + p, 2 * p + 1 - s) for s in range(2) for p in range(pairs)]
    packed, trace, rows = call(
        functools.partial(pack_stat, pairs), [(PACKED, BLOCK), (1, 128), (2 * pairs, 128)], [VMEM, SMEM]
    )(statistics[0, 0], owner_blocks)
    old = lax.ppermute(packed, "rep", shuffle)
    half, sums = call(
        functools.partial(finish_half, devices), [(PACKED, BLOCK), (devices, 2, 128)], [VMEM] * 4
    )(keep_near, got_near, arrived[0], trace)
    other = flip(half, 1)
    sums = lax.all_to_all(sums, AXES, 0, 0)
    facts, square_p, cube_p, out_packed, g_split = call(
        update_stat,
        [(2, 128)] + [(PACKED, BLOCK)] * 3 + [pltpu.HBM((2,) + square, bf16)],
        [VMEM] * 3,
        [pltpu.VMEM((2, 2) + square, bf16), split_square, split_square, pltpu.SemaphoreType.DMA],
        flops=3 * unit,
        out_specs=[VMEM] * 4 + [HBM],
        input_output_aliases={0: 3, 1: 2, 2: 1},
    )(half, other, old)
    new_packed = lax.ppermute(out_packed, "rep", [(t, s) for s, t in shuffle])
    mine_root, totals, g_split = call(
        functools.partial(root, devices),
        [(HALF + HALF // 2, BLOCK), (1, 128), whole],
        [VMEM, HBM] + [VMEM] * 4,
        [pltpu.VMEM(square, bf16)] * 2 + [pltpu.SemaphoreType.DMA],
        flops=unit,
    )(out_packed, in_hbm(g_split), square_p, cube_p, facts, sums)
    other_root = flip(mine_root, 1)
    (middle,) = call(half_way, [whole], [VMEM] * 2, [split_square], flops=unit)(g_split, mine_root)
    mine, most, rest, prec = call(last_product, [piece, (MOST, BLOCK), (HALF - MOST, BLOCK), (2 * stripes, 1, 128)], [VMEM] * 2, [split_square], flops=unit)(middle, other_root)

    bit = 2
    while bit < rep_count:
        prec = prec + flip(prec, bit)
        bit *= 2

    def spread_over_chips(x):
        found, bit = [x], 2
        while bit < rep_count:
            found = found + [flip(y, bit) for y in found]
            bit *= 2
        return found[1:]

    most = spread_over_chips(most)
    rest = spread_over_chips(rest)
    across = flip(mine, 1)
    near = [(s + stripes // 4) % stripes for s in range(stripes)]
    groups = [[(2 * q + c) * stripes + s for s in near for c in range(2)] for q in range(pairs)]
    prec = lax.all_to_all(prec, AXES, 0, 0, axis_index_groups=groups)
    (new_stat,) = call(unpack_stat, [square], [VMEM])(new_packed)
    slab = (pairs * BLOCK, out_grads.shape[1])

    def landing(found):
        count = sum(x.shape[0] for x in found)
        return [pltpu.VMEM((count, BLOCK), f32), pltpu.SemaphoreType.DMA((count // CHUNK,))]

    def place(placed, plan, *found):
        (placed,) = call(
            functools.partial(place_next, plan),
            [slab],
            [VMEM] * (len(plan) + 2) + [HBM],
            landing(found),
            out_specs=[HBM],
            input_output_aliases={len(plan) + 2: 0},
        )(*found, scale, rows, placed)
        return placed

    far = range(1, pairs)
    plan, found = [(0, 0), (pairs, 0)], (mine, across)
    placed, scale = call(
        functools.partial(place_first, plan), [slab, (1, 128)], [VMEM] * 5, landing(found), out_specs=[HBM, VMEM]
    )(*found, prec, totals, rows)
    most_across = [flip(x, 1) for x in most]
    rest_across = [flip(x, 1) for x in rest]
    plan = [(j, 0) for j in far] + [(pairs + j, 0) for j in far] + [(j, MOST) for j in far]
    placed = place(placed, plan, *most, *most_across, *rest)
    placed = place(placed, [(pairs + j, MOST) for j in far], *rest_across)
    return placed, new_stat[None, None]


def solution(mesh):
    in_specs = (
        P("rep", None),
        P("rep", "stripe"),
        P("rep", "stripe", None, None),
        P("stripe", None),
    )
    out_specs = (P(None, "stripe"), P("rep", "stripe", None, None))
    return jax.shard_map(per_device, mesh=mesh, in_specs=in_specs, out_specs=out_specs, check_vma=False)
```

profile of v0, /device:TPU:0, one launch (start us, length us, event | category | flops | bytes accessed | tf_op | source)
XLA Modules:
  0.0 75.2 jit_solution(18302837544247468080)
XLA Ops:
  0.7 1.6 %shard_map.60 = f32[1,256,512]{2,1,0:T(8,128)S(1)} custom-call(bf16[256,1024]{1,0:T(8,128)(2,1)} %acts.3, bf16[256,512]{1,0:T(8,128)(2,1)} %grads.3, s32[1,2]{1,0:T(1,128)} %owners.5), custom_call_target="tpu_custom_call" | custom-call | flops 67108864 | bytes 1048576 | tf_op jit(solution)/shard_map/pallas_call | solution.py:354
  2.8 1.7 %shard_map.59 = (f32[1,256,512]{2,1,0:T(8,128)S(1)}, f32[1,256,512]{2,1,0:T(8,128)S(1)}, f32[1,256,512]{2,1,0:T(8,128)S(1)}) custom-call(bf16[256,1024]{1,0:T(8,128)(2,1)} %acts.3, bf16[256,512]{1,0:T(8,128)(2,1)} %grads.3, s32[1,2]{1,0:T(1,128)} %owners.5), custom_call_target="tpu_custom_call" | custom-call | flops 201326592 | bytes 1048576 | tf_op jit(solution)/shard_map/pallas_call | solution.py:354
  4.7 3.0 %collective-permute-start.2 = (f32[256,512]{1,0:T(8,128)S(1)}, f32[256,512]{1,0:T(8,128)S(1)}, u32[]{:S(2)}, u32[]{:S(2)}) collective-permute-start(f32[256,512]{1,0:T(8,128)S(1)} %add_bitcast_fusion), channel_id=1, source_target_pairs={{0,16},{8,24},{16,0},{24,8},{1,17},{9,25},{17,1},{25,9},{2,18},{10... | collective-permute-start | bytes 1572872 | tf_op jit(solution)/shard_map/ppermute | solution.py:69
  8.4 11.7 %collective-permute-done.2.rest = f32[256,512]{1,0:T(8,128)S(1)} collective-permute-done((f32[256,512]{1,0:T(8,128)S(1)}, f32[256,512]{1,0:T(8,128)S(1)}, u32[]{:S(2)}, u32[]{:S(2)}) %collective-permute-start.2) | collective-permute-done | bytes 524320 | tf_op jit(solution)/shard_map/ppermute | solution.py:69
  20.1 0.8 %shard_map.62 = (f32[264,512]{1,0:T(8,128)S(1)}, f32[32,2,128]{2,1,0:T(2,128)}) custom-call(f32[1,256,512]{2,1,0:T(8,128)S(1)} %get-tuple-element.24.keep, f32[1,256,512]{2,1,0:T(8,128)S(1)} %collective-permute-done.got, f32[256,512]{1,0:T(8,128)S(1)} %collective-permute-done.2.rest, f32[1,128]{1,0:T(1,128)S(1)} %get-tuple-element.27.trace), custom_call_target="tpu_custom_call" | custom-call | bytes 1048576 | tf_op jit(solution)/shard_map/pallas_call | solution.py:382
  20.9 7.0 %all-to-all-start = ((f32[32,2,128]{2,1,0:T(2,128)}), f32[32,2,128]{2,1,0:T(2,128)S(1)}, u32[]{:S(2)}, u32[]{:S(2)}) async-start(f32[32,2,128]{2,1,0:T(2,128)} %get-tuple-element.35), calls=%async_computation | async-start | bytes 65536 | tf_op jit(solution)/shard_map/all_to_all | solution.py:386
  27.9 3.4 %shard_map.63 = (f32[2,128]{1,0:T(2,128)S(1)}, f32[264,512]{1,0:T(8,128)S(1)}, f32[264,512]{1,0:T(8,128)S(1)}, f32[264,512]{1,0:T(8,128)S(1)}, bf16[2,512,512]{2,1,0:T(8,128)(2,1)}) custom-call(f32[264,512]{1,0:T(8,128)S(1)} %get-tuple-element.28.half, ...), custom_call_target="tpu_custom_call", output_to_operand_aliasing={{3}: (0, {}), {2}: (1, {}), {1}: (2, {})} | custom-call | flops 2415919104 | bytes 1048576 | tf_op jit(solution)/shard_map/pallas_call | solution.py:387
  31.2 3.8 %all-to-all-done.sums = f32[32,2,128]{2,1,0:T(2,128)S(1)} async-done(((f32[32,2,128]{2,1,0:T(2,128)}), f32[32,2,128]{2,1,0:T(2,128)S(1)}, u32[]{:S(2)}, u32[]{:S(2)}) %all-to-all-start) | async-done | bytes 32800 | tf_op jit(solution)/shard_map/all_to_all | solution.py:386
  35.0 1.2 %shard_map.64 = (f32[384,512]{1,0:T(8,128)S(1)}, f32[1,128]{1,0:T(1,128)S(1)}, bf16[2,512,512]{2,1,0:T(8,128)(2,1)S(1)}) custom-call(f32[264,512]{1,0:T(8,128)S(1)} %get-tuple-element.30.stat, bf16[2,512,512]{2,1,0:T(8,128)(2,1)} %get-tuple-element.31.g_in, f32[264,512]{1,0:T(8,128)S(1)} %get-tuple-element.32.square, ...), custom_call_target="tpu_custom_call" | custom-call | flops 805306368 | bytes 1048576 | tf_op jit(solution)/shard_map/pallas_call | solution.py:397
  36.5 1.2 %shard_map.65.middle = bf16[2,512,512]{2,1,0:T(8,128)(2,1)S(1)} custom-call(bf16[2,512,512]{2,1,0:T(8,128)(2,1)S(1)} %get-tuple-element.36.g, f32[384,512]{1,0:T(8,128)S(1)} %get-tuple-element.37.packed), custom_call_target="tpu_custom_call" | custom-call | flops 805306368 | bytes 1048576 | tf_op jit(solution)/shard_map/pallas_call | solution.py:405
  37.6 1.0 %collective-permute-done.5.packed = f32[384,512]{1,0:T(8,128)S(1)} collective-permute-done((f32[384,512]{1,0:T(8,128)S(1)}, f32[384,512]{1,0:T(8,128)S(1)}, u32[]{:S(2)}, u32[]{:S(2)}) %collective-permute-start.5) | collective-permute-done | bytes 786464 | tf_op jit(solution)/shard_map/ppermute | solution.py:69
  39.3 0.7 collective-permute-start.10
  40.0 1.4 %collective-permute-start.12 = (f32[264,512]{1,0:T(8,128)S(1)}, f32[264,512]{1,0:T(8,128)S(1)}, u32[]{:S(2)}, u32[]{:S(2)}) collective-permute-start(f32[264,512]{1,0:T(8,128)S(1)} %get-tuple-element.30.stat), channel_id=1, source_target_pairs={{8,0},{24,8},{0,16},{16,24},{9,1},{25,9},{1,17},{17,25},{10,2},{26... | collective-permute-start | bytes 1622024 | tf_op jit(solution)/shard_map/ppermute | solution.py:396
  41.4 10.0 %collective-permute-done.10.refs_0_ = f32[192,512]{1,0:T(8,128)S(1)} collective-permute-done((f32[192,512]{1,0:T(8,128)S(1)}, f32[192,512]{1,0:T(8,128)S(1)}, u32[]{:S(2)}, u32[]{:S(2)}) %collective-permute-start.10) | collective-permute-done | bytes 393248 | tf_op jit(solution)/shard_map/ppermute | solution.py:69
  51.4 6.4 %collective-permute-done.6.refs_2_ = f32[64,512]{1,0:T(8,128)S(1)} collective-permute-done((f32[64,512]{1,0:T(8,128)S(1)}, f32[64,512]{1,0:T(8,128)S(1)}, u32[]{:S(2)}, u32[]{:S(2)}) %collective-permute-start.6) | collective-permute-done | bytes 131104 | tf_op jit(solution)/shard_map/ppermute | solution.py:69
  57.7 1.2 %collective-permute-start.7 = (f32[64,512]{1,0:T(8,128)S(1)}, f32[64,512]{1,0:T(8,128)S(1)}, u32[]{:S(2)}, u32[]{:S(2)}) collective-permute-start(f32[64,512]{1,0:T(8,128)S(1)} %collective-permute-done.6.refs_2_), channel_id=1, source_target_pairs={{0,8},{8,0},{16,24},{24,16},{1,9},{9,1},{17,25},{25,17},{2,10},{10... | collective-permute-start | bytes 393224 | tf_op jit(solution)/shard_map/ppermute | solution.py:69
  58.9 0.8 %collective-permute-start.9 = (f32[16,1,128]{2,1,0:T(1,128)S(1)}, f32[16,1,128]{2,1,0:T(1,128)S(1)}, u32[]{:S(2)}, u32[]{:S(2)}) collective-permute-start(f32[16,1,128]{2,1,0:T(1,128)S(1)} %get-tuple-element.40), channel_id=1, source_target_pairs={{0,16},{8,24},{16,0},{24,8},{1,17},{9,25},{17,1},{25,9},{2,18},{10... | collective-permute-start | bytes 24584 | tf_op jit(solution)/shard_map/ppermute | solution.py:69
  59.8 2.8 %collective-permute-done.9 = f32[16,1,128]{2,1,0:T(1,128)S(1)} collective-permute-done((f32[16,1,128]{2,1,0:T(1,128)S(1)}, f32[16,1,128]{2,1,0:T(1,128)S(1)}, u32[]{:S(2)}, u32[]{:S(2)}) %collective-permute-start.9) | collective-permute-done | bytes 8224 | tf_op jit(solution)/shard_map/ppermute | solution.py:69
  63.2 3.8 %all-to-all-start.1 = ((f32[16,1,128]{2,1,0:T(1,128)}), f32[16,1,128]{2,1,0:T(1,128)S(1)}, u32[]{:S(2)}, u32[]{:S(2)}) async-start(f32[16,1,128]{2,1,0:T(1,128)} %add.11), calls=%async_computation.1 | async-start | bytes 16384 | tf_op jit(solution)/shard_map/all_to_all | solution.py:425
  67.0 1.2 %shard_map.70 = f32[512,512]{1,0:T(8,128)} custom-call(f32[264,512]{1,0:T(8,128)S(1)} %collective-permute-done.12.packed), custom_call_target="tpu_custom_call" | custom-call | bytes 1048576 | tf_op jit(solution)/shard_map/pallas_call | solution.py:426
  68.2 3.8 %all-to-all-done.1.refs_2_ = f32[16,1,128]{2,1,0:T(1,128)S(1)} async-done(((f32[16,1,128]{2,1,0:T(1,128)}), f32[16,1,128]{2,1,0:T(1,128)S(1)}, u32[]{:S(2)}, u32[]{:S(2)}) %all-to-all-start.1) | async-done | bytes 8224 | tf_op jit(solution)/shard_map/all_to_all | solution.py:425
  72.0 1.2 %shard_map.67 = (f32[1024,512]{1,0:T(8,128)}, f32[1,128]{1,0:T(1,128)S(1)}) custom-call(f32[256,512]{1,0:T(8,128)S(1)} %get-tuple-element.39.refs_0_, f32[256,512]{1,0:T(8,128)S(1)} %collective-permute-done.8.refs_1_, f32[16,1,128]{2,1,0:T(1,128)S(1)} %all-to-all-done.1.refs_2_, f32[1,128]{1,0:T(1,128)S(1)} %get-tuple-element.41.refs_3_, ...), custom_call_target="tpu_custom_call" | custom-call | bytes 1048576 | tf_op jit(solution)/shard_map/pallas_call | solution.py:446
  73.3 1.1 %shard_map.68.refs_3_ = f32[1024,512]{1,0:T(8,128)} custom-call(f32[192,512]{1,0:T(8,128)S(1)} %collective-permute-done.10.refs_0_, f32[192,512]{1,0:T(8,128)S(1)} %collective-permute-done.11.refs_1_, f32[64,512]{1,0:T(8,128)S(1)} %collective-permute-done.6.refs_2_, f32[1,128]{1,0:T(1,128)S(1)} %get-tuple-element.43.refs_3_.refs_1_, ...), custom_call_target="tpu_custom_call", output_to_operand_aliasing={{}: (5, {})} | custom-call | bytes 1048576 | tf_op jit(solution)/shard_map/pallas_call | solution.py:434
  74.4 0.8 %shard_map.69 = f32[1024,512]{1,0:T(8,128)} custom-call(f32[64,512]{1,0:T(8,128)S(1)} %collective-permute-done.7.refs_0_, f32[1,128]{1,0:T(1,128)S(1)} %get-tuple-element.43.refs_3_.refs_1_, f32[4,128]{1,0:T(4,128)S(1)} %get-tuple-element.42.refs_4_.refs_2_, f32[1024,512]{1,0:T(8,128)} %shard_map.68.refs_3_), custom_call_target="tpu_custom_call", output_to_operand_aliasing={{}: (3, {})} | custom-call | bytes 1048576 | tf_op jit(solution)/shard_map/pallas_call | solution.py:434
  (24 shorter events, 2.8 us)
Async XLA Ops:
  0.6 7.1 %copy-start.1 = (s32[1,2]{1,0:T(1,128)S(1)}, s32[1,2]{1,0:T(1,128)}, u32[]{:S(2)}) copy-start(s32[1,2]{1,0:T(1,128)} %owners.5) | copy-start | bytes 28
  0.6 7.1 %copy-start = (f32[1,1,512,512]{3,2,1,0:T(8,128)S(1)}, f32[1,1,512,512]{3,2,1,0:T(8,128)}, u32[]{:S(2)}) copy-start(f32[1,1,512,512]{3,2,1,0:T(8,128)} %param.6) | copy-start | bytes 3145732
  2.3 2.4 %collective-permute-start.1 = (f32[1,256,512]{2,1,0:T(8,128)S(1)}, f32[1,256,512]{2,1,0:T(8,128)S(1)}, u32[]{:S(2)}, u32[]{:S(2)}) collective-permute-start(f32[1,256,512]{2,1,0:T(8,128)S(1)} %shard_map.60), channel_id=1, source_target_pairs={{0,8},{8,0},{16,24},{24,16},{1,9},{9,1},{17,25},{25,17},{2,10},{10... | collective-permute-start | bytes 1572872 | tf_op jit(solution)/shard_map/ppermute | solution.py:69
  4.5 3.8 %collective-permute-start = (f32[1,256,512]{2,1,0:T(8,128)S(1)}, f32[1,256,512]{2,1,0:T(8,128)S(1)}, u32[]{:S(2)}, u32[]{:S(2)}) collective-permute-start(f32[1,256,512]{2,1,0:T(8,128)S(1)} %get-tuple-element.25), channel_id=1, source_target_pairs={{0,8},{8,0},{16,24},{24,16},{1,9},{9,1},{17,25},{25,17},{2,10},{10... | collective-permute-start | bytes 1572872 | tf_op jit(solution)/shard_map/ppermute | solution.py:69
  4.7 15.3 %collective-permute-start.2 = (f32[256,512]{1,0:T(8,128)S(1)}, f32[256,512]{1,0:T(8,128)S(1)}, u32[]{:S(2)}, u32[]{:S(2)}) collective-permute-start(f32[256,512]{1,0:T(8,128)S(1)} %add_bitcast_fusion), channel_id=1, source_target_pairs={{0,16},{8,24},{16,0},{24,8},{1,17},{9,25},{17,1},{25,9},{2,18},{10... | collective-permute-start | bytes 1572872 | tf_op jit(solution)/shard_map/ppermute | solution.py:69
  8.4 19.5 %collective-permute-start.4 = (f32[264,512]{1,0:T(8,128)S(1)}, f32[264,512]{1,0:T(8,128)S(1)}, u32[]{:S(2)}, u32[]{:S(2)}) collective-permute-start(f32[264,512]{1,0:T(8,128)S(1)} %get-tuple-element.29), channel_id=1, source_target_pairs={{0,8},{8,24},{16,0},{24,16},{1,9},{9,25},{17,1},{25,17},{2,10},{10... | collective-permute-start | bytes 1622024 | tf_op jit(solution)/shard_map/ppermute | solution.py:381
  20.9 7.0 %collective-permute-start.3 = (f32[264,512]{1,0:T(8,128)S(1)}, f32[264,512]{1,0:T(8,128)S(1)}, u32[]{:S(2)}, u32[]{:S(2)}) collective-permute-start(f32[264,512]{1,0:T(8,128)S(1)} %get-tuple-element.28.half), channel_id=1, source_target_pairs={{0,8},{8,0},{16,24},{24,16},{1,9},{9,1},{17,25},{25,17},{2,10},{10... | collective-permute-start | bytes 1622024 | tf_op jit(solution)/shard_map/ppermute | solution.py:69
  20.9 14.2 %all-to-all-start = ((f32[32,2,128]{2,1,0:T(2,128)}), f32[32,2,128]{2,1,0:T(2,128)S(1)}, u32[]{:S(2)}, u32[]{:S(2)}) async-start(f32[32,2,128]{2,1,0:T(2,128)} %get-tuple-element.35), calls=%async_computation | async-start | bytes 65536 | tf_op jit(solution)/shard_map/all_to_all | solution.py:386
  36.3 2.4 %collective-permute-start.5 = (f32[384,512]{1,0:T(8,128)S(1)}, f32[384,512]{1,0:T(8,128)S(1)}, u32[]{:S(2)}, u32[]{:S(2)}) collective-permute-start(f32[384,512]{1,0:T(8,128)S(1)} %get-tuple-element.37.packed), channel_id=1, source_target_pairs={{0,8},{8,0},{16,24},{24,16},{1,9},{9,1},{17,25},{25,17},{2,10},{10... | collective-permute-start | bytes 2359304 | tf_op jit(solution)/shard_map/ppermute | solution.py:69
  39.3 12.1 %collective-permute-start.10 = (f32[192,512]{1,0:T(8,128)S(1)}, f32[192,512]{1,0:T(8,128)S(1)}, u32[]{:S(2)}, u32[]{:S(2)}) collective-permute-start(f32[192,512]{1,0:T(8,128)S(1)} %get-tuple-element.44), channel_id=1, source_target_pairs={{0,16},{8,24},{16,0},{24,8},{1,17},{9,25},{17,1},{25,9},{2,18},{10... | collective-permute-start | bytes 1179656 | tf_op jit(solution)/shard_map/ppermute | solution.py:69
  40.0 27.0 %collective-permute-start.12 = (f32[264,512]{1,0:T(8,128)S(1)}, f32[264,512]{1,0:T(8,128)S(1)}, u32[]{:S(2)}, u32[]{:S(2)}) collective-permute-start(f32[264,512]{1,0:T(8,128)S(1)} %get-tuple-element.30.stat), channel_id=1, source_target_pairs={{8,0},{24,8},{0,16},{16,24},{9,1},{25,9},{1,17},{17,25},{10,2},{26... | collective-permute-start | bytes 1622024 | tf_op jit(solution)/shard_map/ppermute | solution.py:396
  41.4 30.6 %collective-permute-start.8 = (f32[256,512]{1,0:T(8,128)S(1)}, f32[256,512]{1,0:T(8,128)S(1)}, u32[]{:S(2)}, u32[]{:S(2)}) collective-permute-start(f32[256,512]{1,0:T(8,128)S(1)} %get-tuple-element.39.refs_0_), channel_id=1, source_target_pairs={{0,8},{8,0},{16,24},{24,16},{1,9},{9,1},{17,25},{25,17},{2,10},{10... | collective-permute-start | bytes 1572872 | tf_op jit(solution)/shard_map/ppermute | solution.py:69
  51.4 21.9 %collective-permute-start.11 = (f32[192,512]{1,0:T(8,128)S(1)}, f32[192,512]{1,0:T(8,128)S(1)}, u32[]{:S(2)}, u32[]{:S(2)}) collective-permute-start(f32[192,512]{1,0:T(8,128)S(1)} %collective-permute-done.10.refs_0_), channel_id=1, source_target_pairs={{0,8},{8,0},{16,24},{24,16},{1,9},{9,1},{17,25},{25,17},{2,10},{10... | collective-permute-start | bytes 1179656 | tf_op jit(solution)/shard_map/ppermute | solution.py:69
  51.4 6.4 %collective-permute-start.6 = (f32[64,512]{1,0:T(8,128)S(1)}, f32[64,512]{1,0:T(8,128)S(1)}, u32[]{:S(2)}, u32[]{:S(2)}) collective-permute-start(f32[64,512]{1,0:T(8,128)S(1)} %get-tuple-element.38), channel_id=1, source_target_pairs={{0,16},{8,24},{16,0},{24,8},{1,17},{9,25},{17,1},{25,9},{2,18},{10... | collective-permute-start | bytes 393224 | tf_op jit(solution)/shard_map/ppermute | solution.py:69
  57.7 16.7 %collective-permute-start.7 = (f32[64,512]{1,0:T(8,128)S(1)}, f32[64,512]{1,0:T(8,128)S(1)}, u32[]{:S(2)}, u32[]{:S(2)}) collective-permute-start(f32[64,512]{1,0:T(8,128)S(1)} %collective-permute-done.6.refs_2_), channel_id=1, source_target_pairs={{0,8},{8,0},{16,24},{24,16},{1,9},{9,1},{17,25},{25,17},{2,10},{10... | collective-permute-start | bytes 393224 | tf_op jit(solution)/shard_map/ppermute | solution.py:69
  58.9 3.7 %collective-permute-start.9 = (f32[16,1,128]{2,1,0:T(1,128)S(1)}, f32[16,1,128]{2,1,0:T(1,128)S(1)}, u32[]{:S(2)}, u32[]{:S(2)}) collective-permute-start(f32[16,1,128]{2,1,0:T(1,128)S(1)} %get-tuple-element.40), channel_id=1, source_target_pairs={{0,16},{8,24},{16,0},{24,8},{1,17},{9,25},{17,1},{25,9},{2,18},{10... | collective-permute-start | bytes 24584 | tf_op jit(solution)/shard_map/ppermute | solution.py:69
  63.2 8.8 %all-to-all-start.1 = ((f32[16,1,128]{2,1,0:T(1,128)}), f32[16,1,128]{2,1,0:T(1,128)S(1)}, u32[]{:S(2)}, u32[]{:S(2)}) async-start(f32[16,1,128]{2,1,0:T(1,128)} %add.11), calls=%async_computation.1 | async-start | bytes 16384 | tf_op jit(solution)/shard_map/all_to_all | solution.py:425
where the time goes:
time: 75.5 us; the launch traced here: 75.2 us
  waiting for transfers between devices  39.5 us (52%)
  starting transfers between devices  18.8 us (25%)
  Pallas kernels  15.5 us (21%)
  between operations  0.79 us (1%)
    ppermute x11, waiting for transfers between devices, flip(): lax.ppermute(x, 'rep', [(i, i ^ mask) for i in range(lax.axis_size('rep'))])  31.8 us
    all_to_all x1, starting transfers between devices, per_device(): sums = lax.all_to_all(sums, AXES, 0, 0)  6.97 us
    ppermute x11, starting transfers between devices, flip(): lax.ppermute(x, 'rep', [(i, i ^ mask) for i in range(lax.axis_size('rep'))])  6.58 us
    all_to_all x1, starting transfers between devices, per_device(): prec = lax.all_to_all(prec, AXES, 0, 0, axis_index_groups=groups)  3.83 us
    all_to_all x1, waiting for transfers between devices, per_device(): sums = lax.all_to_all(sums, AXES, 0, 0)  3.81 us
    all_to_all x1, waiting for transfers between devices, per_device(): prec = lax.all_to_all(prec, AXES, 0, 0, axis_index_groups=groups)  3.8 us
    pallas_call x1, Pallas kernels, per_device(): call(update_stat, [(2, 128)] + [(PACKED, BLOCK)] * 3 + [pltpu.HBM((2,) +...  3.35 us
    pallas_call x2, Pallas kernels, terms(): call(functools.partial(grad_terms, plan), [(len(chips),) + piece for chip...  3.33 us
  transfers between devices with their start and end apart: 15, of which 7 were waited for; matrix products, arithmetic and copies ran while one was open for 1% of the time, Pallas kernels for 15%

commit v1 on v0

--- a/solution.py
+++ b/solution.py
@@ -130,10 +130,9 @@
 def grad_terms(plan, acts, grads, owners, *refs):
     outs, (av, gv, ov, sems) = refs[: len(plan)], refs[len(plan) :]
     chip, core = chip_core()
-    parts = [(owners, ov)]
-    for src, dst in ((grads, gv), (acts, av)):
-        parts += [(src.at[pl.ds(r, CHUNK)], dst.at[pl.ds(r, CHUNK)]) for r in range(0, src.shape[0], CHUNK)]
-    copies = [pltpu.make_async_copy(src, dst, sems.at[k]) for k, (src, dst) in enumerate(parts)]
+    copies = [
+        pltpu.make_async_copy(src, dst, sems.at[k]) for k, (src, dst) in enumerate(((owners, ov), (acts, av), (grads, gv)))
+    ]
     for copy in copies:
         copy.start()
     for copy in copies:
@@ -359,7 +358,7 @@
                 pltpu.VMEM(activations.shape, bf16),
                 pltpu.VMEM(out_grads.shape, bf16),
                 pltpu.SMEM(owner_blocks.shape, jnp.int32),
-                pltpu.SemaphoreType.DMA((1 + 2 * (tokens // CHUNK),)),
+                pltpu.SemaphoreType.DMA((3,)),
             ],
             flops=2 * tokens * HALF * BLOCK * sum(len(chips) for chips, _ in plan),
         )(*(in_hbm(x) for x in (activations, out_grads, owner_blocks)))

time: 75.5 us -> 75.2 us (level)
  no operation moved by 1% of the time
where the time goes in v1:
time: 75.2 us; the launch traced here: 74.9 us
  waiting for transfers between devices  39.5 us (53%)
  starting transfers between devices  18.8 us (25%)
  Pallas kernels  15.2 us (20%)
  between operations  0.79 us (1%)
    ppermute x11, waiting for transfers between devices, flip(): lax.ppermute(x, 'rep', [(i, i ^ mask) for i in range(lax.axis_size('rep'))])  31.8 us
    all_to_all x1, starting transfers between devices, per_device(): sums = lax.all_to_all(sums, AXES, 0, 0)  6.95 us
    ppermute x11, starting transfers between devices, flip(): lax.ppermute(x, 'rep', [(i, i ^ mask) for i in range(lax.axis_size('rep'))])  6.59 us
    all_to_all x1, starting transfers between devices, per_device(): prec = lax.all_to_all(prec, AXES, 0, 0, axis_index_groups=groups)  3.83 us
    all_to_all x1, waiting for transfers between devices, per_device(): sums = lax.all_to_all(sums, AXES, 0, 0)  3.81 us
    all_to_all x1, waiting for transfers between devices, per_device(): prec = lax.all_to_all(prec, AXES, 0, 0, axis_index_groups=groups)  3.8 us
    pallas_call x1, Pallas kernels, per_device(): call(update_stat, [(2, 128)] + [(PACKED, BLOCK)] * 3 + [pltpu.HBM((2,) +...  3.35 us
    pallas_call x2, Pallas kernels, terms(): call(functools.partial(grad_terms, plan), [(len(chips),) + piece for chip...  3.04 us
  transfers between devices with their start and end apart: 15, of which 7 were waited for; matrix products, arithmetic and copies ran while one was open for 1% of the time, Pallas kernels for 15%

profile of v1, /device:TPU:0, one launch (start us, length us, event | category | flops | bytes accessed | tf_op | source)
XLA Modules:
  0.0 74.9 jit_solution(4408507966077363331)
XLA Ops:
  0.7 1.5 %shard_map.60 = f32[1,256,512]{2,1,0:T(8,128)S(1)} custom-call(bf16[256,1024]{1,0:T(8,128)(2,1)} %acts.3, bf16[256,512]{1,0:T(8,128)(2,1)} %grads.3, s32[1,2]{1,0:T(1,128)} %owners.5), custom_call_target="tpu_custom_call" | custom-call | flops 67108864 | bytes 1048576 | tf_op jit(solution)/shard_map/pallas_call | solution.py:353
  2.7 1.5 %shard_map.59 = (f32[1,256,512]{2,1,0:T(8,128)S(1)}, f32[1,256,512]{2,1,0:T(8,128)S(1)}, f32[1,256,512]{2,1,0:T(8,128)S(1)}) custom-call(bf16[256,1024]{1,0:T(8,128)(2,1)} %acts.3, bf16[256,512]{1,0:T(8,128)(2,1)} %grads.3, s32[1,2]{1,0:T(1,128)} %owners.5), custom_call_target="tpu_custom_call" | custom-call | flops 201326592 | bytes 1048576 | tf_op jit(solution)/shard_map/pallas_call | solution.py:353
  4.4 3.0 %collective-permute-start.2 = (f32[256,512]{1,0:T(8,128)S(1)}, f32[256,512]{1,0:T(8,128)S(1)}, u32[]{:S(2)}, u32[]{:S(2)}) collective-permute-start(f32[256,512]{1,0:T(8,128)S(1)} %add_bitcast_fusion), channel_id=1, source_target_pairs={{0,16},{8,24},{16,0},{24,8},{1,17},{9,25},{17,1},{25,9},{2,18},{10... | collective-permute-start | bytes 1572872 | tf_op jit(solution)/shard_map/ppermute | solution.py:69
  8.1 11.7 %collective-permute-done.2.rest = f32[256,512]{1,0:T(8,128)S(1)} collective-permute-done((f32[256,512]{1,0:T(8,128)S(1)}, f32[256,512]{1,0:T(8,128)S(1)}, u32[]{:S(2)}, u32[]{:S(2)}) %collective-permute-start.2) | collective-permute-done | bytes 524320 | tf_op jit(solution)/shard_map/ppermute | solution.py:69
  19.8 0.8 %shard_map.62 = (f32[264,512]{1,0:T(8,128)S(1)}, f32[32,2,128]{2,1,0:T(2,128)}) custom-call(f32[1,256,512]{2,1,0:T(8,128)S(1)} %get-tuple-element.24.keep, f32[1,256,512]{2,1,0:T(8,128)S(1)} %collective-permute-done.got, f32[256,512]{1,0:T(8,128)S(1)} %collective-permute-done.2.rest, f32[1,128]{1,0:T(1,128)S(1)} %get-tuple-element.27.trace), custom_call_target="tpu_custom_call" | custom-call | bytes 1048576 | tf_op jit(solution)/shard_map/pallas_call | solution.py:381
  20.6 6.9 %all-to-all-start = ((f32[32,2,128]{2,1,0:T(2,128)}), f32[32,2,128]{2,1,0:T(2,128)S(1)}, u32[]{:S(2)}, u32[]{:S(2)}) async-start(f32[32,2,128]{2,1,0:T(2,128)} %get-tuple-element.35), calls=%async_computation | async-start | bytes 65536 | tf_op jit(solution)/shard_map/all_to_all | solution.py:385
  27.6 3.4 %shard_map.63 = (f32[2,128]{1,0:T(2,128)S(1)}, f32[264,512]{1,0:T(8,128)S(1)}, f32[264,512]{1,0:T(8,128)S(1)}, f32[264,512]{1,0:T(8,128)S(1)}, bf16[2,512,512]{2,1,0:T(8,128)(2,1)}) custom-call(f32[264,512]{1,0:T(8,128)S(1)} %get-tuple-element.28.half, ...), custom_call_target="tpu_custom_call", output_to_operand_aliasing={{3}: (0, {}), {2}: (1, {}), {1}: (2, {})} | custom-call | flops 2415919104 | bytes 1048576 | tf_op jit(solution)/shard_map/pallas_call | solution.py:386
  30.9 3.8 %all-to-all-done.sums = f32[32,2,128]{2,1,0:T(2,128)S(1)} async-done(((f32[32,2,128]{2,1,0:T(2,128)}), f32[32,2,128]{2,1,0:T(2,128)S(1)}, u32[]{:S(2)}, u32[]{:S(2)}) %all-to-all-start) | async-done | bytes 32800 | tf_op jit(solution)/shard_map/all_to_all | solution.py:385
  34.7 1.2 %shard_map.64 = (f32[384,512]{1,0:T(8,128)S(1)}, f32[1,128]{1,0:T(1,128)S(1)}, bf16[2,512,512]{2,1,0:T(8,128)(2,1)S(1)}) custom-call(f32[264,512]{1,0:T(8,128)S(1)} %get-tuple-element.30.stat, bf16[2,512,512]{2,1,0:T(8,128)(2,1)} %get-tuple-element.31.g_in, f32[264,512]{1,0:T(8,128)S(1)} %get-tuple-element.32.square, ...), custom_call_target="tpu_custom_call" | custom-call | flops 805306368 | bytes 1048576 | tf_op jit(solution)/shard_map/pallas_call | solution.py:396
  36.2 1.2 %shard_map.65.middle = bf16[2,512,512]{2,1,0:T(8,128)(2,1)S(1)} custom-call(bf16[2,512,512]{2,1,0:T(8,128)(2,1)S(1)} %get-tuple-element.36.g, f32[384,512]{1,0:T(8,128)S(1)} %get-tuple-element.37.packed), custom_call_target="tpu_custom_call" | custom-call | flops 805306368 | bytes 1048576 | tf_op jit(solution)/shard_map/pallas_call | solution.py:404
  37.3 1.0 %collective-permute-done.5.packed = f32[384,512]{1,0:T(8,128)S(1)} collective-permute-done((f32[384,512]{1,0:T(8,128)S(1)}, f32[384,512]{1,0:T(8,128)S(1)}, u32[]{:S(2)}, u32[]{:S(2)}) %collective-permute-start.5) | collective-permute-done | bytes 786464 | tf_op jit(solution)/shard_map/ppermute | solution.py:69
  39.0 0.7 collective-permute-start.10
  39.7 1.4 %collective-permute-start.12 = (f32[264,512]{1,0:T(8,128)S(1)}, f32[264,512]{1,0:T(8,128)S(1)}, u32[]{:S(2)}, u32[]{:S(2)}) collective-permute-start(f32[264,512]{1,0:T(8,128)S(1)} %get-tuple-element.30.stat), channel_id=1, source_target_pairs={{8,0},{24,8},{0,16},{16,24},{9,1},{25,9},{1,17},{17,25},{10,2},{26... | collective-permute-start | bytes 1622024 | tf_op jit(solution)/shard_map/ppermute | solution.py:395
  41.1 10.0 %collective-permute-done.10.refs_0_ = f32[192,512]{1,0:T(8,128)S(1)} collective-permute-done((f32[192,512]{1,0:T(8,128)S(1)}, f32[192,512]{1,0:T(8,128)S(1)}, u32[]{:S(2)}, u32[]{:S(2)}) %collective-permute-start.10) | collective-permute-done | bytes 393248 | tf_op jit(solution)/shard_map/ppermute | solution.py:69
  51.1 6.4 %collective-permute-done.6.refs_2_ = f32[64,512]{1,0:T(8,128)S(1)} collective-permute-done((f32[64,512]{1,0:T(8,128)S(1)}, f32[64,512]{1,0:T(8,128)S(1)}, u32[]{:S(2)}, u32[]{:S(2)}) %collective-permute-start.6) | collective-permute-done | bytes 131104 | tf_op jit(solution)/shard_map/ppermute | solution.py:69
  57.4 1.2 %collective-permute-start.7 = (f32[64,512]{1,0:T(8,128)S(1)}, f32[64,512]{1,0:T(8,128)S(1)}, u32[]{:S(2)}, u32[]{:S(2)}) collective-permute-start(f32[64,512]{1,0:T(8,128)S(1)} %collective-permute-done.6.refs_2_), channel_id=1, source_target_pairs={{0,8},{8,0},{16,24},{24,16},{1,9},{9,1},{17,25},{25,17},{2,10},{10... | collective-permute-start | bytes 393224 | tf_op jit(solution)/shard_map/ppermute | solution.py:69
  58.6 0.8 %collective-permute-start.9 = (f32[16,1,128]{2,1,0:T(1,128)S(1)}, f32[16,1,128]{2,1,0:T(1,128)S(1)}, u32[]{:S(2)}, u32[]{:S(2)}) collective-permute-start(f32[16,1,128]{2,1,0:T(1,128)S(1)} %get-tuple-element.40), channel_id=1, source_target_pairs={{0,16},{8,24},{16,0},{24,8},{1,17},{9,25},{17,1},{25,9},{2,18},{10... | collective-permute-start | bytes 24584 | tf_op jit(solution)/shard_map/ppermute | solution.py:69
  59.5 2.8 %collective-permute-done.9 = f32[16,1,128]{2,1,0:T(1,128)S(1)} collective-permute-done((f32[16,1,128]{2,1,0:T(1,128)S(1)}, f32[16,1,128]{2,1,0:T(1,128)S(1)}, u32[]{:S(2)}, u32[]{:S(2)}) %collective-permute-start.9) | collective-permute-done | bytes 8224 | tf_op jit(solution)/shard_map/ppermute | solution.py:69
  62.9 3.8 %all-to-all-start.1 = ((f32[16,1,128]{2,1,0:T(1,128)}), f32[16,1,128]{2,1,0:T(1,128)S(1)}, u32[]{:S(2)}, u32[]{:S(2)}) async-start(f32[16,1,128]{2,1,0:T(1,128)} %add.11), calls=%async_computation.1 | async-start | bytes 16384 | tf_op jit(solution)/shard_map/all_to_all | solution.py:424
  66.7 1.2 %shard_map.70 = f32[512,512]{1,0:T(8,128)} custom-call(f32[264,512]{1,0:T(8,128)S(1)} %collective-permute-done.12.packed), custom_call_target="tpu_custom_call" | custom-call | bytes 1048576 | tf_op jit(solution)/shard_map/pallas_call | solution.py:425
  67.9 3.8 %all-to-all-done.1.refs_2_ = f32[16,1,128]{2,1,0:T(1,128)S(1)} async-done(((f32[16,1,128]{2,1,0:T(1,128)}), f32[16,1,128]{2,1,0:T(1,128)S(1)}, u32[]{:S(2)}, u32[]{:S(2)}) %all-to-all-start.1) | async-done | bytes 8224 | tf_op jit(solution)/shard_map/all_to_all | solution.py:424
  71.7 1.2 %shard_map.67 = (f32[1024,512]{1,0:T(8,128)}, f32[1,128]{1,0:T(1,128)S(1)}) custom-call(f32[256,512]{1,0:T(8,128)S(1)} %get-tuple-element.39.refs_0_, f32[256,512]{1,0:T(8,128)S(1)} %collective-permute-done.8.refs_1_, f32[16,1,128]{2,1,0:T(1,128)S(1)} %all-to-all-done.1.refs_2_, f32[1,128]{1,0:T(1,128)S(1)} %get-tuple-element.41.refs_3_, ...), custom_call_target="tpu_custom_call" | custom-call | bytes 1048576 | tf_op jit(solution)/shard_map/pallas_call | solution.py:445
  73.0 1.1 %shard_map.68.refs_3_ = f32[1024,512]{1,0:T(8,128)} custom-call(f32[192,512]{1,0:T(8,128)S(1)} %collective-permute-done.10.refs_0_, f32[192,512]{1,0:T(8,128)S(1)} %collective-permute-done.11.refs_1_, f32[64,512]{1,0:T(8,128)S(1)} %collective-permute-done.6.refs_2_, f32[1,128]{1,0:T(1,128)S(1)} %get-tuple-element.43.refs_3_.refs_1_, ...), custom_call_target="tpu_custom_call", output_to_operand_aliasing={{}: (5, {})} | custom-call | bytes 1048576 | tf_op jit(solution)/shard_map/pallas_call | solution.py:433
  74.1 0.8 %shard_map.69 = f32[1024,512]{1,0:T(8,128)} custom-call(f32[64,512]{1,0:T(8,128)S(1)} %collective-permute-done.7.refs_0_, f32[1,128]{1,0:T(1,128)S(1)} %get-tuple-element.43.refs_3_.refs_1_, f32[4,128]{1,0:T(4,128)S(1)} %get-tuple-element.42.refs_4_.refs_2_, f32[1024,512]{1,0:T(8,128)} %shard_map.68.refs_3_), custom_call_target="tpu_custom_call", output_to_operand_aliasing={{}: (3, {})} | custom-call | bytes 1048576 | tf_op jit(solution)/shard_map/pallas_call | solution.py:433
  (24 shorter events, 2.8 us)
Async XLA Ops:
  0.6 6.8 %copy-start.1 = (s32[1,2]{1,0:T(1,128)S(1)}, s32[1,2]{1,0:T(1,128)}, u32[]{:S(2)}) copy-start(s32[1,2]{1,0:T(1,128)} %owners.5) | copy-start | bytes 28
  0.6 6.8 %copy-start = (f32[1,1,512,512]{3,2,1,0:T(8,128)S(1)}, f32[1,1,512,512]{3,2,1,0:T(8,128)}, u32[]{:S(2)}) copy-start(f32[1,1,512,512]{3,2,1,0:T(8,128)} %param.6) | copy-start | bytes 3145732
  2.1 2.2 %collective-permute-start.1 = (f32[1,256,512]{2,1,0:T(8,128)S(1)}, f32[1,256,512]{2,1,0:T(8,128)S(1)}, u32[]{:S(2)}, u32[]{:S(2)}) collective-permute-start(f32[1,256,512]{2,1,0:T(8,128)S(1)} %shard_map.60), channel_id=1, source_target_pairs={{0,8},{8,0},{16,24},{24,16},{1,9},{9,1},{17,25},{25,17},{2,10},{10... | collective-permute-start | bytes 1572872 | tf_op jit(solution)/shard_map/ppermute | solution.py:69
  4.3 3.8 %collective-permute-start = (f32[1,256,512]{2,1,0:T(8,128)S(1)}, f32[1,256,512]{2,1,0:T(8,128)S(1)}, u32[]{:S(2)}, u32[]{:S(2)}) collective-permute-start(f32[1,256,512]{2,1,0:T(8,128)S(1)} %get-tuple-element.25), channel_id=1, source_target_pairs={{0,8},{8,0},{16,24},{24,16},{1,9},{9,1},{17,25},{25,17},{2,10},{10... | collective-permute-start | bytes 1572872 | tf_op jit(solution)/shard_map/ppermute | solution.py:69
  4.4 15.3 %collective-permute-start.2 = (f32[256,512]{1,0:T(8,128)S(1)}, f32[256,512]{1,0:T(8,128)S(1)}, u32[]{:S(2)}, u32[]{:S(2)}) collective-permute-start(f32[256,512]{1,0:T(8,128)S(1)} %add_bitcast_fusion), channel_id=1, source_target_pairs={{0,16},{8,24},{16,0},{24,8},{1,17},{9,25},{17,1},{25,9},{2,18},{10... | collective-permute-start | bytes 1572872 | tf_op jit(solution)/shard_map/ppermute | solution.py:69
  8.1 19.5 %collective-permute-start.4 = (f32[264,512]{1,0:T(8,128)S(1)}, f32[264,512]{1,0:T(8,128)S(1)}, u32[]{:S(2)}, u32[]{:S(2)}) collective-permute-start(f32[264,512]{1,0:T(8,128)S(1)} %get-tuple-element.29), channel_id=1, source_target_pairs={{0,8},{8,24},{16,0},{24,16},{1,9},{9,25},{17,1},{25,17},{2,10},{10... | collective-permute-start | bytes 1622024 | tf_op jit(solution)/shard_map/ppermute | solution.py:380
  20.6 7.0 %collective-permute-start.3 = (f32[264,512]{1,0:T(8,128)S(1)}, f32[264,512]{1,0:T(8,128)S(1)}, u32[]{:S(2)}, u32[]{:S(2)}) collective-permute-start(f32[264,512]{1,0:T(8,128)S(1)} %get-tuple-element.28.half), channel_id=1, source_target_pairs={{0,8},{8,0},{16,24},{24,16},{1,9},{9,1},{17,25},{25,17},{2,10},{10... | collective-permute-start | bytes 1622024 | tf_op jit(solution)/shard_map/ppermute | solution.py:69
  20.6 14.1 %all-to-all-start = ((f32[32,2,128]{2,1,0:T(2,128)}), f32[32,2,128]{2,1,0:T(2,128)S(1)}, u32[]{:S(2)}, u32[]{:S(2)}) async-start(f32[32,2,128]{2,1,0:T(2,128)} %get-tuple-element.35), calls=%async_computation | async-start | bytes 65536 | tf_op jit(solution)/shard_map/all_to_all | solution.py:385
  36.0 2.4 %collective-permute-start.5 = (f32[384,512]{1,0:T(8,128)S(1)}, f32[384,512]{1,0:T(8,128)S(1)}, u32[]{:S(2)}, u32[]{:S(2)}) collective-permute-start(f32[384,512]{1,0:T(8,128)S(1)} %get-tuple-element.37.packed), channel_id=1, source_target_pairs={{0,8},{8,0},{16,24},{24,16},{1,9},{9,1},{17,25},{25,17},{2,10},{10... | collective-permute-start | bytes 2359304 | tf_op jit(solution)/shard_map/ppermute | solution.py:69
  39.0 12.1 %collective-permute-start.10 = (f32[192,512]{1,0:T(8,128)S(1)}, f32[192,512]{1,0:T(8,128)S(1)}, u32[]{:S(2)}, u32[]{:S(2)}) collective-permute-start(f32[192,512]{1,0:T(8,128)S(1)} %get-tuple-element.44), channel_id=1, source_target_pairs={{0,16},{8,24},{16,0},{24,8},{1,17},{9,25},{17,1},{25,9},{2,18},{10... | collective-permute-start | bytes 1179656 | tf_op jit(solution)/shard_map/ppermute | solution.py:69
  39.7 27.0 %collective-permute-start.12 = (f32[264,512]{1,0:T(8,128)S(1)}, f32[264,512]{1,0:T(8,128)S(1)}, u32[]{:S(2)}, u32[]{:S(2)}) collective-permute-start(f32[264,512]{1,0:T(8,128)S(1)} %get-tuple-element.30.stat), channel_id=1, source_target_pairs={{8,0},{24,8},{0,16},{16,24},{9,1},{25,9},{1,17},{17,25},{10,2},{26... | collective-permute-start | bytes 1622024 | tf_op jit(solution)/shard_map/ppermute | solution.py:395
  41.1 30.6 %collective-permute-start.8 = (f32[256,512]{1,0:T(8,128)S(1)}, f32[256,512]{1,0:T(8,128)S(1)}, u32[]{:S(2)}, u32[]{:S(2)}) collective-permute-start(f32[256,512]{1,0:T(8,128)S(1)} %get-tuple-element.39.refs_0_), channel_id=1, source_target_pairs={{0,8},{8,0},{16,24},{24,16},{1,9},{9,1},{17,25},{25,17},{2,10},{10... | collective-permute-start | bytes 1572872 | tf_op jit(solution)/shard_map/ppermute | solution.py:69
  51.0 21.9 %collective-permute-start.11 = (f32[192,512]{1,0:T(8,128)S(1)}, f32[192,512]{1,0:T(8,128)S(1)}, u32[]{:S(2)}, u32[]{:S(2)}) collective-permute-start(f32[192,512]{1,0:T(8,128)S(1)} %collective-permute-done.10.refs_0_), channel_id=1, source_target_pairs={{0,8},{8,0},{16,24},{24,16},{1,9},{9,1},{17,25},{25,17},{2,10},{10... | collective-permute-start | bytes 1179656 | tf_op jit(solution)/shard_map/ppermute | solution.py:69
  51.1 6.4 %collective-permute-start.6 = (f32[64,512]{1,0:T(8,128)S(1)}, f32[64,512]{1,0:T(8,128)S(1)}, u32[]{:S(2)}, u32[]{:S(2)}) collective-permute-start(f32[64,512]{1,0:T(8,128)S(1)} %get-tuple-element.38), channel_id=1, source_target_pairs={{0,16},{8,24},{16,0},{24,8},{1,17},{9,25},{17,1},{25,9},{2,18},{10... | collective-permute-start | bytes 393224 | tf_op jit(solution)/shard_map/ppermute | solution.py:69
  57.4 16.7 %collective-permute-start.7 = (f32[64,512]{1,0:T(8,128)S(1)}, f32[64,512]{1,0:T(8,128)S(1)}, u32[]{:S(2)}, u32[]{:S(2)}) collective-permute-start(f32[64,512]{1,0:T(8,128)S(1)} %collective-permute-done.6.refs_2_), channel_id=1, source_target_pairs={{0,8},{8,0},{16,24},{24,16},{1,9},{9,1},{17,25},{25,17},{2,10},{10... | collective-permute-start | bytes 393224 | tf_op jit(solution)/shard_map/ppermute | solution.py:69
  58.6 3.7 %collective-permute-start.9 = (f32[16,1,128]{2,1,0:T(1,128)S(1)}, f32[16,1,128]{2,1,0:T(1,128)S(1)}, u32[]{:S(2)}, u32[]{:S(2)}) collective-permute-start(f32[16,1,128]{2,1,0:T(1,128)S(1)} %get-tuple-element.40), channel_id=1, source_target_pairs={{0,16},{8,24},{16,0},{24,8},{1,17},{9,25},{17,1},{25,9},{2,18},{10... | collective-permute-start | bytes 24584 | tf_op jit(solution)/shard_map/ppermute | solution.py:69
  62.9 8.8 %all-to-all-start.1 = ((f32[16,1,128]{2,1,0:T(1,128)}), f32[16,1,128]{2,1,0:T(1,128)S(1)}, u32[]{:S(2)}, u32[]{:S(2)}) async-start(f32[16,1,128]{2,1,0:T(1,128)} %add.11), calls=%async_computation.1 | async-start | bytes 16384 | tf_op jit(solution)/shard_map/all_to_all | solution.py:424

commit v2 on v1

--- a/solution.py
+++ b/solution.py
@@ -252,21 +252,16 @@
         dst[LOW] = polynomial(k, powers, 0).astype(bf16)
         dst[TOP, TOP] = polynomial(k, powers, 1).astype(bf16)
         dst[TOP, LOW] = dst[LOW, TOP].T
-    out[LOW] = mm(left[LOW], right[...]) + polynomial(rest, powers, 0)
+    top = mm(left[LOW], right[...]) + polynomial(rest, powers, 0)
     corner = mm(left[TOP], right[:, TOP]) + polynomial(rest, powers, 1)
-    out[HALF:, LOW] = corner[: HALF // 2]
-    out[HALF:, TOP] = corner[HALF // 2 :]
+    pack_into(out, top[:, :HALF], top[:, HALF:], corner)
     totals[...] = jnp.broadcast_to(grad_sq, (1, 128))
     fetch.wait()
 
 
-def root_corner(packed):
-    return jnp.concatenate([packed[HALF:, LOW], packed[HALF:, TOP]], axis=0)
-
-
 def half_way(g, packed, out, x):
     _, core = chip_core()
-    spread(packed[LOW], root_corner(packed), x)
+    spread(*unpack_upper(packed), x)
 
     @pl.when(core == 1)
     def _():
@@ -283,12 +278,12 @@
 
     @pl.when(core == 1)
     def _():
-        spread(packed[LOW], root_corner(packed), x)
+        spread(*unpack_upper(packed), x)
         mine[...] = dot3((middle[0, LOW], middle[1, LOW]), (x[0], x[1]))
 
     @pl.when(core == 0)
     def _():
-        mine[...] = dot3(split(packed[LOW]), (middle[0], middle[1]))
+        mine[...] = dot3(split(unpack_upper(packed)[0]), (middle[0], middle[1]))
 
     most[...], rest[...] = mine[:MOST], mine[MOST:]
     sums[...] = jnp.broadcast_to(lanes(mine[...] * mine[...])[None], sums.shape)
@@ -395,7 +390,7 @@
     new_packed = lax.ppermute(out_packed, "rep", [(t, s) for s, t in shuffle])
     mine_root, totals, g_split = call(
         functools.partial(root, devices),
-        [(HALF + HALF // 2, BLOCK), (1, 128), whole],
+        [(PACKED, BLOCK), (1, 128), whole],
         [VMEM, HBM] + [VMEM] * 4,
         [pltpu.VMEM(square, bf16)] * 2 + [pltpu.SemaphoreType.DMA],
         flops=unit,

time: 75.2 us -> 75.3 us (level)
  no operation moved by 1% of the time
where the time goes in v2:
time: 75.3 us; the launch traced here: 75 us
  waiting for transfers between devices  39.1 us (52%)
  starting transfers between devices  18.8 us (25%)
  Pallas kernels  15.6 us (21%)
  between operations  0.79 us (1%)
    ppermute x11, waiting for transfers between devices, flip(): lax.ppermute(x, 'rep', [(i, i ^ mask) for i in range(lax.axis_size('rep'))])  31.4 us
    all_to_all x1, starting transfers between devices, per_device(): sums = lax.all_to_all(sums, AXES, 0, 0)  6.95 us
    ppermute x11, starting transfers between devices, flip(): lax.ppermute(x, 'rep', [(i, i ^ mask) for i in range(lax.axis_size('rep'))])  6.62 us
    all_to_all x1, starting transfers between devices, per_device(): prec = lax.all_to_all(prec, AXES, 0, 0, axis_index_groups=groups)  3.83 us
    all_to_all x1, waiting for transfers between devices, per_device(): sums = lax.all_to_all(sums, AXES, 0, 0)  3.81 us
    all_to_all x1, waiting for transfers between devices, per_device(): prec = lax.all_to_all(prec, AXES, 0, 0, axis_index_groups=groups)  3.8 us
    pallas_call x1, Pallas kernels, per_device(): call(update_stat, [(2, 128)] + [(PACKED, BLOCK)] * 3 + [pltpu.HBM((2,) +...  3.35 us
    pallas_call x2, Pallas kernels, terms(): call(functools.partial(grad_terms, plan), [(len(chips),) + piece for chip...  3.04 us
  transfers between devices with their start and end apart: 15, of which 7 were waited for; matrix products, arithmetic and copies ran while one was open for 1% of the time, Pallas kernels for 15%

profile of v2, /device:TPU:0, one launch (start us, length us, event | category | flops | bytes accessed | tf_op | source)
XLA Modules:
  0.0 75.0 jit_solution(872009282362309410)
XLA Ops:
  0.7 1.5 %shard_map.60 = f32[1,256,512]{2,1,0:T(8,128)S(1)} custom-call(bf16[256,1024]{1,0:T(8,128)(2,1)} %acts.3, bf16[256,512]{1,0:T(8,128)(2,1)} %grads.3, s32[1,2]{1,0:T(1,128)} %owners.5), custom_call_target="tpu_custom_call" | custom-call | flops 67108864 | bytes 1048576 | tf_op jit(solution)/shard_map/pallas_call | solution.py:348
  2.7 1.5 %shard_map.59 = (f32[1,256,512]{2,1,0:T(8,128)S(1)}, f32[1,256,512]{2,1,0:T(8,128)S(1)}, f32[1,256,512]{2,1,0:T(8,128)S(1)}) custom-call(bf16[256,1024]{1,0:T(8,128)(2,1)} %acts.3, bf16[256,512]{1,0:T(8,128)(2,1)} %grads.3, s32[1,2]{1,0:T(1,128)} %owners.5), custom_call_target="tpu_custom_call" | custom-call | flops 201326592 | bytes 1048576 | tf_op jit(solution)/shard_map/pallas_call | solution.py:348
  4.4 3.0 %collective-permute-start.2 = (f32[256,512]{1,0:T(8,128)S(1)}, f32[256,512]{1,0:T(8,128)S(1)}, u32[]{:S(2)}, u32[]{:S(2)}) collective-permute-start(f32[256,512]{1,0:T(8,128)S(1)} %add_bitcast_fusion), channel_id=1, source_target_pairs={{0,16},{8,24},{16,0},{24,8},{1,17},{9,25},{17,1},{25,9},{2,18},{10... | collective-permute-start | bytes 1572872 | tf_op jit(solution)/shard_map/ppermute | solution.py:69
  8.1 11.7 %collective-permute-done.2.rest = f32[256,512]{1,0:T(8,128)S(1)} collective-permute-done((f32[256,512]{1,0:T(8,128)S(1)}, f32[256,512]{1,0:T(8,128)S(1)}, u32[]{:S(2)}, u32[]{:S(2)}) %collective-permute-start.2) | collective-permute-done | bytes 524320 | tf_op jit(solution)/shard_map/ppermute | solution.py:69
  19.8 0.8 %shard_map.62 = (f32[264,512]{1,0:T(8,128)S(1)}, f32[32,2,128]{2,1,0:T(2,128)}) custom-call(f32[1,256,512]{2,1,0:T(8,128)S(1)} %get-tuple-element.24.keep, f32[1,256,512]{2,1,0:T(8,128)S(1)} %collective-permute-done.got, f32[256,512]{1,0:T(8,128)S(1)} %collective-permute-done.2.rest, f32[1,128]{1,0:T(1,128)S(1)} %get-tuple-element.27.trace), custom_call_target="tpu_custom_call" | custom-call | bytes 1048576 | tf_op jit(solution)/shard_map/pallas_call | solution.py:376
  20.6 6.9 %all-to-all-start = ((f32[32,2,128]{2,1,0:T(2,128)}), f32[32,2,128]{2,1,0:T(2,128)S(1)}, u32[]{:S(2)}, u32[]{:S(2)}) async-start(f32[32,2,128]{2,1,0:T(2,128)} %get-tuple-element.35), calls=%async_computation | async-start | bytes 65536 | tf_op jit(solution)/shard_map/all_to_all | solution.py:380
  27.6 3.4 %shard_map.63 = (f32[2,128]{1,0:T(2,128)S(1)}, f32[264,512]{1,0:T(8,128)S(1)}, f32[264,512]{1,0:T(8,128)S(1)}, f32[264,512]{1,0:T(8,128)S(1)}, bf16[2,512,512]{2,1,0:T(8,128)(2,1)}) custom-call(f32[264,512]{1,0:T(8,128)S(1)} %get-tuple-element.28.half, ...), custom_call_target="tpu_custom_call", output_to_operand_aliasing={{3}: (0, {}), {2}: (1, {}), {1}: (2, {})} | custom-call | flops 2415919104 | bytes 1048576 | tf_op jit(solution)/shard_map/pallas_call | solution.py:381
  30.9 3.8 %all-to-all-done.sums = f32[32,2,128]{2,1,0:T(2,128)S(1)} async-done(((f32[32,2,128]{2,1,0:T(2,128)}), f32[32,2,128]{2,1,0:T(2,128)S(1)}, u32[]{:S(2)}, u32[]{:S(2)}) %all-to-all-start) | async-done | bytes 32800 | tf_op jit(solution)/shard_map/all_to_all | solution.py:380
  34.7 1.6 %shard_map.64 = (f32[264,512]{1,0:T(8,128)S(1)}, f32[1,128]{1,0:T(1,128)S(1)}, bf16[2,512,512]{2,1,0:T(8,128)(2,1)S(1)}) custom-call(f32[264,512]{1,0:T(8,128)S(1)} %get-tuple-element.30.stat, bf16[2,512,512]{2,1,0:T(8,128)(2,1)} %get-tuple-element.31.g_in, f32[264,512]{1,0:T(8,128)S(1)} %get-tuple-element.32.square, ...), custom_call_target="tpu_custom_call" | custom-call | flops 805306368 | bytes 1048576 | tf_op jit(solution)/shard_map/pallas_call | solution.py:391
  36.5 1.2 %shard_map.65.middle = bf16[2,512,512]{2,1,0:T(8,128)(2,1)S(1)} custom-call(bf16[2,512,512]{2,1,0:T(8,128)(2,1)S(1)} %get-tuple-element.36.g, f32[264,512]{1,0:T(8,128)S(1)} %get-tuple-element.37.packed), custom_call_target="tpu_custom_call" | custom-call | flops 805306368 | bytes 1048576 | tf_op jit(solution)/shard_map/pallas_call | solution.py:399
  38.3 0.7 shard_map.66
  39.1 0.7 collective-permute-start.10
  39.8 1.4 %collective-permute-start.12 = (f32[264,512]{1,0:T(8,128)S(1)}, f32[264,512]{1,0:T(8,128)S(1)}, u32[]{:S(2)}, u32[]{:S(2)}) collective-permute-start(f32[264,512]{1,0:T(8,128)S(1)} %get-tuple-element.30.stat), channel_id=1, source_target_pairs={{8,0},{24,8},{0,16},{16,24},{9,1},{25,9},{1,17},{17,25},{10,2},{26... | collective-permute-start | bytes 1622024 | tf_op jit(solution)/shard_map/ppermute | solution.py:390
  41.2 10.0 %collective-permute-done.10.refs_0_ = f32[192,512]{1,0:T(8,128)S(1)} collective-permute-done((f32[192,512]{1,0:T(8,128)S(1)}, f32[192,512]{1,0:T(8,128)S(1)}, u32[]{:S(2)}, u32[]{:S(2)}) %collective-permute-start.10) | collective-permute-done | bytes 393248 | tf_op jit(solution)/shard_map/ppermute | solution.py:69
  51.1 6.4 %collective-permute-done.6.refs_2_ = f32[64,512]{1,0:T(8,128)S(1)} collective-permute-done((f32[64,512]{1,0:T(8,128)S(1)}, f32[64,512]{1,0:T(8,128)S(1)}, u32[]{:S(2)}, u32[]{:S(2)}) %collective-permute-start.6) | collective-permute-done | bytes 131104 | tf_op jit(solution)/shard_map/ppermute | solution.py:69
  57.5 1.3 %collective-permute-start.7 = (f32[64,512]{1,0:T(8,128)S(1)}, f32[64,512]{1,0:T(8,128)S(1)}, u32[]{:S(2)}, u32[]{:S(2)}) collective-permute-start(f32[64,512]{1,0:T(8,128)S(1)} %collective-permute-done.6.refs_2_), channel_id=1, source_target_pairs={{0,8},{8,0},{16,24},{24,16},{1,9},{9,1},{17,25},{25,17},{2,10},{10... | collective-permute-start | bytes 393224 | tf_op jit(solution)/shard_map/ppermute | solution.py:69
  58.7 0.8 %collective-permute-start.9 = (f32[16,1,128]{2,1,0:T(1,128)S(1)}, f32[16,1,128]{2,1,0:T(1,128)S(1)}, u32[]{:S(2)}, u32[]{:S(2)}) collective-permute-start(f32[16,1,128]{2,1,0:T(1,128)S(1)} %get-tuple-element.40), channel_id=1, source_target_pairs={{0,16},{8,24},{16,0},{24,8},{1,17},{9,25},{17,1},{25,9},{2,18},{10... | collective-permute-start | bytes 24584 | tf_op jit(solution)/shard_map/ppermute | solution.py:69
  59.6 2.8 %collective-permute-done.9 = f32[16,1,128]{2,1,0:T(1,128)S(1)} collective-permute-done((f32[16,1,128]{2,1,0:T(1,128)S(1)}, f32[16,1,128]{2,1,0:T(1,128)S(1)}, u32[]{:S(2)}, u32[]{:S(2)}) %collective-permute-start.9) | collective-permute-done | bytes 8224 | tf_op jit(solution)/shard_map/ppermute | solution.py:69
  63.0 3.8 %all-to-all-start.1 = ((f32[16,1,128]{2,1,0:T(1,128)}), f32[16,1,128]{2,1,0:T(1,128)S(1)}, u32[]{:S(2)}, u32[]{:S(2)}) async-start(f32[16,1,128]{2,1,0:T(1,128)} %add.11), calls=%async_computation.1 | async-start | bytes 16384 | tf_op jit(solution)/shard_map/all_to_all | solution.py:419
  66.8 1.2 %shard_map.70 = f32[512,512]{1,0:T(8,128)} custom-call(f32[264,512]{1,0:T(8,128)S(1)} %collective-permute-done.12.packed), custom_call_target="tpu_custom_call" | custom-call | bytes 1048576 | tf_op jit(solution)/shard_map/pallas_call | solution.py:420
  68.0 3.8 %all-to-all-done.1.refs_2_ = f32[16,1,128]{2,1,0:T(1,128)S(1)} async-done(((f32[16,1,128]{2,1,0:T(1,128)}), f32[16,1,128]{2,1,0:T(1,128)S(1)}, u32[]{:S(2)}, u32[]{:S(2)}) %all-to-all-start.1) | async-done | bytes 8224 | tf_op jit(solution)/shard_map/all_to_all | solution.py:419
  71.8 1.2 %shard_map.67 = (f32[1024,512]{1,0:T(8,128)}, f32[1,128]{1,0:T(1,128)S(1)}) custom-call(f32[256,512]{1,0:T(8,128)S(1)} %get-tuple-element.39.refs_0_, f32[256,512]{1,0:T(8,128)S(1)} %collective-permute-done.8.refs_1_, f32[16,1,128]{2,1,0:T(1,128)S(1)} %all-to-all-done.1.refs_2_, f32[1,128]{1,0:T(1,128)S(1)} %get-tuple-element.41.refs_3_, ...), custom_call_target="tpu_custom_call" | custom-call | bytes 1048576 | tf_op jit(solution)/shard_map/pallas_call | solution.py:440
  73.1 1.1 %shard_map.68.refs_3_ = f32[1024,512]{1,0:T(8,128)} custom-call(f32[192,512]{1,0:T(8,128)S(1)} %collective-permute-done.10.refs_0_, f32[192,512]{1,0:T(8,128)S(1)} %collective-permute-done.11.refs_1_, f32[64,512]{1,0:T(8,128)S(1)} %collective-permute-done.6.refs_2_, f32[1,128]{1,0:T(1,128)S(1)} %get-tuple-element.43.refs_3_.refs_1_, ...), custom_call_target="tpu_custom_call", output_to_operand_aliasing={{}: (5, {})} | custom-call | bytes 1048576 | tf_op jit(solution)/shard_map/pallas_call | solution.py:428
  74.2 0.8 %shard_map.69 = f32[1024,512]{1,0:T(8,128)} custom-call(f32[64,512]{1,0:T(8,128)S(1)} %collective-permute-done.7.refs_0_, f32[1,128]{1,0:T(1,128)S(1)} %get-tuple-element.43.refs_3_.refs_1_, f32[4,128]{1,0:T(4,128)S(1)} %get-tuple-element.42.refs_4_.refs_2_, f32[1024,512]{1,0:T(8,128)} %shard_map.68.refs_3_), custom_call_target="tpu_custom_call", output_to_operand_aliasing={{}: (3, {})} | custom-call | bytes 1048576 | tf_op jit(solution)/shard_map/pallas_call | solution.py:428
  (24 shorter events, 2.8 us)
Async XLA Ops:
  0.6 6.8 %copy-start.1 = (s32[1,2]{1,0:T(1,128)S(1)}, s32[1,2]{1,0:T(1,128)}, u32[]{:S(2)}) copy-start(s32[1,2]{1,0:T(1,128)} %owners.5) | copy-start | bytes 28
  0.6 6.8 %copy-start = (f32[1,1,512,512]{3,2,1,0:T(8,128)S(1)}, f32[1,1,512,512]{3,2,1,0:T(8,128)}, u32[]{:S(2)}) copy-start(f32[1,1,512,512]{3,2,1,0:T(8,128)} %param.6) | copy-start | bytes 3145732
  2.1 2.2 %collective-permute-start.1 = (f32[1,256,512]{2,1,0:T(8,128)S(1)}, f32[1,256,512]{2,1,0:T(8,128)S(1)}, u32[]{:S(2)}, u32[]{:S(2)}) collective-permute-start(f32[1,256,512]{2,1,0:T(8,128)S(1)} %shard_map.60), channel_id=1, source_target_pairs={{0,8},{8,0},{16,24},{24,16},{1,9},{9,1},{17,25},{25,17},{2,10},{10... | collective-permute-start | bytes 1572872 | tf_op jit(solution)/shard_map/ppermute | solution.py:69
  4.3 3.8 %collective-permute-start = (f32[1,256,512]{2,1,0:T(8,128)S(1)}, f32[1,256,512]{2,1,0:T(8,128)S(1)}, u32[]{:S(2)}, u32[]{:S(2)}) collective-permute-start(f32[1,256,512]{2,1,0:T(8,128)S(1)} %get-tuple-element.25), channel_id=1, source_target_pairs={{0,8},{8,0},{16,24},{24,16},{1,9},{9,1},{17,25},{25,17},{2,10},{10... | collective-permute-start | bytes 1572872 | tf_op jit(solution)/shard_map/ppermute | solution.py:69
  4.4 15.3 %collective-permute-start.2 = (f32[256,512]{1,0:T(8,128)S(1)}, f32[256,512]{1,0:T(8,128)S(1)}, u32[]{:S(2)}, u32[]{:S(2)}) collective-permute-start(f32[256,512]{1,0:T(8,128)S(1)} %add_bitcast_fusion), channel_id=1, source_target_pairs={{0,16},{8,24},{16,0},{24,8},{1,17},{9,25},{17,1},{25,9},{2,18},{10... | collective-permute-start | bytes 1572872 | tf_op jit(solution)/shard_map/ppermute | solution.py:69
  8.1 19.5 %collective-permute-start.4 = (f32[264,512]{1,0:T(8,128)S(1)}, f32[264,512]{1,0:T(8,128)S(1)}, u32[]{:S(2)}, u32[]{:S(2)}) collective-permute-start(f32[264,512]{1,0:T(8,128)S(1)} %get-tuple-element.29), channel_id=1, source_target_pairs={{0,8},{8,24},{16,0},{24,16},{1,9},{9,25},{17,1},{25,17},{2,10},{10... | collective-permute-start | bytes 1622024 | tf_op jit(solution)/shard_map/ppermute | solution.py:375
  20.6 7.0 %collective-permute-start.3 = (f32[264,512]{1,0:T(8,128)S(1)}, f32[264,512]{1,0:T(8,128)S(1)}, u32[]{:S(2)}, u32[]{:S(2)}) collective-permute-start(f32[264,512]{1,0:T(8,128)S(1)} %get-tuple-element.28.half), channel_id=1, source_target_pairs={{0,8},{8,0},{16,24},{24,16},{1,9},{9,1},{17,25},{25,17},{2,10},{10... | collective-permute-start | bytes 1622024 | tf_op jit(solution)/shard_map/ppermute | solution.py:69
  20.6 14.1 %all-to-all-start = ((f32[32,2,128]{2,1,0:T(2,128)}), f32[32,2,128]{2,1,0:T(2,128)S(1)}, u32[]{:S(2)}, u32[]{:S(2)}) async-start(f32[32,2,128]{2,1,0:T(2,128)} %get-tuple-element.35), calls=%async_computation | async-start | bytes 65536 | tf_op jit(solution)/shard_map/all_to_all | solution.py:380
  36.3 2.0 %collective-permute-start.5 = (f32[264,512]{1,0:T(8,128)S(1)}, f32[264,512]{1,0:T(8,128)S(1)}, u32[]{:S(2)}, u32[]{:S(2)}) collective-permute-start(f32[264,512]{1,0:T(8,128)S(1)} %get-tuple-element.37.packed), channel_id=1, source_target_pairs={{0,8},{8,0},{16,24},{24,16},{1,9},{9,1},{17,25},{25,17},{2,10},{10... | collective-permute-start | bytes 1622024 | tf_op jit(solution)/shard_map/ppermute | solution.py:69
  39.1 12.1 %collective-permute-start.10 = (f32[192,512]{1,0:T(8,128)S(1)}, f32[192,512]{1,0:T(8,128)S(1)}, u32[]{:S(2)}, u32[]{:S(2)}) collective-permute-start(f32[192,512]{1,0:T(8,128)S(1)} %get-tuple-element.44), channel_id=1, source_target_pairs={{0,16},{8,24},{16,0},{24,8},{1,17},{9,25},{17,1},{25,9},{2,18},{10... | collective-permute-start | bytes 1179656 | tf_op jit(solution)/shard_map/ppermute | solution.py:69
  39.8 27.1 %collective-permute-start.12 = (f32[264,512]{1,0:T(8,128)S(1)}, f32[264,512]{1,0:T(8,128)S(1)}, u32[]{:S(2)}, u32[]{:S(2)}) collective-permute-start(f32[264,512]{1,0:T(8,128)S(1)} %get-tuple-element.30.stat), channel_id=1, source_target_pairs={{8,0},{24,8},{0,16},{16,24},{9,1},{25,9},{1,17},{17,25},{10,2},{26... | collective-permute-start | bytes 1622024 | tf_op jit(solution)/shard_map/ppermute | solution.py:390
  41.1 30.7 %collective-permute-start.8 = (f32[256,512]{1,0:T(8,128)S(1)}, f32[256,512]{1,0:T(8,128)S(1)}, u32[]{:S(2)}, u32[]{:S(2)}) collective-permute-start(f32[256,512]{1,0:T(8,128)S(1)} %get-tuple-element.39.refs_0_), channel_id=1, source_target_pairs={{0,8},{8,0},{16,24},{24,16},{1,9},{9,1},{17,25},{25,17},{2,10},{10... | collective-permute-start | bytes 1572872 | tf_op jit(solution)/shard_map/ppermute | solution.py:69
  51.1 21.9 %collective-permute-start.11 = (f32[192,512]{1,0:T(8,128)S(1)}, f32[192,512]{1,0:T(8,128)S(1)}, u32[]{:S(2)}, u32[]{:S(2)}) collective-permute-start(f32[192,512]{1,0:T(8,128)S(1)} %collective-permute-done.10.refs_0_), channel_id=1, source_target_pairs={{0,8},{8,0},{16,24},{24,16},{1,9},{9,1},{17,25},{25,17},{2,10},{10... | collective-permute-start | bytes 1179656 | tf_op jit(solution)/shard_map/ppermute | solution.py:69
  51.1 6.4 %collective-permute-start.6 = (f32[64,512]{1,0:T(8,128)S(1)}, f32[64,512]{1,0:T(8,128)S(1)}, u32[]{:S(2)}, u32[]{:S(2)}) collective-permute-start(f32[64,512]{1,0:T(8,128)S(1)} %get-tuple-element.38), channel_id=1, source_target_pairs={{0,16},{8,24},{16,0},{24,8},{1,17},{9,25},{17,1},{25,9},{2,18},{10... | collective-permute-start | bytes 393224 | tf_op jit(solution)/shard_map/ppermute | solution.py:69
  57.5 16.7 %collective-permute-start.7 = (f32[64,512]{1,0:T(8,128)S(1)}, f32[64,512]{1,0:T(8,128)S(1)}, u32[]{:S(2)}, u32[]{:S(2)}) collective-permute-start(f32[64,512]{1,0:T(8,128)S(1)} %collective-permute-done.6.refs_2_), channel_id=1, source_target_pairs={{0,8},{8,0},{16,24},{24,16},{1,9},{9,1},{17,25},{25,17},{2,10},{10... | collective-permute-start | bytes 393224 | tf_op jit(solution)/shard_map/ppermute | solution.py:69
  58.7 3.7 %collective-permute-start.9 = (f32[16,1,128]{2,1,0:T(1,128)S(1)}, f32[16,1,128]{2,1,0:T(1,128)S(1)}, u32[]{:S(2)}, u32[]{:S(2)}) collective-permute-start(f32[16,1,128]{2,1,0:T(1,128)S(1)} %get-tuple-element.40), channel_id=1, source_target_pairs={{0,16},{8,24},{16,0},{24,8},{1,17},{9,25},{17,1},{25,9},{2,18},{10... | collective-permute-start | bytes 24584 | tf_op jit(solution)/shard_map/ppermute | solution.py:69
  63.0 8.8 %all-to-all-start.1 = ((f32[16,1,128]{2,1,0:T(1,128)}), f32[16,1,128]{2,1,0:T(1,128)S(1)}, u32[]{:S(2)}, u32[]{:S(2)}) async-start(f32[16,1,128]{2,1,0:T(1,128)} %add.11), calls=%async_computation.1 | async-start | bytes 16384 | tf_op jit(solution)/shard_map/all_to_all | solution.py:419

commit v3 on v2

--- a/solution.py
+++ b/solution.py
@@ -138,16 +138,16 @@
     for copy in copies:
         copy.wait()
     cotangent = gv[...]
-    for out, (chips, swapped) in zip(outs, plan):
+    for out, (chips, swapped, first, count) in zip(outs, plan):
         half = 1 - core if swapped else core
         for n, j in enumerate(chips):
-            start = ov[0, chip ^ j] * BLOCK + half * HALF
-            cols = av[:, pl.ds(pl.multiple_of(start, HALF), HALF)]
+            start = ov[0, chip ^ j] * BLOCK + half * HALF + first
+            cols = av[:, pl.ds(pl.multiple_of(start, 128), count)]
             out[n] = lax.dot_general(cols, cotangent, (((0,), (0,)), ((), ())), preferred_element_type=f32)
 
 
-def finish_half(devices, keep, got, rest, trace, half, sums):
-    value = keep[0] + got[0] + rest[...]
+def finish_half(devices, keep, got, rest_a, rest_b, trace, half, sums):
+    value = keep[0] + got[0] + jnp.concatenate([rest_a[...], rest_b[...]], axis=0)
     half[LOW] = value
     half[HALF:] = jnp.zeros((PACKED - HALF, BLOCK), f32)
     both = jnp.concatenate([lanes(value * value), trace[...]], axis=0)
@@ -233,7 +233,7 @@
     return taken(SMALL_CUBIC, jnp.ones_like(e)), taken(ROOT_FACTOR, outer), taken(ROOT_REST, outer), grad_sq
 
 
-def root(devices, stat, g_in, square, cubed, facts, sums, out, totals, g, left, right, sem):
+def root(devices, stat, g_in, square, cubed, facts, sums, out, low, totals, g, left, right, sem):
     fetch = pltpu.make_async_copy(g_in, g, sem)
     fetch.start()
     small, factor, rest, grad_sq = coefficients(devices, facts, sums)
@@ -252,16 +252,15 @@
         dst[LOW] = polynomial(k, powers, 0).astype(bf16)
         dst[TOP, TOP] = polynomial(k, powers, 1).astype(bf16)
         dst[TOP, LOW] = dst[LOW, TOP].T
-    top = mm(left[LOW], right[...]) + polynomial(rest, powers, 0)
-    corner = mm(left[TOP], right[:, TOP]) + polynomial(rest, powers, 1)
-    pack_into(out, top[:, :HALF], top[:, HALF:], corner)
+    out[...] = mm(left[LOW], right[...]) + polynomial(rest, powers, 0)
+    low[...] = mm(left[TOP], right[:, TOP]) + polynomial(rest, powers, 1)
     totals[...] = jnp.broadcast_to(grad_sq, (1, 128))
     fetch.wait()
 
 
-def half_way(g, packed, out, x):
+def half_way(g, upper, corner, out, x):
     _, core = chip_core()
-    spread(*unpack_upper(packed), x)
+    spread(upper[...], corner[...], x)
 
     @pl.when(core == 1)
     def _():
@@ -273,17 +272,17 @@
         out[0], out[1] = split(dot3((g[0], g[1]), (x[0], x[1])))
 
 
-def last_product(middle, packed, mine, most, rest, sums, x):
+def last_product(middle, upper, corner, mine, most, rest, sums, x):
     _, core = chip_core()
 
     @pl.when(core == 1)
     def _():
-        spread(*unpack_upper(packed), x)
+        spread(upper[...], corner[...], x)
         mine[...] = dot3((middle[0, LOW], middle[1, LOW]), (x[0], x[1]))
 
     @pl.when(core == 0)
     def _():
-        mine[...] = dot3(split(unpack_upper(packed)[0]), (middle[0], middle[1]))
+        mine[...] = dot3(split(upper[...]), (middle[0], middle[1]))
 
     most[...], rest[...] = mine[:MOST], mine[MOST:]
     sums[...] = jnp.broadcast_to(lanes(mine[...] * mine[...])[None], sums.shape)
@@ -347,7 +346,7 @@
     def terms(*plan):
         return call(
             functools.partial(grad_terms, plan),
-            [(len(chips),) + piece for chips, _ in plan],
+            [(len(chips), count, BLOCK) for chips, _, _, count in plan],
             [HBM] * 3,
             [
                 pltpu.VMEM(activations.shape, bf16),
@@ -355,27 +354,35 @@
                 pltpu.SMEM(owner_blocks.shape, jnp.int32),
                 pltpu.SemaphoreType.DMA((3,)),
             ],
-            flops=2 * tokens * HALF * BLOCK * sum(len(chips) for chips, _ in plan),
+            flops=2 * tokens * HALF * BLOCK * len(plan),
         )(*(in_hbm(x) for x in (activations, out_grads, owner_blocks)))
 
     above, below = range(m, pairs), range(m)
-    (send_far,) = terms((above, True))
-    got_far = flip(send_far, 1)
-    keep_far, send_near, keep_near = terms((above, False), (below, True), (below, False))
+    quarter = HALF // 2
+    send_a, send_b, keep_a, keep_b = terms(
+        (above, True, 0, quarter), (above, True, quarter, quarter), (above, False, 0, quarter), (above, False, quarter, quarter)
+    )
+    got_a = flip(send_a, 1)
+    got_b = flip(send_b, 1)
+    arrived_a = [flip(keep_a[j] + got_a[j], 2 * m) for j in range(m)]
+    arrived_b = [flip(keep_b[j] + got_b[j], 2 * m) for j in range(m)]
+    send_near, keep_near = terms((below, True, 0, HALF), (below, False, 0, HALF))
     got_near = flip(send_near, 1)
-    arrived = [flip(keep_far[j] + got_far[j], 2 * m) for j in range(m)]
+    arrived = list(zip(arrived_a, arrived_b))
     while m > 1:
         m //= 2
+        arrived = [jnp.concatenate(x) for x in arrived]
         held = [keep_near[j] + got_near[j] + arrived[j] for j in range(m, 2 * m)]
         arrived = [x + flip(y, 2 * m) for x, y in zip(arrived, held)]
+        arrived = [(x[:quarter], x[quarter:]) for x in arrived]
     shuffle = [(s * pairs + p, 2 * p + 1 - s) for s in range(2) for p in range(pairs)]
     packed, trace, rows = call(
         functools.partial(pack_stat, pairs), [(PACKED, BLOCK), (1, 128), (2 * pairs, 128)], [VMEM, SMEM]
     )(statistics[0, 0], owner_blocks)
     old = lax.ppermute(packed, "rep", shuffle)
     half, sums = call(
-        functools.partial(finish_half, devices), [(PACKED, BLOCK), (devices, 2, 128)], [VMEM] * 4
-    )(keep_near, got_near, arrived[0], trace)
+        functools.partial(finish_half, devices), [(PACKED, BLOCK), (devices, 2, 128)], [VMEM] * 5
+    )(keep_near, got_near, *arrived[0], trace)
     other = flip(half, 1)
     sums = lax.all_to_all(sums, AXES, 0, 0)
     facts, square_p, cube_p, out_packed, g_split = call(
@@ -388,16 +395,17 @@
         input_output_aliases={0: 3, 1: 2, 2: 1},
     )(half, other, old)
     new_packed = lax.ppermute(out_packed, "rep", [(t, s) for s, t in shuffle])
-    mine_root, totals, g_split = call(
+    upper, corner, totals, g_split = call(
         functools.partial(root, devices),
-        [(PACKED, BLOCK), (1, 128), whole],
+        [piece, (HALF, HALF), (1, 128), whole],
         [VMEM, HBM] + [VMEM] * 4,
         [pltpu.VMEM(square, bf16)] * 2 + [pltpu.SemaphoreType.DMA],
         flops=unit,
     )(out_packed, in_hbm(g_split), square_p, cube_p, facts, sums)
-    other_root = flip(mine_root, 1)
-    (middle,) = call(half_way, [whole], [VMEM] * 2, [split_square], flops=unit)(g_split, mine_root)
-    mine, most, rest, prec = call(last_product, [piece, (MOST, BLOCK), (HALF - MOST, BLOCK), (2 * stripes, 1, 128)], [VMEM] * 2, [split_square], flops=unit)(middle, other_root)
+    other_upper = flip(upper, 1)
+    other_corner = flip(corner, 1)
+    (middle,) = call(half_way, [whole], [VMEM] * 3, [split_square], flops=unit)(g_split, upper, corner)
+    mine, most, rest, prec = call(last_product, [piece, (MOST, BLOCK), (HALF - MOST, BLOCK), (2 * stripes, 1, 128)], [VMEM] * 3, [split_square], flops=unit)(middle, other_upper, other_corner)
 
     bit = 2
     while bit < rep_count:

time: 75.3 us -> 76 us (level)
    ppermute x11 -> x14, starting transfers between devices: 6.62 us -> 7.15 us  [flip(): lax.ppermute(x, 'rep', [(i, i ^ mask) for i in range(lax.axis_size('rep'))])]
    ppermute x11 -> x14, waiting for transfers between devices: 31.4 us -> 31.4 us  [flip(): lax.ppermute(x, 'rep', [(i, i ^ mask) for i in range(lax.axis_size('rep'))])]
  transfers between devices with their start and end apart: 15 -> 18, of which waited for: 7 -> 8; matrix products, arithmetic and copies ran while one was open for 1% -> 1% of each run, Pallas kernels for 15% -> 14%
where the time goes in v3:
time: 76 us; the launch traced here: 75.7 us
  waiting for transfers between devices  39 us (51%)
  starting transfers between devices  19.3 us (25%)
  Pallas kernels  16 us (21%)
  between operations  0.79 us (1%)
    ppermute x14, waiting for transfers between devices, flip(): lax.ppermute(x, 'rep', [(i, i ^ mask) for i in range(lax.axis_size('rep'))])  31.4 us
    ppermute x14, starting transfers between devices, flip(): lax.ppermute(x, 'rep', [(i, i ^ mask) for i in range(lax.axis_size('rep'))])  7.15 us
    all_to_all x1, starting transfers between devices, per_device(): sums = lax.all_to_all(sums, AXES, 0, 0)  6.74 us
    all_to_all x1, starting transfers between devices, per_device(): prec = lax.all_to_all(prec, AXES, 0, 0, axis_index_groups=groups)  3.83 us
    all_to_all x1, waiting for transfers between devices, per_device(): sums = lax.all_to_all(sums, AXES, 0, 0)  3.81 us
    all_to_all x1, waiting for transfers between devices, per_device(): prec = lax.all_to_all(prec, AXES, 0, 0, axis_index_groups=groups)  3.8 us
    pallas_call x1, Pallas kernels, per_device(): call(update_stat, [(2, 128)] + [(PACKED, BLOCK)] * 3 + [pltpu.HBM((2,) +...  3.35 us
    pallas_call x2, Pallas kernels, terms(): call(functools.partial(grad_terms, plan), [(len(chips), count, BLOCK) for...  3.04 us
  transfers between devices with their start and end apart: 18, of which 8 were waited for; matrix products, arithmetic and copies ran while one was open for 1% of the time, Pallas kernels for 14%

profile of v3, /device:TPU:0, one launch (start us, length us, event | category | flops | bytes accessed | tf_op | source)
XLA Modules:
  0.0 75.7 jit_solution(2115363183739557543)
XLA Ops:
  0.7 1.6 %shard_map.60 = (f32[1,128,512]{2,1,0:T(8,128)S(1)}, f32[1,128,512]{2,1,0:T(8,128)S(1)}, f32[1,128,512]{2,1,0:T(8,128)S(1)}, f32[1,128,512]{2,1,0:T(8,128)S(1)}) custom-call(bf16[256,1024]{1,0:T(8,128)(2,1)} %acts.3, bf16[256,512]{1,0:T(8,128)(2,1)} %grads.3, s32[1,2]{1,0:T(1,128)} %owners.5), custom_call_target="tpu_custom_call" | custom-call | flops 268435456 | bytes 1048576 | tf_op jit(solution)/shard_map/pallas_call | solution.py:347
  2.9 1.5 %shard_map.59 = (f32[1,256,512]{2,1,0:T(8,128)S(1)}, f32[1,256,512]{2,1,0:T(8,128)S(1)}) custom-call(bf16[256,1024]{1,0:T(8,128)(2,1)} %acts.3, bf16[256,512]{1,0:T(8,128)(2,1)} %grads.3, s32[1,2]{1,0:T(1,128)} %owners.5), custom_call_target="tpu_custom_call" | custom-call | flops 134217728 | bytes 1048576 | tf_op jit(solution)/shard_map/pallas_call | solution.py:347
  4.9 2.6 %collective-permute-start.2 = (f32[128,512]{1,0:T(8,128)S(1)}, f32[128,512]{1,0:T(8,128)S(1)}, u32[]{:S(2)}, u32[]{:S(2)}) collective-permute-start(f32[128,512]{1,0:T(8,128)S(1)} %add_bitcast_fusion.1), channel_id=1, source_target_pairs={{0,16},{8,24},{16,0},{24,8},{1,17},{9,25},{17,1},{25,9},{2,18},{10... | collective-permute-start | bytes 786440 | tf_op jit(solution)/shard_map/ppermute | solution.py:69
  8.4 6.2 %collective-permute-done.2.rest_a = f32[128,512]{1,0:T(8,128)S(1)} collective-permute-done((f32[128,512]{1,0:T(8,128)S(1)}, f32[128,512]{1,0:T(8,128)S(1)}, u32[]{:S(2)}, u32[]{:S(2)}) %collective-permute-start.2) | collective-permute-done | bytes 262176 | tf_op jit(solution)/shard_map/ppermute | solution.py:69
  14.7 5.4 %collective-permute-done.4.rest_b = f32[128,512]{1,0:T(8,128)S(1)} collective-permute-done((f32[128,512]{1,0:T(8,128)S(1)}, f32[128,512]{1,0:T(8,128)S(1)}, u32[]{:S(2)}, u32[]{:S(2)}) %collective-permute-start.4) | collective-permute-done | bytes 262176 | tf_op jit(solution)/shard_map/ppermute | solution.py:69
  20.0 0.8 %shard_map.62 = (f32[264,512]{1,0:T(8,128)S(1)}, f32[32,2,128]{2,1,0:T(2,128)}) custom-call(f32[1,256,512]{2,1,0:T(8,128)S(1)} %get-tuple-element.28.keep, f32[1,256,512]{2,1,0:T(8,128)S(1)} %collective-permute-done.got, f32[128,512]{1,0:T(8,128)S(1)} %collective-permute-done.2.rest_a, f32[128,512]{1,0:T(8,128)S(1)} %collective-permute-done.4.rest_b, ...), custom_call_target="tpu_custom_call" | custom-call | bytes 1048576 | tf_op jit(solution)/shard_map/pallas_call | solution.py:383
  20.8 6.7 %all-to-all-start = ((f32[32,2,128]{2,1,0:T(2,128)}), f32[32,2,128]{2,1,0:T(2,128)S(1)}, u32[]{:S(2)}, u32[]{:S(2)}) async-start(f32[32,2,128]{2,1,0:T(2,128)} %get-tuple-element.42), calls=%async_computation | async-start | bytes 65536 | tf_op jit(solution)/shard_map/all_to_all | solution.py:387
  27.6 3.4 %shard_map.63 = (f32[2,128]{1,0:T(2,128)S(1)}, f32[264,512]{1,0:T(8,128)S(1)}, f32[264,512]{1,0:T(8,128)S(1)}, f32[264,512]{1,0:T(8,128)S(1)}, bf16[2,512,512]{2,1,0:T(8,128)(2,1)}) custom-call(f32[264,512]{1,0:T(8,128)S(1)} %get-tuple-element.35.half, ...), custom_call_target="tpu_custom_call", output_to_operand_aliasing={{3}: (0, {}), {2}: (1, {}), {1}: (2, {})} | custom-call | flops 2415919104 | bytes 1048576 | tf_op jit(solution)/shard_map/pallas_call | solution.py:388
  31.0 3.8 %all-to-all-done.sums = f32[32,2,128]{2,1,0:T(2,128)S(1)} async-done(((f32[32,2,128]{2,1,0:T(2,128)}), f32[32,2,128]{2,1,0:T(2,128)S(1)}, u32[]{:S(2)}, u32[]{:S(2)}) %all-to-all-start) | async-done | bytes 32800 | tf_op jit(solution)/shard_map/all_to_all | solution.py:387
  34.8 2.0 %shard_map.64 = (f32[256,512]{1,0:T(8,128)S(1)}, f32[256,256]{1,0:T(8,128)S(1)}, f32[1,128]{1,0:T(1,128)S(1)}, bf16[2,512,512]{2,1,0:T(8,128)(2,1)S(1)}) custom-call(f32[264,512]{1,0:T(8,128)S(1)} %get-tuple-element.37.stat, bf16[2,512,512]{2,1,0:T(8,128)(2,1)} %get-tuple-element.38.g_in, f32[264,512]{1,0:T(8,128)S(1)} %get-tuple-element.39.square, ...), custom_call_target="tpu_custom_call" | custom-call | flops 805306368 | bytes 1048576 | tf_op jit(solution)/shard_map/pallas_call | solution.py:398
  37.4 1.2 %shard_map.65.middle = bf16[2,512,512]{2,1,0:T(8,128)(2,1)S(1)} custom-call(bf16[2,512,512]{2,1,0:T(8,128)(2,1)S(1)} %get-tuple-element.43.g, f32[256,512]{1,0:T(8,128)S(1)} %get-tuple-element.44.upper, f32[256,256]{1,0:T(8,128)S(1)} %get-tuple-element.45.corner), custom_call_target="tpu_custom_call" | custom-call | flops 805306368 | bytes 1048576 | tf_op jit(solution)/shard_map/pallas_call | solution.py:407
  39.8 0.7 collective-permute-start.13
  40.5 1.4 %collective-permute-start.15 = (f32[264,512]{1,0:T(8,128)S(1)}, f32[264,512]{1,0:T(8,128)S(1)}, u32[]{:S(2)}, u32[]{:S(2)}) collective-permute-start(f32[264,512]{1,0:T(8,128)S(1)} %get-tuple-element.37.stat), channel_id=1, source_target_pairs={{8,0},{24,8},{0,16},{16,24},{9,1},{25,9},{1,17},{17,25},{10,2},{26... | collective-permute-start | bytes 1622024 | tf_op jit(solution)/shard_map/ppermute | solution.py:397
  41.9 10.0 %collective-permute-done.13.refs_0_ = f32[192,512]{1,0:T(8,128)S(1)} collective-permute-done((f32[192,512]{1,0:T(8,128)S(1)}, f32[192,512]{1,0:T(8,128)S(1)}, u32[]{:S(2)}, u32[]{:S(2)}) %collective-permute-start.13) | collective-permute-done | bytes 393248 | tf_op jit(solution)/shard_map/ppermute | solution.py:69
  51.9 6.4 %collective-permute-done.9.refs_2_ = f32[64,512]{1,0:T(8,128)S(1)} collective-permute-done((f32[64,512]{1,0:T(8,128)S(1)}, f32[64,512]{1,0:T(8,128)S(1)}, u32[]{:S(2)}, u32[]{:S(2)}) %collective-permute-start.9) | collective-permute-done | bytes 131104 | tf_op jit(solution)/shard_map/ppermute | solution.py:69
  58.2 1.2 %collective-permute-start.10 = (f32[64,512]{1,0:T(8,128)S(1)}, f32[64,512]{1,0:T(8,128)S(1)}, u32[]{:S(2)}, u32[]{:S(2)}) collective-permute-start(f32[64,512]{1,0:T(8,128)S(1)} %collective-permute-done.9.refs_2_), channel_id=1, source_target_pairs={{0,8},{8,0},{16,24},{24,16},{1,9},{9,1},{17,25},{25,17},{2,10},{10... | collective-permute-start | bytes 393224 | tf_op jit(solution)/shard_map/ppermute | solution.py:69
  59.5 0.8 %collective-permute-start.12 = (f32[16,1,128]{2,1,0:T(1,128)S(1)}, f32[16,1,128]{2,1,0:T(1,128)S(1)}, u32[]{:S(2)}, u32[]{:S(2)}) collective-permute-start(f32[16,1,128]{2,1,0:T(1,128)S(1)} %get-tuple-element.48), channel_id=1, source_target_pairs={{0,16},{8,24},{16,0},{24,8},{1,17},{9,25},{17,1},{25,9},{2,18},{10... | collective-permute-start | bytes 24584 | tf_op jit(solution)/shard_map/ppermute | solution.py:69
  60.3 2.8 %collective-permute-done.12 = f32[16,1,128]{2,1,0:T(1,128)S(1)} collective-permute-done((f32[16,1,128]{2,1,0:T(1,128)S(1)}, f32[16,1,128]{2,1,0:T(1,128)S(1)}, u32[]{:S(2)}, u32[]{:S(2)}) %collective-permute-start.12) | collective-permute-done | bytes 8224 | tf_op jit(solution)/shard_map/ppermute | solution.py:69
  63.7 3.8 %all-to-all-start.1 = ((f32[16,1,128]{2,1,0:T(1,128)}), f32[16,1,128]{2,1,0:T(1,128)S(1)}, u32[]{:S(2)}, u32[]{:S(2)}) async-start(f32[16,1,128]{2,1,0:T(1,128)} %add.19), calls=%async_computation.1 | async-start | bytes 16384 | tf_op jit(solution)/shard_map/all_to_all | solution.py:427
  67.6 1.2 %shard_map.70 = f32[512,512]{1,0:T(8,128)} custom-call(f32[264,512]{1,0:T(8,128)S(1)} %collective-permute-done.15.packed), custom_call_target="tpu_custom_call" | custom-call | bytes 1048576 | tf_op jit(solution)/shard_map/pallas_call | solution.py:428
  68.7 3.8 %all-to-all-done.1.refs_2_ = f32[16,1,128]{2,1,0:T(1,128)S(1)} async-done(((f32[16,1,128]{2,1,0:T(1,128)}), f32[16,1,128]{2,1,0:T(1,128)S(1)}, u32[]{:S(2)}, u32[]{:S(2)}) %all-to-all-start.1) | async-done | bytes 8224 | tf_op jit(solution)/shard_map/all_to_all | solution.py:427
  72.5 1.2 %shard_map.67 = (f32[1024,512]{1,0:T(8,128)}, f32[1,128]{1,0:T(1,128)S(1)}) custom-call(f32[256,512]{1,0:T(8,128)S(1)} %get-tuple-element.47.refs_0_, f32[256,512]{1,0:T(8,128)S(1)} %collective-permute-done.11.refs_1_, f32[16,1,128]{2,1,0:T(1,128)S(1)} %all-to-all-done.1.refs_2_, f32[1,128]{1,0:T(1,128)S(1)} %get-tuple-element.49.refs_3_, ...), custom_call_target="tpu_custom_call" | custom-call | bytes 1048576 | tf_op jit(solution)/shard_map/pallas_call | solution.py:448
  73.8 1.1 %shard_map.68.refs_3_ = f32[1024,512]{1,0:T(8,128)} custom-call(f32[192,512]{1,0:T(8,128)S(1)} %collective-permute-done.13.refs_0_, f32[192,512]{1,0:T(8,128)S(1)} %collective-permute-done.14.refs_1_, f32[64,512]{1,0:T(8,128)S(1)} %collective-permute-done.9.refs_2_, f32[1,128]{1,0:T(1,128)S(1)} %get-tuple-element.51.refs_3_.refs_1_, ...), custom_call_target="tpu_custom_call", output_to_operand_aliasing={{}: (5, {})} | custom-call | bytes 1048576 | tf_op jit(solution)/shard_map/pallas_call | solution.py:436
  74.9 0.8 %shard_map.69 = f32[1024,512]{1,0:T(8,128)} custom-call(f32[64,512]{1,0:T(8,128)S(1)} %collective-permute-done.10.refs_0_, f32[1,128]{1,0:T(1,128)S(1)} %get-tuple-element.51.refs_3_.refs_1_, f32[4,128]{1,0:T(4,128)S(1)} %get-tuple-element.50.refs_4_.refs_2_, f32[1024,512]{1,0:T(8,128)} %shard_map.68.refs_3_), custom_call_target="tpu_custom_call", output_to_operand_aliasing={{}: (3, {})} | custom-call | bytes 1048576 | tf_op jit(solution)/shard_map/pallas_call | solution.py:436
  (31 shorter events, 4.6 us)
Async XLA Ops:
  0.6 7.0 %copy-start.1 = (s32[1,2]{1,0:T(1,128)S(1)}, s32[1,2]{1,0:T(1,128)}, u32[]{:S(2)}) copy-start(s32[1,2]{1,0:T(1,128)} %owners.5) | copy-start | bytes 28
  0.6 7.0 %copy-start = (f32[1,1,512,512]{3,2,1,0:T(8,128)S(1)}, f32[1,1,512,512]{3,2,1,0:T(8,128)}, u32[]{:S(2)}) copy-start(f32[1,1,512,512]{3,2,1,0:T(8,128)} %param.6) | copy-start | bytes 3145732
  2.2 2.6 %collective-permute-start.1 = (f32[1,128,512]{2,1,0:T(8,128)S(1)}, f32[1,128,512]{2,1,0:T(8,128)S(1)}, u32[]{:S(2)}, u32[]{:S(2)}) collective-permute-start(f32[1,128,512]{2,1,0:T(8,128)S(1)} %get-tuple-element.31), channel_id=1, source_target_pairs={{0,8},{8,0},{16,24},{24,16},{1,9},{9,1},{17,25},{25,17},{2,10},{10... | collective-permute-start | bytes 786440 | tf_op jit(solution)/shard_map/ppermute | solution.py:69
  2.8 4.7 %collective-permute-start.3 = (f32[1,128,512]{2,1,0:T(8,128)S(1)}, f32[1,128,512]{2,1,0:T(8,128)S(1)}, u32[]{:S(2)}, u32[]{:S(2)}) collective-permute-start(f32[1,128,512]{2,1,0:T(8,128)S(1)} %get-tuple-element.33), channel_id=1, source_target_pairs={{0,8},{8,0},{16,24},{24,16},{1,9},{9,1},{17,25},{25,17},{2,10},{10... | collective-permute-start | bytes 786440 | tf_op jit(solution)/shard_map/ppermute | solution.py:69
  4.3 15.7 %collective-permute-start = (f32[1,256,512]{2,1,0:T(8,128)S(1)}, f32[1,256,512]{2,1,0:T(8,128)S(1)}, u32[]{:S(2)}, u32[]{:S(2)}) collective-permute-start(f32[1,256,512]{2,1,0:T(8,128)S(1)} %get-tuple-element.29), channel_id=1, source_target_pairs={{0,8},{8,0},{16,24},{24,16},{1,9},{9,1},{17,25},{25,17},{2,10},{10... | collective-permute-start | bytes 1572872 | tf_op jit(solution)/shard_map/ppermute | solution.py:69
  4.9 9.8 %collective-permute-start.2 = (f32[128,512]{1,0:T(8,128)S(1)}, f32[128,512]{1,0:T(8,128)S(1)}, u32[]{:S(2)}, u32[]{:S(2)}) collective-permute-start(f32[128,512]{1,0:T(8,128)S(1)} %add_bitcast_fusion.1), channel_id=1, source_target_pairs={{0,16},{8,24},{16,0},{24,8},{1,17},{9,25},{17,1},{25,9},{2,18},{10... | collective-permute-start | bytes 786440 | tf_op jit(solution)/shard_map/ppermute | solution.py:69
  7.6 12.5 %collective-permute-start.4 = (f32[128,512]{1,0:T(8,128)S(1)}, f32[128,512]{1,0:T(8,128)S(1)}, u32[]{:S(2)}, u32[]{:S(2)}) collective-permute-start(f32[128,512]{1,0:T(8,128)S(1)} %add_bitcast_fusion), channel_id=1, source_target_pairs={{0,16},{8,24},{16,0},{24,8},{1,17},{9,25},{17,1},{25,9},{2,18},{10... | collective-permute-start | bytes 786440 | tf_op jit(solution)/shard_map/ppermute | solution.py:69
  8.3 19.3 %collective-permute-start.6 = (f32[264,512]{1,0:T(8,128)S(1)}, f32[264,512]{1,0:T(8,128)S(1)}, u32[]{:S(2)}, u32[]{:S(2)}) collective-permute-start(f32[264,512]{1,0:T(8,128)S(1)} %get-tuple-element.36), channel_id=1, source_target_pairs={{0,8},{8,24},{16,0},{24,16},{1,9},{9,25},{17,1},{25,17},{2,10},{10... | collective-permute-start | bytes 1622024 | tf_op jit(solution)/shard_map/ppermute | solution.py:382
  20.8 6.8 %collective-permute-start.5 = (f32[264,512]{1,0:T(8,128)S(1)}, f32[264,512]{1,0:T(8,128)S(1)}, u32[]{:S(2)}, u32[]{:S(2)}) collective-permute-start(f32[264,512]{1,0:T(8,128)S(1)} %get-tuple-element.35.half), channel_id=1, source_target_pairs={{0,8},{8,0},{16,24},{24,16},{1,9},{9,1},{17,25},{25,17},{2,10},{10... | collective-permute-start | bytes 1622024 | tf_op jit(solution)/shard_map/ppermute | solution.py:69
  20.8 13.9 %all-to-all-start = ((f32[32,2,128]{2,1,0:T(2,128)}), f32[32,2,128]{2,1,0:T(2,128)S(1)}, u32[]{:S(2)}, u32[]{:S(2)}) async-start(f32[32,2,128]{2,1,0:T(2,128)} %get-tuple-element.42), calls=%async_computation | async-start | bytes 65536 | tf_op jit(solution)/shard_map/all_to_all | solution.py:387
  36.8 2.4 %collective-permute-start.7 = (f32[256,512]{1,0:T(8,128)S(1)}, f32[256,512]{1,0:T(8,128)S(1)}, u32[]{:S(2)}, u32[]{:S(2)}) collective-permute-start(f32[256,512]{1,0:T(8,128)S(1)} %get-tuple-element.44.upper), channel_id=1, source_target_pairs={{0,8},{8,0},{16,24},{24,16},{1,9},{9,1},{17,25},{25,17},{2,10},{10... | collective-permute-start | bytes 1572872 | tf_op jit(solution)/shard_map/ppermute | solution.py:69
  37.0 2.2 %collective-permute-start.8 = (f32[256,256]{1,0:T(8,128)S(1)}, f32[256,256]{1,0:T(8,128)S(1)}, u32[]{:S(2)}, u32[]{:S(2)}) collective-permute-start(f32[256,256]{1,0:T(8,128)S(1)} %get-tuple-element.45.corner), channel_id=1, source_target_pairs={{0,8},{8,0},{16,24},{24,16},{1,9},{9,1},{17,25},{25,17},{2,10},{10... | collective-permute-start | bytes 786440 | tf_op jit(solution)/shard_map/ppermute | solution.py:69
  39.8 12.1 %collective-permute-start.13 = (f32[192,512]{1,0:T(8,128)S(1)}, f32[192,512]{1,0:T(8,128)S(1)}, u32[]{:S(2)}, u32[]{:S(2)}) collective-permute-start(f32[192,512]{1,0:T(8,128)S(1)} %get-tuple-element.52), channel_id=1, source_target_pairs={{0,16},{8,24},{16,0},{24,8},{1,17},{9,25},{17,1},{25,9},{2,18},{10... | collective-permute-start | bytes 1179656 | tf_op jit(solution)/shard_map/ppermute | solution.py:69
  40.5 27.0 %collective-permute-start.15 = (f32[264,512]{1,0:T(8,128)S(1)}, f32[264,512]{1,0:T(8,128)S(1)}, u32[]{:S(2)}, u32[]{:S(2)}) collective-permute-start(f32[264,512]{1,0:T(8,128)S(1)} %get-tuple-element.37.stat), channel_id=1, source_target_pairs={{8,0},{24,8},{0,16},{16,24},{9,1},{25,9},{1,17},{17,25},{10,2},{26... | collective-permute-start | bytes 1622024 | tf_op jit(solution)/shard_map/ppermute | solution.py:397
  41.9 30.6 %collective-permute-start.11 = (f32[256,512]{1,0:T(8,128)S(1)}, f32[256,512]{1,0:T(8,128)S(1)}, u32[]{:S(2)}, u32[]{:S(2)}) collective-permute-start(f32[256,512]{1,0:T(8,128)S(1)} %get-tuple-element.47.refs_0_), channel_id=1, source_target_pairs={{0,8},{8,0},{16,24},{24,16},{1,9},{9,1},{17,25},{25,17},{2,10},{10... | collective-permute-start | bytes 1572872 | tf_op jit(solution)/shard_map/ppermute | solution.py:69
  51.9 21.9 %collective-permute-start.14 = (f32[192,512]{1,0:T(8,128)S(1)}, f32[192,512]{1,0:T(8,128)S(1)}, u32[]{:S(2)}, u32[]{:S(2)}) collective-permute-start(f32[192,512]{1,0:T(8,128)S(1)} %collective-permute-done.13.refs_0_), channel_id=1, source_target_pairs={{0,8},{8,0},{16,24},{24,16},{1,9},{9,1},{17,25},{25,17},{2,10},{10... | collective-permute-start | bytes 1179656 | tf_op jit(solution)/shard_map/ppermute | solution.py:69
  51.9 6.4 %collective-permute-start.9 = (f32[64,512]{1,0:T(8,128)S(1)}, f32[64,512]{1,0:T(8,128)S(1)}, u32[]{:S(2)}, u32[]{:S(2)}) collective-permute-start(f32[64,512]{1,0:T(8,128)S(1)} %get-tuple-element.46), channel_id=1, source_target_pairs={{0,16},{8,24},{16,0},{24,8},{1,17},{9,25},{17,1},{25,9},{2,18},{10... | collective-permute-start | bytes 393224 | tf_op jit(solution)/shard_map/ppermute | solution.py:69
  58.2 16.7 %collective-permute-start.10 = (f32[64,512]{1,0:T(8,128)S(1)}, f32[64,512]{1,0:T(8,128)S(1)}, u32[]{:S(2)}, u32[]{:S(2)}) collective-permute-start(f32[64,512]{1,0:T(8,128)S(1)} %collective-permute-done.9.refs_2_), channel_id=1, source_target_pairs={{0,8},{8,0},{16,24},{24,16},{1,9},{9,1},{17,25},{25,17},{2,10},{10... | collective-permute-start | bytes 393224 | tf_op jit(solution)/shard_map/ppermute | solution.py:69
  59.5 3.7 %collective-permute-start.12 = (f32[16,1,128]{2,1,0:T(1,128)S(1)}, f32[16,1,128]{2,1,0:T(1,128)S(1)}, u32[]{:S(2)}, u32[]{:S(2)}) collective-permute-start(f32[16,1,128]{2,1,0:T(1,128)S(1)} %get-tuple-element.48), channel_id=1, source_target_pairs={{0,16},{8,24},{16,0},{24,8},{1,17},{9,25},{17,1},{25,9},{2,18},{10... | collective-permute-start | bytes 24584 | tf_op jit(solution)/shard_map/ppermute | solution.py:69
  63.7 8.8 %all-to-all-start.1 = ((f32[16,1,128]{2,1,0:T(1,128)}), f32[16,1,128]{2,1,0:T(1,128)S(1)}, u32[]{:S(2)}, u32[]{:S(2)}) async-start(f32[16,1,128]{2,1,0:T(1,128)} %add.19), calls=%async_computation.1 | async-start | bytes 16384 | tf_op jit(solution)/shard_map/all_to_all | solution.py:427

commit v4 on v3

--- a/solution.py
+++ b/solution.py
@@ -233,7 +233,7 @@
     return taken(SMALL_CUBIC, jnp.ones_like(e)), taken(ROOT_FACTOR, outer), taken(ROOT_REST, outer), grad_sq
 
 
-def root(devices, stat, g_in, square, cubed, facts, sums, out, low, totals, g, left, right, sem):
+def root(devices, stat, g_in, square, cubed, facts, sums, out, totals, g, left, right, sem):
     fetch = pltpu.make_async_copy(g_in, g, sem)
     fetch.start()
     small, factor, rest, grad_sq = coefficients(devices, facts, sums)
@@ -252,15 +252,21 @@
         dst[LOW] = polynomial(k, powers, 0).astype(bf16)
         dst[TOP, TOP] = polynomial(k, powers, 1).astype(bf16)
         dst[TOP, LOW] = dst[LOW, TOP].T
-    out[...] = mm(left[LOW], right[...]) + polynomial(rest, powers, 0)
-    low[...] = mm(left[TOP], right[:, TOP]) + polynomial(rest, powers, 1)
+    out[LOW] = mm(left[LOW], right[...]) + polynomial(rest, powers, 0)
+    corner = mm(left[TOP], right[:, TOP]) + polynomial(rest, powers, 1)
+    out[HALF:, LOW] = corner[: HALF // 2]
+    out[HALF:, TOP] = corner[HALF // 2 :]
     totals[...] = jnp.broadcast_to(grad_sq, (1, 128))
     fetch.wait()
 
 
-def half_way(g, upper, corner, out, x):
+def root_corner(packed):
+    return jnp.concatenate([packed[HALF:, LOW], packed[HALF:, TOP]], axis=0)
+
+
+def half_way(g, packed, out, x):
     _, core = chip_core()
-    spread(upper[...], corner[...], x)
+    spread(packed[LOW], root_corner(packed), x)
 
     @pl.when(core == 1)
     def _():
@@ -272,17 +278,17 @@
         out[0], out[1] = split(dot3((g[0], g[1]), (x[0], x[1])))
 
 
-def last_product(middle, upper, corner, mine, most, rest, sums, x):
+def last_product(middle, packed, mine, most, rest, sums, x):
     _, core = chip_core()
 
     @pl.when(core == 1)
     def _():
-        spread(upper[...], corner[...], x)
+        spread(packed[LOW], root_corner(packed), x)
         mine[...] = dot3((middle[0, LOW], middle[1, LOW]), (x[0], x[1]))
 
     @pl.when(core == 0)
     def _():
-        mine[...] = dot3(split(upper[...]), (middle[0], middle[1]))
+        mine[...] = dot3(split(packed[LOW]), (middle[0], middle[1]))
 
     most[...], rest[...] = mine[:MOST], mine[MOST:]
     sums[...] = jnp.broadcast_to(lanes(mine[...] * mine[...])[None], sums.shape)
@@ -395,17 +401,16 @@
         input_output_aliases={0: 3, 1: 2, 2: 1},
     )(half, other, old)
     new_packed = lax.ppermute(out_packed, "rep", [(t, s) for s, t in shuffle])
-    upper, corner, totals, g_split = call(
+    mine_root, totals, g_split = call(
         functools.partial(root, devices),
-        [piece, (HALF, HALF), (1, 128), whole],
+        [(HALF + HALF // 2, BLOCK), (1, 128), whole],
         [VMEM, HBM] + [VMEM] * 4,
         [pltpu.VMEM(square, bf16)] * 2 + [pltpu.SemaphoreType.DMA],
         flops=unit,
     )(out_packed, in_hbm(g_split), square_p, cube_p, facts, sums)
-    other_upper = flip(upper, 1)
-    other_corner = flip(corner, 1)
-    (middle,) = call(half_way, [whole], [VMEM] * 3, [split_square], flops=unit)(g_split, upper, corner)
-    mine, most, rest, prec = call(last_product, [piece, (MOST, BLOCK), (HALF - MOST, BLOCK), (2 * stripes, 1, 128)], [VMEM] * 3, [split_square], flops=unit)(middle, other_upper, other_corner)
+    other_root = flip(mine_root, 1)
+    (middle,) = call(half_way, [whole], [VMEM] * 2, [split_square], flops=unit)(g_split, mine_root)
+    mine, most, rest, prec = call(last_product, [piece, (MOST, BLOCK), (HALF - MOST, BLOCK), (2 * stripes, 1, 128)], [VMEM] * 2, [split_square], flops=unit)(middle, other_root)
 
     bit = 2
     while bit < rep_count:

time: 76 us -> 75.2 us (0.989)
  Pallas kernels: 16 us -> 15.2 us
    ppermute x14 -> x13, starting transfers between devices: 7.15 us -> 6.75 us  [flip(): lax.ppermute(x, 'rep', [(i, i ^ mask) for i in range(lax.axis_size('rep'))])]
    ppermute x14 -> x13, waiting for transfers between devices: 31.4 us -> 31.8 us  [flip(): lax.ppermute(x, 'rep', [(i, i ^ mask) for i in range(lax.axis_size('rep'))])]
  transfers between devices with their start and end apart: 18 -> 17, of which waited for: 8 -> 8; matrix products, arithmetic and copies ran while one was open for 1% -> 1% of each run, Pallas kernels for 14% -> 15%
where the time goes in v4:
time: 75.2 us; the launch traced here: 75 us
  waiting for transfers between devices  39.4 us (52%)
  starting transfers between devices  18.9 us (25%)
  Pallas kernels  15.2 us (20%)
  between operations  0.79 us (1%)
    ppermute x13, waiting for transfers between devices, flip(): lax.ppermute(x, 'rep', [(i, i ^ mask) for i in range(lax.axis_size('rep'))])  31.8 us
    ppermute x13, starting transfers between devices, flip(): lax.ppermute(x, 'rep', [(i, i ^ mask) for i in range(lax.axis_size('rep'))])  6.75 us
    all_to_all x1, starting transfers between devices, per_device(): sums = lax.all_to_all(sums, AXES, 0, 0)  6.74 us
    all_to_all x1, starting transfers between devices, per_device(): prec = lax.all_to_all(prec, AXES, 0, 0, axis_index_groups=groups)  3.83 us
    all_to_all x1, waiting for transfers between devices, per_device(): sums = lax.all_to_all(sums, AXES, 0, 0)  3.81 us
    all_to_all x1, waiting for transfers between devices, per_device(): prec = lax.all_to_all(prec, AXES, 0, 0, axis_index_groups=groups)  3.8 us
    pallas_call x1, Pallas kernels, per_device(): call(update_stat, [(2, 128)] + [(PACKED, BLOCK)] * 3 + [pltpu.HBM((2,) +...  3.35 us
    pallas_call x2, Pallas kernels, terms(): call(functools.partial(grad_terms, plan), [(len(chips), count, BLOCK) for...  3.04 us
  transfers between devices with their start and end apart: 17, of which 8 were waited for; matrix products, arithmetic and copies ran while one was open for 1% of the time, Pallas kernels for 15%

profile of v4, /device:TPU:0, one launch (start us, length us, event | category | flops | bytes accessed | tf_op | source)
XLA Modules:
  0.0 75.0 jit_solution(10728666526346054454)
XLA Ops:
  0.7 1.6 %shard_map.60 = (f32[1,128,512]{2,1,0:T(8,128)S(1)}, f32[1,128,512]{2,1,0:T(8,128)S(1)}, f32[1,128,512]{2,1,0:T(8,128)S(1)}, f32[1,128,512]{2,1,0:T(8,128)S(1)}) custom-call(bf16[256,1024]{1,0:T(8,128)(2,1)} %acts.3, bf16[256,512]{1,0:T(8,128)(2,1)} %grads.3, s32[1,2]{1,0:T(1,128)} %owners.5), custom_call_target="tpu_custom_call" | custom-call | flops 268435456 | bytes 1048576 | tf_op jit(solution)/shard_map/pallas_call | solution.py:353
  2.9 1.5 %shard_map.59 = (f32[1,256,512]{2,1,0:T(8,128)S(1)}, f32[1,256,512]{2,1,0:T(8,128)S(1)}) custom-call(bf16[256,1024]{1,0:T(8,128)(2,1)} %acts.3, bf16[256,512]{1,0:T(8,128)(2,1)} %grads.3, s32[1,2]{1,0:T(1,128)} %owners.5), custom_call_target="tpu_custom_call" | custom-call | flops 134217728 | bytes 1048576 | tf_op jit(solution)/shard_map/pallas_call | solution.py:353
  4.9 2.6 %collective-permute-start.2 = (f32[128,512]{1,0:T(8,128)S(1)}, f32[128,512]{1,0:T(8,128)S(1)}, u32[]{:S(2)}, u32[]{:S(2)}) collective-permute-start(f32[128,512]{1,0:T(8,128)S(1)} %add_bitcast_fusion.1), channel_id=1, source_target_pairs={{0,16},{8,24},{16,0},{24,8},{1,17},{9,25},{17,1},{25,9},{2,18},{10... | collective-permute-start | bytes 786440 | tf_op jit(solution)/shard_map/ppermute | solution.py:69
  8.4 6.2 %collective-permute-done.2.rest_a = f32[128,512]{1,0:T(8,128)S(1)} collective-permute-done((f32[128,512]{1,0:T(8,128)S(1)}, f32[128,512]{1,0:T(8,128)S(1)}, u32[]{:S(2)}, u32[]{:S(2)}) %collective-permute-start.2) | collective-permute-done | bytes 262176 | tf_op jit(solution)/shard_map/ppermute | solution.py:69
  14.7 5.4 %collective-permute-done.4.rest_b = f32[128,512]{1,0:T(8,128)S(1)} collective-permute-done((f32[128,512]{1,0:T(8,128)S(1)}, f32[128,512]{1,0:T(8,128)S(1)}, u32[]{:S(2)}, u32[]{:S(2)}) %collective-permute-start.4) | collective-permute-done | bytes 262176 | tf_op jit(solution)/shard_map/ppermute | solution.py:69
  20.0 0.8 %shard_map.62 = (f32[264,512]{1,0:T(8,128)S(1)}, f32[32,2,128]{2,1,0:T(2,128)}) custom-call(f32[1,256,512]{2,1,0:T(8,128)S(1)} %get-tuple-element.27.keep, f32[1,256,512]{2,1,0:T(8,128)S(1)} %collective-permute-done.got, f32[128,512]{1,0:T(8,128)S(1)} %collective-permute-done.2.rest_a, f32[128,512]{1,0:T(8,128)S(1)} %collective-permute-done.4.rest_b, ...), custom_call_target="tpu_custom_call" | custom-call | bytes 1048576 | tf_op jit(solution)/shard_map/pallas_call | solution.py:389
  20.8 6.7 %all-to-all-start = ((f32[32,2,128]{2,1,0:T(2,128)}), f32[32,2,128]{2,1,0:T(2,128)S(1)}, u32[]{:S(2)}, u32[]{:S(2)}) async-start(f32[32,2,128]{2,1,0:T(2,128)} %get-tuple-element.41), calls=%async_computation | async-start | bytes 65536 | tf_op jit(solution)/shard_map/all_to_all | solution.py:393
  27.6 3.4 %shard_map.63 = (f32[2,128]{1,0:T(2,128)S(1)}, f32[264,512]{1,0:T(8,128)S(1)}, f32[264,512]{1,0:T(8,128)S(1)}, f32[264,512]{1,0:T(8,128)S(1)}, bf16[2,512,512]{2,1,0:T(8,128)(2,1)}) custom-call(f32[264,512]{1,0:T(8,128)S(1)} %get-tuple-element.34.half, ...), custom_call_target="tpu_custom_call", output_to_operand_aliasing={{3}: (0, {}), {2}: (1, {}), {1}: (2, {})} | custom-call | flops 2415919104 | bytes 1048576 | tf_op jit(solution)/shard_map/pallas_call | solution.py:394
  31.0 3.8 %all-to-all-done.sums = f32[32,2,128]{2,1,0:T(2,128)S(1)} async-done(((f32[32,2,128]{2,1,0:T(2,128)}), f32[32,2,128]{2,1,0:T(2,128)S(1)}, u32[]{:S(2)}, u32[]{:S(2)}) %all-to-all-start) | async-done | bytes 32800 | tf_op jit(solution)/shard_map/all_to_all | solution.py:393
  34.8 1.2 %shard_map.64 = (f32[384,512]{1,0:T(8,128)S(1)}, f32[1,128]{1,0:T(1,128)S(1)}, bf16[2,512,512]{2,1,0:T(8,128)(2,1)S(1)}) custom-call(f32[264,512]{1,0:T(8,128)S(1)} %get-tuple-element.36.stat, bf16[2,512,512]{2,1,0:T(8,128)(2,1)} %get-tuple-element.37.g_in, f32[264,512]{1,0:T(8,128)S(1)} %get-tuple-element.38.square, ...), custom_call_target="tpu_custom_call" | custom-call | flops 805306368 | bytes 1048576 | tf_op jit(solution)/shard_map/pallas_call | solution.py:404
  36.2 1.2 %shard_map.65.middle = bf16[2,512,512]{2,1,0:T(8,128)(2,1)S(1)} custom-call(bf16[2,512,512]{2,1,0:T(8,128)(2,1)S(1)} %get-tuple-element.42.g, f32[384,512]{1,0:T(8,128)S(1)} %get-tuple-element.43.packed), custom_call_target="tpu_custom_call" | custom-call | flops 805306368 | bytes 1048576 | tf_op jit(solution)/shard_map/pallas_call | solution.py:412
  37.4 1.0 %collective-permute-done.7.packed = f32[384,512]{1,0:T(8,128)S(1)} collective-permute-done((f32[384,512]{1,0:T(8,128)S(1)}, f32[384,512]{1,0:T(8,128)S(1)}, u32[]{:S(2)}, u32[]{:S(2)}) %collective-permute-start.7) | collective-permute-done | bytes 786464 | tf_op jit(solution)/shard_map/ppermute | solution.py:69
  39.7 1.4 %collective-permute-start.14 = (f32[264,512]{1,0:T(8,128)S(1)}, f32[264,512]{1,0:T(8,128)S(1)}, u32[]{:S(2)}, u32[]{:S(2)}) collective-permute-start(f32[264,512]{1,0:T(8,128)S(1)} %get-tuple-element.36.stat), channel_id=1, source_target_pairs={{8,0},{24,8},{0,16},{16,24},{9,1},{25,9},{1,17},{17,25},{10,2},{26... | collective-permute-start | bytes 1622024 | tf_op jit(solution)/shard_map/ppermute | solution.py:403
  41.1 10.0 %collective-permute-done.12.refs_0_ = f32[192,512]{1,0:T(8,128)S(1)} collective-permute-done((f32[192,512]{1,0:T(8,128)S(1)}, f32[192,512]{1,0:T(8,128)S(1)}, u32[]{:S(2)}, u32[]{:S(2)}) %collective-permute-start.12) | collective-permute-done | bytes 393248 | tf_op jit(solution)/shard_map/ppermute | solution.py:69
  51.1 6.4 %collective-permute-done.8.refs_2_ = f32[64,512]{1,0:T(8,128)S(1)} collective-permute-done((f32[64,512]{1,0:T(8,128)S(1)}, f32[64,512]{1,0:T(8,128)S(1)}, u32[]{:S(2)}, u32[]{:S(2)}) %collective-permute-start.8) | collective-permute-done | bytes 131104 | tf_op jit(solution)/shard_map/ppermute | solution.py:69
  57.5 1.2 %collective-permute-start.9 = (f32[64,512]{1,0:T(8,128)S(1)}, f32[64,512]{1,0:T(8,128)S(1)}, u32[]{:S(2)}, u32[]{:S(2)}) collective-permute-start(f32[64,512]{1,0:T(8,128)S(1)} %collective-permute-done.8.refs_2_), channel_id=1, source_target_pairs={{0,8},{8,0},{16,24},{24,16},{1,9},{9,1},{17,25},{25,17},{2,10},{10... | collective-permute-start | bytes 393224 | tf_op jit(solution)/shard_map/ppermute | solution.py:69
  58.7 0.8 %collective-permute-start.11 = (f32[16,1,128]{2,1,0:T(1,128)S(1)}, f32[16,1,128]{2,1,0:T(1,128)S(1)}, u32[]{:S(2)}, u32[]{:S(2)}) collective-permute-start(f32[16,1,128]{2,1,0:T(1,128)S(1)} %get-tuple-element.46), channel_id=1, source_target_pairs={{0,16},{8,24},{16,0},{24,8},{1,17},{9,25},{17,1},{25,9},{2,18},{10... | collective-permute-start | bytes 24584 | tf_op jit(solution)/shard_map/ppermute | solution.py:69
  59.5 2.8 %collective-permute-done.11 = f32[16,1,128]{2,1,0:T(1,128)S(1)} collective-permute-done((f32[16,1,128]{2,1,0:T(1,128)S(1)}, f32[16,1,128]{2,1,0:T(1,128)S(1)}, u32[]{:S(2)}, u32[]{:S(2)}) %collective-permute-start.11) | collective-permute-done | bytes 8224 | tf_op jit(solution)/shard_map/ppermute | solution.py:69
  63.0 3.8 %all-to-all-start.1 = ((f32[16,1,128]{2,1,0:T(1,128)}), f32[16,1,128]{2,1,0:T(1,128)S(1)}, u32[]{:S(2)}, u32[]{:S(2)}) async-start(f32[16,1,128]{2,1,0:T(1,128)} %add.19), calls=%async_computation.1 | async-start | bytes 16384 | tf_op jit(solution)/shard_map/all_to_all | solution.py:432
  66.8 1.2 %shard_map.70 = f32[512,512]{1,0:T(8,128)} custom-call(f32[264,512]{1,0:T(8,128)S(1)} %collective-permute-done.14.packed), custom_call_target="tpu_custom_call" | custom-call | bytes 1048576 | tf_op jit(solution)/shard_map/pallas_call | solution.py:433
  68.0 3.8 %all-to-all-done.1.refs_2_ = f32[16,1,128]{2,1,0:T(1,128)S(1)} async-done(((f32[16,1,128]{2,1,0:T(1,128)}), f32[16,1,128]{2,1,0:T(1,128)S(1)}, u32[]{:S(2)}, u32[]{:S(2)}) %all-to-all-start.1) | async-done | bytes 8224 | tf_op jit(solution)/shard_map/all_to_all | solution.py:432
  71.8 1.2 %shard_map.67 = (f32[1024,512]{1,0:T(8,128)}, f32[1,128]{1,0:T(1,128)S(1)}) custom-call(f32[256,512]{1,0:T(8,128)S(1)} %get-tuple-element.45.refs_0_, f32[256,512]{1,0:T(8,128)S(1)} %collective-permute-done.10.refs_1_, f32[16,1,128]{2,1,0:T(1,128)S(1)} %all-to-all-done.1.refs_2_, f32[1,128]{1,0:T(1,128)S(1)} %get-tuple-element.47.refs_3_, ...), custom_call_target="tpu_custom_call" | custom-call | bytes 1048576 | tf_op jit(solution)/shard_map/pallas_call | solution.py:453
  73.0 1.1 %shard_map.68.refs_3_ = f32[1024,512]{1,0:T(8,128)} custom-call(f32[192,512]{1,0:T(8,128)S(1)} %collective-permute-done.12.refs_0_, f32[192,512]{1,0:T(8,128)S(1)} %collective-permute-done.13.refs_1_, f32[64,512]{1,0:T(8,128)S(1)} %collective-permute-done.8.refs_2_, f32[1,128]{1,0:T(1,128)S(1)} %get-tuple-element.49.refs_3_.refs_1_, ...), custom_call_target="tpu_custom_call", output_to_operand_aliasing={{}: (5, {})} | custom-call | bytes 1048576 | tf_op jit(solution)/shard_map/pallas_call | solution.py:441
  74.1 0.8 %shard_map.69 = f32[1024,512]{1,0:T(8,128)} custom-call(f32[64,512]{1,0:T(8,128)S(1)} %collective-permute-done.9.refs_0_, f32[1,128]{1,0:T(1,128)S(1)} %get-tuple-element.49.refs_3_.refs_1_, f32[4,128]{1,0:T(4,128)S(1)} %get-tuple-element.48.refs_4_.refs_2_, f32[1024,512]{1,0:T(8,128)} %shard_map.68.refs_3_), custom_call_target="tpu_custom_call", output_to_operand_aliasing={{}: (3, {})} | custom-call | bytes 1048576 | tf_op jit(solution)/shard_map/pallas_call | solution.py:441
  (29 shorter events, 4.3 us)
Async XLA Ops:
  0.6 7.0 %copy-start.1 = (s32[1,2]{1,0:T(1,128)S(1)}, s32[1,2]{1,0:T(1,128)}, u32[]{:S(2)}) copy-start(s32[1,2]{1,0:T(1,128)} %owners.5) | copy-start | bytes 28
  0.6 7.0 %copy-start = (f32[1,1,512,512]{3,2,1,0:T(8,128)S(1)}, f32[1,1,512,512]{3,2,1,0:T(8,128)}, u32[]{:S(2)}) copy-start(f32[1,1,512,512]{3,2,1,0:T(8,128)} %param.6) | copy-start | bytes 3145732
  2.2 2.6 %collective-permute-start.1 = (f32[1,128,512]{2,1,0:T(8,128)S(1)}, f32[1,128,512]{2,1,0:T(8,128)S(1)}, u32[]{:S(2)}, u32[]{:S(2)}) collective-permute-start(f32[1,128,512]{2,1,0:T(8,128)S(1)} %get-tuple-element.30), channel_id=1, source_target_pairs={{0,8},{8,0},{16,24},{24,16},{1,9},{9,1},{17,25},{25,17},{2,10},{10... | collective-permute-start | bytes 786440 | tf_op jit(solution)/shard_map/ppermute | solution.py:69
  2.8 4.7 %collective-permute-start.3 = (f32[1,128,512]{2,1,0:T(8,128)S(1)}, f32[1,128,512]{2,1,0:T(8,128)S(1)}, u32[]{:S(2)}, u32[]{:S(2)}) collective-permute-start(f32[1,128,512]{2,1,0:T(8,128)S(1)} %get-tuple-element.32), channel_id=1, source_target_pairs={{0,8},{8,0},{16,24},{24,16},{1,9},{9,1},{17,25},{25,17},{2,10},{10... | collective-permute-start | bytes 786440 | tf_op jit(solution)/shard_map/ppermute | solution.py:69
  4.3 15.7 %collective-permute-start = (f32[1,256,512]{2,1,0:T(8,128)S(1)}, f32[1,256,512]{2,1,0:T(8,128)S(1)}, u32[]{:S(2)}, u32[]{:S(2)}) collective-permute-start(f32[1,256,512]{2,1,0:T(8,128)S(1)} %get-tuple-element.28), channel_id=1, source_target_pairs={{0,8},{8,0},{16,24},{24,16},{1,9},{9,1},{17,25},{25,17},{2,10},{10... | collective-permute-start | bytes 1572872 | tf_op jit(solution)/shard_map/ppermute | solution.py:69
  4.9 9.8 %collective-permute-start.2 = (f32[128,512]{1,0:T(8,128)S(1)}, f32[128,512]{1,0:T(8,128)S(1)}, u32[]{:S(2)}, u32[]{:S(2)}) collective-permute-start(f32[128,512]{1,0:T(8,128)S(1)} %add_bitcast_fusion.1), channel_id=1, source_target_pairs={{0,16},{8,24},{16,0},{24,8},{1,17},{9,25},{17,1},{25,9},{2,18},{10... | collective-permute-start | bytes 786440 | tf_op jit(solution)/shard_map/ppermute | solution.py:69
  7.6 12.5 %collective-permute-start.4 = (f32[128,512]{1,0:T(8,128)S(1)}, f32[128,512]{1,0:T(8,128)S(1)}, u32[]{:S(2)}, u32[]{:S(2)}) collective-permute-start(f32[128,512]{1,0:T(8,128)S(1)} %add_bitcast_fusion), channel_id=1, source_target_pairs={{0,16},{8,24},{16,0},{24,8},{1,17},{9,25},{17,1},{25,9},{2,18},{10... | collective-permute-start | bytes 786440 | tf_op jit(solution)/shard_map/ppermute | solution.py:69
  8.3 19.3 %collective-permute-start.6 = (f32[264,512]{1,0:T(8,128)S(1)}, f32[264,512]{1,0:T(8,128)S(1)}, u32[]{:S(2)}, u32[]{:S(2)}) collective-permute-start(f32[264,512]{1,0:T(8,128)S(1)} %get-tuple-element.35), channel_id=1, source_target_pairs={{0,8},{8,24},{16,0},{24,16},{1,9},{9,25},{17,1},{25,17},{2,10},{10... | collective-permute-start | bytes 1622024 | tf_op jit(solution)/shard_map/ppermute | solution.py:388
  20.8 6.8 %collective-permute-start.5 = (f32[264,512]{1,0:T(8,128)S(1)}, f32[264,512]{1,0:T(8,128)S(1)}, u32[]{:S(2)}, u32[]{:S(2)}) collective-permute-start(f32[264,512]{1,0:T(8,128)S(1)} %get-tuple-element.34.half), channel_id=1, source_target_pairs={{0,8},{8,0},{16,24},{24,16},{1,9},{9,1},{17,25},{25,17},{2,10},{10... | collective-permute-start | bytes 1622024 | tf_op jit(solution)/shard_map/ppermute | solution.py:69
  20.8 13.9 %all-to-all-start = ((f32[32,2,128]{2,1,0:T(2,128)}), f32[32,2,128]{2,1,0:T(2,128)S(1)}, u32[]{:S(2)}, u32[]{:S(2)}) async-start(f32[32,2,128]{2,1,0:T(2,128)} %get-tuple-element.41), calls=%async_computation | async-start | bytes 65536 | tf_op jit(solution)/shard_map/all_to_all | solution.py:393
  36.0 2.4 %collective-permute-start.7 = (f32[384,512]{1,0:T(8,128)S(1)}, f32[384,512]{1,0:T(8,128)S(1)}, u32[]{:S(2)}, u32[]{:S(2)}) collective-permute-start(f32[384,512]{1,0:T(8,128)S(1)} %get-tuple-element.43.packed), channel_id=1, source_target_pairs={{0,8},{8,0},{16,24},{24,16},{1,9},{9,1},{17,25},{25,17},{2,10},{10... | collective-permute-start | bytes 2359304 | tf_op jit(solution)/shard_map/ppermute | solution.py:69
  39.1 12.1 %collective-permute-start.12 = (f32[192,512]{1,0:T(8,128)S(1)}, f32[192,512]{1,0:T(8,128)S(1)}, u32[]{:S(2)}, u32[]{:S(2)}) collective-permute-start(f32[192,512]{1,0:T(8,128)S(1)} %get-tuple-element.50), channel_id=1, source_target_pairs={{0,16},{8,24},{16,0},{24,8},{1,17},{9,25},{17,1},{25,9},{2,18},{10... | collective-permute-start | bytes 1179656 | tf_op jit(solution)/shard_map/ppermute | solution.py:69
  39.7 27.0 %collective-permute-start.14 = (f32[264,512]{1,0:T(8,128)S(1)}, f32[264,512]{1,0:T(8,128)S(1)}, u32[]{:S(2)}, u32[]{:S(2)}) collective-permute-start(f32[264,512]{1,0:T(8,128)S(1)} %get-tuple-element.36.stat), channel_id=1, source_target_pairs={{8,0},{24,8},{0,16},{16,24},{9,1},{25,9},{1,17},{17,25},{10,2},{26... | collective-permute-start | bytes 1622024 | tf_op jit(solution)/shard_map/ppermute | solution.py:403
  41.1 30.6 %collective-permute-start.10 = (f32[256,512]{1,0:T(8,128)S(1)}, f32[256,512]{1,0:T(8,128)S(1)}, u32[]{:S(2)}, u32[]{:S(2)}) collective-permute-start(f32[256,512]{1,0:T(8,128)S(1)} %get-tuple-element.45.refs_0_), channel_id=1, source_target_pairs={{0,8},{8,0},{16,24},{24,16},{1,9},{9,1},{17,25},{25,17},{2,10},{10... | collective-permute-start | bytes 1572872 | tf_op jit(solution)/shard_map/ppermute | solution.py:69
  51.1 21.9 %collective-permute-start.13 = (f32[192,512]{1,0:T(8,128)S(1)}, f32[192,512]{1,0:T(8,128)S(1)}, u32[]{:S(2)}, u32[]{:S(2)}) collective-permute-start(f32[192,512]{1,0:T(8,128)S(1)} %collective-permute-done.12.refs_0_), channel_id=1, source_target_pairs={{0,8},{8,0},{16,24},{24,16},{1,9},{9,1},{17,25},{25,17},{2,10},{10... | collective-permute-start | bytes 1179656 | tf_op jit(solution)/shard_map/ppermute | solution.py:69
  51.1 6.4 %collective-permute-start.8 = (f32[64,512]{1,0:T(8,128)S(1)}, f32[64,512]{1,0:T(8,128)S(1)}, u32[]{:S(2)}, u32[]{:S(2)}) collective-permute-start(f32[64,512]{1,0:T(8,128)S(1)} %get-tuple-element.44), channel_id=1, source_target_pairs={{0,16},{8,24},{16,0},{24,8},{1,17},{9,25},{17,1},{25,9},{2,18},{10... | collective-permute-start | bytes 393224 | tf_op jit(solution)/shard_map/ppermute | solution.py:69
  57.5 16.7 %collective-permute-start.9 = (f32[64,512]{1,0:T(8,128)S(1)}, f32[64,512]{1,0:T(8,128)S(1)}, u32[]{:S(2)}, u32[]{:S(2)}) collective-permute-start(f32[64,512]{1,0:T(8,128)S(1)} %collective-permute-done.8.refs_2_), channel_id=1, source_target_pairs={{0,8},{8,0},{16,24},{24,16},{1,9},{9,1},{17,25},{25,17},{2,10},{10... | collective-permute-start | bytes 393224 | tf_op jit(solution)/shard_map/ppermute | solution.py:69
  58.7 3.7 %collective-permute-start.11 = (f32[16,1,128]{2,1,0:T(1,128)S(1)}, f32[16,1,128]{2,1,0:T(1,128)S(1)}, u32[]{:S(2)}, u32[]{:S(2)}) collective-permute-start(f32[16,1,128]{2,1,0:T(1,128)S(1)} %get-tuple-element.46), channel_id=1, source_target_pairs={{0,16},{8,24},{16,0},{24,8},{1,17},{9,25},{17,1},{25,9},{2,18},{10... | collective-permute-start | bytes 24584 | tf_op jit(solution)/shard_map/ppermute | solution.py:69
  63.0 8.8 %all-to-all-start.1 = ((f32[16,1,128]{2,1,0:T(1,128)}), f32[16,1,128]{2,1,0:T(1,128)S(1)}, u32[]{:S(2)}, u32[]{:S(2)}) async-start(f32[16,1,128]{2,1,0:T(1,128)} %add.19), calls=%async_computation.1 | async-start | bytes 16384 | tf_op jit(solution)/shard_map/all_to_all | solution.py:432

commit v5 on v4

--- a/solution.py
+++ b/solution.py
@@ -318,7 +318,7 @@
 
 
 def first_row(rows, n):
-    return jnp.max(rows[n : n + 1, :]).astype(jnp.int32)
+    return rows[n, 0].astype(jnp.int32)
 
 
 def place_first(plan, *refs):
@@ -427,8 +427,7 @@
     most = spread_over_chips(most)
     rest = spread_over_chips(rest)
     across = flip(mine, 1)
-    near = [(s + stripes // 4) % stripes for s in range(stripes)]
-    groups = [[(2 * q + c) * stripes + s for s in near for c in range(2)] for q in range(pairs)]
+    groups = [[(2 * q + c) * stripes + s for s in range(stripes) for c in range(2)] for q in range(pairs)]
     prec = lax.all_to_all(prec, AXES, 0, 0, axis_index_groups=groups)
     (new_stat,) = call(unpack_stat, [square], [VMEM])(new_packed)
     slab = (pairs * BLOCK, out_grads.shape[1])

time: 75.2 us -> 76.1 us (1.012)
  waiting for transfers between devices: 39.4 us -> 40.7 us
    all_to_all x1, waiting for transfers between devices: 3.8 us -> 5.14 us  [per_device(): prec = lax.all_to_all(prec, AXES, 0, 0, axis_index_groups=groups)]
  transfers between devices with their start and end apart: 17 -> 17, of which waited for: 8 -> 8; matrix products, arithmetic and copies ran while one was open for 1% -> 1% of each run, Pallas kernels for 15% -> 14%
where the time goes in v5:
time: 76.1 us; the launch traced here: 75.8 us
  waiting for transfers between devices  40.7 us (53%)
  starting transfers between devices  18.5 us (24%)
  Pallas kernels  15.1 us (20%)
  between operations  0.8 us (1%)
    ppermute x13, waiting for transfers between devices, flip(): lax.ppermute(x, 'rep', [(i, i ^ mask) for i in range(lax.axis_size('rep'))])  31.8 us
    ppermute x13, starting transfers between devices, flip(): lax.ppermute(x, 'rep', [(i, i ^ mask) for i in range(lax.axis_size('rep'))])  6.75 us
    all_to_all x1, starting transfers between devices, per_device(): sums = lax.all_to_all(sums, AXES, 0, 0)  6.74 us
    all_to_all x1, waiting for transfers between devices, per_device(): prec = lax.all_to_all(prec, AXES, 0, 0, axis_index_groups=groups)  5.14 us
    all_to_all x1, waiting for transfers between devices, per_device(): sums = lax.all_to_all(sums, AXES, 0, 0)  3.81 us
    all_to_all x1, starting transfers between devices, per_device(): prec = lax.all_to_all(prec, AXES, 0, 0, axis_index_groups=groups)  3.47 us
    pallas_call x1, Pallas kernels, per_device(): call(update_stat, [(2, 128)] + [(PACKED, BLOCK)] * 3 + [pltpu.HBM((2,) +...  3.35 us
    pallas_call x2, Pallas kernels, terms(): call(functools.partial(grad_terms, plan), [(len(chips), count, BLOCK) for...  3.04 us
  transfers between devices with their start and end apart: 17, of which 8 were waited for; matrix products, arithmetic and copies ran while one was open for 1% of the time, Pallas kernels for 14%

profile of v5, /device:TPU:0, one launch (start us, length us, event | category | flops | bytes accessed | tf_op | source)
XLA Modules:
  0.0 75.8 jit_solution(13879611044259728299)
XLA Ops:
  0.7 1.6 %shard_map.60 = (f32[1,128,512]{2,1,0:T(8,128)S(1)}, f32[1,128,512]{2,1,0:T(8,128)S(1)}, f32[1,128,512]{2,1,0:T(8,128)S(1)}, f32[1,128,512]{2,1,0:T(8,128)S(1)}) custom-call(bf16[256,1024]{1,0:T(8,128)(2,1)} %acts.3, bf16[256,512]{1,0:T(8,128)(2,1)} %grads.3, s32[1,2]{1,0:T(1,128)} %owners.5), custom_call_target="tpu_custom_call" | custom-call | flops 268435456 | bytes 1048576 | tf_op jit(solution)/shard_map/pallas_call | solution.py:353
  2.9 1.5 %shard_map.59 = (f32[1,256,512]{2,1,0:T(8,128)S(1)}, f32[1,256,512]{2,1,0:T(8,128)S(1)}) custom-call(bf16[256,1024]{1,0:T(8,128)(2,1)} %acts.3, bf16[256,512]{1,0:T(8,128)(2,1)} %grads.3, s32[1,2]{1,0:T(1,128)} %owners.5), custom_call_target="tpu_custom_call" | custom-call | flops 134217728 | bytes 1048576 | tf_op jit(solution)/shard_map/pallas_call | solution.py:353
  4.9 2.6 %collective-permute-start.2 = (f32[128,512]{1,0:T(8,128)S(1)}, f32[128,512]{1,0:T(8,128)S(1)}, u32[]{:S(2)}, u32[]{:S(2)}) collective-permute-start(f32[128,512]{1,0:T(8,128)S(1)} %add_bitcast_fusion.1), channel_id=1, source_target_pairs={{0,16},{8,24},{16,0},{24,8},{1,17},{9,25},{17,1},{25,9},{2,18},{10... | collective-permute-start | bytes 786440 | tf_op jit(solution)/shard_map/ppermute | solution.py:69
  8.4 6.2 %collective-permute-done.2.rest_a = f32[128,512]{1,0:T(8,128)S(1)} collective-permute-done((f32[128,512]{1,0:T(8,128)S(1)}, f32[128,512]{1,0:T(8,128)S(1)}, u32[]{:S(2)}, u32[]{:S(2)}) %collective-permute-start.2) | collective-permute-done | bytes 262176 | tf_op jit(solution)/shard_map/ppermute | solution.py:69
  14.7 5.4 %collective-permute-done.4.rest_b = f32[128,512]{1,0:T(8,128)S(1)} collective-permute-done((f32[128,512]{1,0:T(8,128)S(1)}, f32[128,512]{1,0:T(8,128)S(1)}, u32[]{:S(2)}, u32[]{:S(2)}) %collective-permute-start.4) | collective-permute-done | bytes 262176 | tf_op jit(solution)/shard_map/ppermute | solution.py:69
  20.0 0.8 %shard_map.62 = (f32[264,512]{1,0:T(8,128)S(1)}, f32[32,2,128]{2,1,0:T(2,128)}) custom-call(f32[1,256,512]{2,1,0:T(8,128)S(1)} %get-tuple-element.27.keep, f32[1,256,512]{2,1,0:T(8,128)S(1)} %collective-permute-done.got, f32[128,512]{1,0:T(8,128)S(1)} %collective-permute-done.2.rest_a, f32[128,512]{1,0:T(8,128)S(1)} %collective-permute-done.4.rest_b, ...), custom_call_target="tpu_custom_call" | custom-call | bytes 1048576 | tf_op jit(solution)/shard_map/pallas_call | solution.py:389
  20.8 6.7 %all-to-all-start = ((f32[32,2,128]{2,1,0:T(2,128)}), f32[32,2,128]{2,1,0:T(2,128)S(1)}, u32[]{:S(2)}, u32[]{:S(2)}) async-start(f32[32,2,128]{2,1,0:T(2,128)} %get-tuple-element.41), calls=%async_computation | async-start | bytes 65536 | tf_op jit(solution)/shard_map/all_to_all | solution.py:393
  27.6 3.4 %shard_map.63 = (f32[2,128]{1,0:T(2,128)S(1)}, f32[264,512]{1,0:T(8,128)S(1)}, f32[264,512]{1,0:T(8,128)S(1)}, f32[264,512]{1,0:T(8,128)S(1)}, bf16[2,512,512]{2,1,0:T(8,128)(2,1)}) custom-call(f32[264,512]{1,0:T(8,128)S(1)} %get-tuple-element.34.half, ...), custom_call_target="tpu_custom_call", output_to_operand_aliasing={{3}: (0, {}), {2}: (1, {}), {1}: (2, {})} | custom-call | flops 2415919104 | bytes 1048576 | tf_op jit(solution)/shard_map/pallas_call | solution.py:394
  31.0 3.8 %all-to-all-done.sums = f32[32,2,128]{2,1,0:T(2,128)S(1)} async-done(((f32[32,2,128]{2,1,0:T(2,128)}), f32[32,2,128]{2,1,0:T(2,128)S(1)}, u32[]{:S(2)}, u32[]{:S(2)}) %all-to-all-start) | async-done | bytes 32800 | tf_op jit(solution)/shard_map/all_to_all | solution.py:393
  34.8 1.2 %shard_map.64 = (f32[384,512]{1,0:T(8,128)S(1)}, f32[1,128]{1,0:T(1,128)S(1)}, bf16[2,512,512]{2,1,0:T(8,128)(2,1)S(1)}) custom-call(f32[264,512]{1,0:T(8,128)S(1)} %get-tuple-element.36.stat, bf16[2,512,512]{2,1,0:T(8,128)(2,1)} %get-tuple-element.37.g_in, f32[264,512]{1,0:T(8,128)S(1)} %get-tuple-element.38.square, ...), custom_call_target="tpu_custom_call" | custom-call | flops 805306368 | bytes 1048576 | tf_op jit(solution)/shard_map/pallas_call | solution.py:404
  36.2 1.2 %shard_map.65.middle = bf16[2,512,512]{2,1,0:T(8,128)(2,1)S(1)} custom-call(bf16[2,512,512]{2,1,0:T(8,128)(2,1)S(1)} %get-tuple-element.42.g, f32[384,512]{1,0:T(8,128)S(1)} %get-tuple-element.43.packed), custom_call_target="tpu_custom_call" | custom-call | flops 805306368 | bytes 1048576 | tf_op jit(solution)/shard_map/pallas_call | solution.py:412
  37.4 1.0 %collective-permute-done.7.packed = f32[384,512]{1,0:T(8,128)S(1)} collective-permute-done((f32[384,512]{1,0:T(8,128)S(1)}, f32[384,512]{1,0:T(8,128)S(1)}, u32[]{:S(2)}, u32[]{:S(2)}) %collective-permute-start.7) | collective-permute-done | bytes 786464 | tf_op jit(solution)/shard_map/ppermute | solution.py:69
  39.7 1.4 %collective-permute-start.14 = (f32[264,512]{1,0:T(8,128)S(1)}, f32[264,512]{1,0:T(8,128)S(1)}, u32[]{:S(2)}, u32[]{:S(2)}) collective-permute-start(f32[264,512]{1,0:T(8,128)S(1)} %get-tuple-element.36.stat), channel_id=1, source_target_pairs={{8,0},{24,8},{0,16},{16,24},{9,1},{25,9},{1,17},{17,25},{10,2},{26... | collective-permute-start | bytes 1622024 | tf_op jit(solution)/shard_map/ppermute | solution.py:403
  41.1 10.0 %collective-permute-done.12.refs_0_ = f32[192,512]{1,0:T(8,128)S(1)} collective-permute-done((f32[192,512]{1,0:T(8,128)S(1)}, f32[192,512]{1,0:T(8,128)S(1)}, u32[]{:S(2)}, u32[]{:S(2)}) %collective-permute-start.12) | collective-permute-done | bytes 393248 | tf_op jit(solution)/shard_map/ppermute | solution.py:69
  51.1 6.4 %collective-permute-done.8.refs_2_ = f32[64,512]{1,0:T(8,128)S(1)} collective-permute-done((f32[64,512]{1,0:T(8,128)S(1)}, f32[64,512]{1,0:T(8,128)S(1)}, u32[]{:S(2)}, u32[]{:S(2)}) %collective-permute-start.8) | collective-permute-done | bytes 131104 | tf_op jit(solution)/shard_map/ppermute | solution.py:69
  57.5 1.2 %collective-permute-start.9 = (f32[64,512]{1,0:T(8,128)S(1)}, f32[64,512]{1,0:T(8,128)S(1)}, u32[]{:S(2)}, u32[]{:S(2)}) collective-permute-start(f32[64,512]{1,0:T(8,128)S(1)} %collective-permute-done.8.refs_2_), channel_id=1, source_target_pairs={{0,8},{8,0},{16,24},{24,16},{1,9},{9,1},{17,25},{25,17},{2,10},{10... | collective-permute-start | bytes 393224 | tf_op jit(solution)/shard_map/ppermute | solution.py:69
  58.7 0.8 %collective-permute-start.11 = (f32[16,1,128]{2,1,0:T(1,128)S(1)}, f32[16,1,128]{2,1,0:T(1,128)S(1)}, u32[]{:S(2)}, u32[]{:S(2)}) collective-permute-start(f32[16,1,128]{2,1,0:T(1,128)S(1)} %get-tuple-element.46), channel_id=1, source_target_pairs={{0,16},{8,24},{16,0},{24,8},{1,17},{9,25},{17,1},{25,9},{2,18},{10... | collective-permute-start | bytes 24584 | tf_op jit(solution)/shard_map/ppermute | solution.py:69
  59.5 2.8 %collective-permute-done.11 = f32[16,1,128]{2,1,0:T(1,128)S(1)} collective-permute-done((f32[16,1,128]{2,1,0:T(1,128)S(1)}, f32[16,1,128]{2,1,0:T(1,128)S(1)}, u32[]{:S(2)}, u32[]{:S(2)}) %collective-permute-start.11) | collective-permute-done | bytes 8224 | tf_op jit(solution)/shard_map/ppermute | solution.py:69
  63.0 3.5 %all-to-all-start.1 = ((f32[16,1,128]{2,1,0:T(1,128)}), f32[16,1,128]{2,1,0:T(1,128)S(1)}, u32[]{:S(2)}, u32[]{:S(2)}) async-start(f32[16,1,128]{2,1,0:T(1,128)} %add.19), calls=%async_computation.1 | async-start | bytes 16384 | tf_op jit(solution)/shard_map/all_to_all | solution.py:431
  66.4 1.2 %shard_map.70 = f32[512,512]{1,0:T(8,128)} custom-call(f32[264,512]{1,0:T(8,128)S(1)} %collective-permute-done.14.packed), custom_call_target="tpu_custom_call" | custom-call | bytes 1048576 | tf_op jit(solution)/shard_map/pallas_call | solution.py:432
  67.6 5.1 %all-to-all-done.1.refs_2_ = f32[16,1,128]{2,1,0:T(1,128)S(1)} async-done(((f32[16,1,128]{2,1,0:T(1,128)}), f32[16,1,128]{2,1,0:T(1,128)S(1)}, u32[]{:S(2)}, u32[]{:S(2)}) %all-to-all-start.1) | async-done | bytes 8224 | tf_op jit(solution)/shard_map/all_to_all | solution.py:431
  72.8 1.2 %shard_map.67 = (f32[1024,512]{1,0:T(8,128)}, f32[1,128]{1,0:T(1,128)S(1)}) custom-call(f32[256,512]{1,0:T(8,128)S(1)} %get-tuple-element.45.refs_0_, f32[256,512]{1,0:T(8,128)S(1)} %collective-permute-done.10.refs_1_, f32[16,1,128]{2,1,0:T(1,128)S(1)} %all-to-all-done.1.refs_2_, f32[1,128]{1,0:T(1,128)S(1)} %get-tuple-element.47.refs_3_, ...), custom_call_target="tpu_custom_call" | custom-call | bytes 1048576 | tf_op jit(solution)/shard_map/pallas_call | solution.py:452
  74.0 1.1 %shard_map.68.refs_3_ = f32[1024,512]{1,0:T(8,128)} custom-call(f32[192,512]{1,0:T(8,128)S(1)} %collective-permute-done.12.refs_0_, f32[192,512]{1,0:T(8,128)S(1)} %collective-permute-done.13.refs_1_, f32[64,512]{1,0:T(8,128)S(1)} %collective-permute-done.8.refs_2_, f32[1,128]{1,0:T(1,128)S(1)} %get-tuple-element.49.refs_3_.refs_1_, ...), custom_call_target="tpu_custom_call", output_to_operand_aliasing={{}: (5, {})} | custom-call | bytes 1048576 | tf_op jit(solution)/shard_map/pallas_call | solution.py:440
  75.1 0.7 shard_map.69
  (29 shorter events, 4.3 us)
Async XLA Ops:
  0.6 7.0 %copy-start.1 = (s32[1,2]{1,0:T(1,128)S(1)}, s32[1,2]{1,0:T(1,128)}, u32[]{:S(2)}) copy-start(s32[1,2]{1,0:T(1,128)} %owners.5) | copy-start | bytes 28
  0.6 7.0 %copy-start = (f32[1,1,512,512]{3,2,1,0:T(8,128)S(1)}, f32[1,1,512,512]{3,2,1,0:T(8,128)}, u32[]{:S(2)}) copy-start(f32[1,1,512,512]{3,2,1,0:T(8,128)} %param.6) | copy-start | bytes 3145732
  2.2 2.6 %collective-permute-start.1 = (f32[1,128,512]{2,1,0:T(8,128)S(1)}, f32[1,128,512]{2,1,0:T(8,128)S(1)}, u32[]{:S(2)}, u32[]{:S(2)}) collective-permute-start(f32[1,128,512]{2,1,0:T(8,128)S(1)} %get-tuple-element.30), channel_id=1, source_target_pairs={{0,8},{8,0},{16,24},{24,16},{1,9},{9,1},{17,25},{25,17},{2,10},{10... | collective-permute-start | bytes 786440 | tf_op jit(solution)/shard_map/ppermute | solution.py:69
  2.8 4.7 %collective-permute-start.3 = (f32[1,128,512]{2,1,0:T(8,128)S(1)}, f32[1,128,512]{2,1,0:T(8,128)S(1)}, u32[]{:S(2)}, u32[]{:S(2)}) collective-permute-start(f32[1,128,512]{2,1,0:T(8,128)S(1)} %get-tuple-element.32), channel_id=1, source_target_pairs={{0,8},{8,0},{16,24},{24,16},{1,9},{9,1},{17,25},{25,17},{2,10},{10... | collective-permute-start | bytes 786440 | tf_op jit(solution)/shard_map/ppermute | solution.py:69
  4.3 15.7 %collective-permute-start = (f32[1,256,512]{2,1,0:T(8,128)S(1)}, f32[1,256,512]{2,1,0:T(8,128)S(1)}, u32[]{:S(2)}, u32[]{:S(2)}) collective-permute-start(f32[1,256,512]{2,1,0:T(8,128)S(1)} %get-tuple-element.28), channel_id=1, source_target_pairs={{0,8},{8,0},{16,24},{24,16},{1,9},{9,1},{17,25},{25,17},{2,10},{10... | collective-permute-start | bytes 1572872 | tf_op jit(solution)/shard_map/ppermute | solution.py:69
  4.9 9.8 %collective-permute-start.2 = (f32[128,512]{1,0:T(8,128)S(1)}, f32[128,512]{1,0:T(8,128)S(1)}, u32[]{:S(2)}, u32[]{:S(2)}) collective-permute-start(f32[128,512]{1,0:T(8,128)S(1)} %add_bitcast_fusion.1), channel_id=1, source_target_pairs={{0,16},{8,24},{16,0},{24,8},{1,17},{9,25},{17,1},{25,9},{2,18},{10... | collective-permute-start | bytes 786440 | tf_op jit(solution)/shard_map/ppermute | solution.py:69
  7.6 12.5 %collective-permute-start.4 = (f32[128,512]{1,0:T(8,128)S(1)}, f32[128,512]{1,0:T(8,128)S(1)}, u32[]{:S(2)}, u32[]{:S(2)}) collective-permute-start(f32[128,512]{1,0:T(8,128)S(1)} %add_bitcast_fusion), channel_id=1, source_target_pairs={{0,16},{8,24},{16,0},{24,8},{1,17},{9,25},{17,1},{25,9},{2,18},{10... | collective-permute-start | bytes 786440 | tf_op jit(solution)/shard_map/ppermute | solution.py:69
  8.3 19.3 %collective-permute-start.6 = (f32[264,512]{1,0:T(8,128)S(1)}, f32[264,512]{1,0:T(8,128)S(1)}, u32[]{:S(2)}, u32[]{:S(2)}) collective-permute-start(f32[264,512]{1,0:T(8,128)S(1)} %get-tuple-element.35), channel_id=1, source_target_pairs={{0,8},{8,24},{16,0},{24,16},{1,9},{9,25},{17,1},{25,17},{2,10},{10... | collective-permute-start | bytes 1622024 | tf_op jit(solution)/shard_map/ppermute | solution.py:388
  20.8 6.8 %collective-permute-start.5 = (f32[264,512]{1,0:T(8,128)S(1)}, f32[264,512]{1,0:T(8,128)S(1)}, u32[]{:S(2)}, u32[]{:S(2)}) collective-permute-start(f32[264,512]{1,0:T(8,128)S(1)} %get-tuple-element.34.half), channel_id=1, source_target_pairs={{0,8},{8,0},{16,24},{24,16},{1,9},{9,1},{17,25},{25,17},{2,10},{10... | collective-permute-start | bytes 1622024 | tf_op jit(solution)/shard_map/ppermute | solution.py:69
  20.8 13.9 %all-to-all-start = ((f32[32,2,128]{2,1,0:T(2,128)}), f32[32,2,128]{2,1,0:T(2,128)S(1)}, u32[]{:S(2)}, u32[]{:S(2)}) async-start(f32[32,2,128]{2,1,0:T(2,128)} %get-tuple-element.41), calls=%async_computation | async-start | bytes 65536 | tf_op jit(solution)/shard_map/all_to_all | solution.py:393
  36.0 2.4 %collective-permute-start.7 = (f32[384,512]{1,0:T(8,128)S(1)}, f32[384,512]{1,0:T(8,128)S(1)}, u32[]{:S(2)}, u32[]{:S(2)}) collective-permute-start(f32[384,512]{1,0:T(8,128)S(1)} %get-tuple-element.43.packed), channel_id=1, source_target_pairs={{0,8},{8,0},{16,24},{24,16},{1,9},{9,1},{17,25},{25,17},{2,10},{10... | collective-permute-start | bytes 2359304 | tf_op jit(solution)/shard_map/ppermute | solution.py:69
  39.1 12.1 %collective-permute-start.12 = (f32[192,512]{1,0:T(8,128)S(1)}, f32[192,512]{1,0:T(8,128)S(1)}, u32[]{:S(2)}, u32[]{:S(2)}) collective-permute-start(f32[192,512]{1,0:T(8,128)S(1)} %get-tuple-element.50), channel_id=1, source_target_pairs={{0,16},{8,24},{16,0},{24,8},{1,17},{9,25},{17,1},{25,9},{2,18},{10... | collective-permute-start | bytes 1179656 | tf_op jit(solution)/shard_map/ppermute | solution.py:69
  39.7 26.7 %collective-permute-start.14 = (f32[264,512]{1,0:T(8,128)S(1)}, f32[264,512]{1,0:T(8,128)S(1)}, u32[]{:S(2)}, u32[]{:S(2)}) collective-permute-start(f32[264,512]{1,0:T(8,128)S(1)} %get-tuple-element.36.stat), channel_id=1, source_target_pairs={{8,0},{24,8},{0,16},{16,24},{9,1},{25,9},{1,17},{17,25},{10,2},{26... | collective-permute-start | bytes 1622024 | tf_op jit(solution)/shard_map/ppermute | solution.py:403
  41.1 31.6 %collective-permute-start.10 = (f32[256,512]{1,0:T(8,128)S(1)}, f32[256,512]{1,0:T(8,128)S(1)}, u32[]{:S(2)}, u32[]{:S(2)}) collective-permute-start(f32[256,512]{1,0:T(8,128)S(1)} %get-tuple-element.45.refs_0_), channel_id=1, source_target_pairs={{0,8},{8,0},{16,24},{24,16},{1,9},{9,1},{17,25},{25,17},{2,10},{10... | collective-permute-start | bytes 1572872 | tf_op jit(solution)/shard_map/ppermute | solution.py:69
  51.1 22.9 %collective-permute-start.13 = (f32[192,512]{1,0:T(8,128)S(1)}, f32[192,512]{1,0:T(8,128)S(1)}, u32[]{:S(2)}, u32[]{:S(2)}) collective-permute-start(f32[192,512]{1,0:T(8,128)S(1)} %collective-permute-done.12.refs_0_), channel_id=1, source_target_pairs={{0,8},{8,0},{16,24},{24,16},{1,9},{9,1},{17,25},{25,17},{2,10},{10... | collective-permute-start | bytes 1179656 | tf_op jit(solution)/shard_map/ppermute | solution.py:69
  51.1 6.4 %collective-permute-start.8 = (f32[64,512]{1,0:T(8,128)S(1)}, f32[64,512]{1,0:T(8,128)S(1)}, u32[]{:S(2)}, u32[]{:S(2)}) collective-permute-start(f32[64,512]{1,0:T(8,128)S(1)} %get-tuple-element.44), channel_id=1, source_target_pairs={{0,16},{8,24},{16,0},{24,8},{1,17},{9,25},{17,1},{25,9},{2,18},{10... | collective-permute-start | bytes 393224 | tf_op jit(solution)/shard_map/ppermute | solution.py:69
  57.5 17.6 %collective-permute-start.9 = (f32[64,512]{1,0:T(8,128)S(1)}, f32[64,512]{1,0:T(8,128)S(1)}, u32[]{:S(2)}, u32[]{:S(2)}) collective-permute-start(f32[64,512]{1,0:T(8,128)S(1)} %collective-permute-done.8.refs_2_), channel_id=1, source_target_pairs={{0,8},{8,0},{16,24},{24,16},{1,9},{9,1},{17,25},{25,17},{2,10},{10... | collective-permute-start | bytes 393224 | tf_op jit(solution)/shard_map/ppermute | solution.py:69
  58.7 3.7 %collective-permute-start.11 = (f32[16,1,128]{2,1,0:T(1,128)S(1)}, f32[16,1,128]{2,1,0:T(1,128)S(1)}, u32[]{:S(2)}, u32[]{:S(2)}) collective-permute-start(f32[16,1,128]{2,1,0:T(1,128)S(1)} %get-tuple-element.46), channel_id=1, source_target_pairs={{0,16},{8,24},{16,0},{24,8},{1,17},{9,25},{17,1},{25,9},{2,18},{10... | collective-permute-start | bytes 24584 | tf_op jit(solution)/shard_map/ppermute | solution.py:69
  63.0 9.8 %all-to-all-start.1 = ((f32[16,1,128]{2,1,0:T(1,128)}), f32[16,1,128]{2,1,0:T(1,128)S(1)}, u32[]{:S(2)}, u32[]{:S(2)}) async-start(f32[16,1,128]{2,1,0:T(1,128)} %add.19), calls=%async_computation.1 | async-start | bytes 16384 | tf_op jit(solution)/shard_map/all_to_all | solution.py:431

commit v6 on v4

--- a/solution.py
+++ b/solution.py
@@ -318,7 +318,7 @@
 
 
 def first_row(rows, n):
-    return jnp.max(rows[n : n + 1, :]).astype(jnp.int32)
+    return rows[n, 0].astype(jnp.int32)
 
 
 def place_first(plan, *refs):
@@ -449,14 +449,14 @@
         return placed
 
     far = range(1, pairs)
-    plan, found = [(0, 0), (pairs, 0)], (mine, across)
+    plan, found = [(0, 0)], (mine,)
     placed, scale = call(
-        functools.partial(place_first, plan), [slab, (1, 128)], [VMEM] * 5, landing(found), out_specs=[HBM, VMEM]
+        functools.partial(place_first, plan), [slab, (1, 128)], [VMEM] * 4, landing(found), out_specs=[HBM, VMEM]
     )(*found, prec, totals, rows)
     most_across = [flip(x, 1) for x in most]
     rest_across = [flip(x, 1) for x in rest]
-    plan = [(j, 0) for j in far] + [(pairs + j, 0) for j in far] + [(j, MOST) for j in far]
-    placed = place(placed, plan, *most, *most_across, *rest)
+    plan = [(pairs, 0)] + [(j, 0) for j in far] + [(pairs + j, 0) for j in far] + [(j, MOST) for j in far]
+    placed = place(placed, plan, across, *most, *most_across, *rest)
     placed = place(placed, [(pairs + j, MOST) for j in far], *rest_across)
     return placed, new_stat[None, None]
 

time: 75.2 us -> 75.1 us (level)
  transfers between devices with their start and end apart: 17 -> 17, of which waited for: 8 -> 8; matrix products, arithmetic and copies ran while one was open for 1% -> 1% of each run, Pallas kernels for 15% -> 14%
where the time goes in v6:
time: 75.1 us; the launch traced here: 74.8 us
  waiting for transfers between devices  39.4 us (52%)
  starting transfers between devices  18.9 us (25%)
  Pallas kernels  15.1 us (20%)
  between operations  0.79 us (1%)
    ppermute x13, waiting for transfers between devices, flip(): lax.ppermute(x, 'rep', [(i, i ^ mask) for i in range(lax.axis_size('rep'))])  31.8 us
    ppermute x13, starting transfers between devices, flip(): lax.ppermute(x, 'rep', [(i, i ^ mask) for i in range(lax.axis_size('rep'))])  6.75 us
    all_to_all x1, starting transfers between devices, per_device(): sums = lax.all_to_all(sums, AXES, 0, 0)  6.74 us
    all_to_all x1, starting transfers between devices, per_device(): prec = lax.all_to_all(prec, AXES, 0, 0, axis_index_groups=groups)  3.83 us
    all_to_all x1, waiting for transfers between devices, per_device(): sums = lax.all_to_all(sums, AXES, 0, 0)  3.81 us
    all_to_all x1, waiting for transfers between devices, per_device(): prec = lax.all_to_all(prec, AXES, 0, 0, axis_index_groups=groups)  3.8 us
    pallas_call x1, Pallas kernels, per_device(): call(update_stat, [(2, 128)] + [(PACKED, BLOCK)] * 3 + [pltpu.HBM((2,) +...  3.35 us
    pallas_call x2, Pallas kernels, terms(): call(functools.partial(grad_terms, plan), [(len(chips), count, BLOCK) for...  3.04 us
  transfers between devices with their start and end apart: 17, of which 8 were waited for; matrix products, arithmetic and copies ran while one was open for 1% of the time, Pallas kernels for 14%

profile of v6, /device:TPU:0, one launch (start us, length us, event | category | flops | bytes accessed | tf_op | source)
XLA Modules:
  0.0 74.8 jit_solution(6352726697288501050)
XLA Ops:
  0.7 1.6 %shard_map.60 = (f32[1,128,512]{2,1,0:T(8,128)S(1)}, f32[1,128,512]{2,1,0:T(8,128)S(1)}, f32[1,128,512]{2,1,0:T(8,128)S(1)}, f32[1,128,512]{2,1,0:T(8,128)S(1)}) custom-call(bf16[256,1024]{1,0:T(8,128)(2,1)} %acts.3, bf16[256,512]{1,0:T(8,128)(2,1)} %grads.3, s32[1,2]{1,0:T(1,128)} %owners.5), custom_call_target="tpu_custom_call" | custom-call | flops 268435456 | bytes 1048576 | tf_op jit(solution)/shard_map/pallas_call | solution.py:353
  2.9 1.5 %shard_map.59 = (f32[1,256,512]{2,1,0:T(8,128)S(1)}, f32[1,256,512]{2,1,0:T(8,128)S(1)}) custom-call(bf16[256,1024]{1,0:T(8,128)(2,1)} %acts.3, bf16[256,512]{1,0:T(8,128)(2,1)} %grads.3, s32[1,2]{1,0:T(1,128)} %owners.5), custom_call_target="tpu_custom_call" | custom-call | flops 134217728 | bytes 1048576 | tf_op jit(solution)/shard_map/pallas_call | solution.py:353
  4.9 2.6 %collective-permute-start.2 = (f32[128,512]{1,0:T(8,128)S(1)}, f32[128,512]{1,0:T(8,128)S(1)}, u32[]{:S(2)}, u32[]{:S(2)}) collective-permute-start(f32[128,512]{1,0:T(8,128)S(1)} %add_bitcast_fusion.1), channel_id=1, source_target_pairs={{0,16},{8,24},{16,0},{24,8},{1,17},{9,25},{17,1},{25,9},{2,18},{10... | collective-permute-start | bytes 786440 | tf_op jit(solution)/shard_map/ppermute | solution.py:69
  8.4 6.2 %collective-permute-done.2.rest_a = f32[128,512]{1,0:T(8,128)S(1)} collective-permute-done((f32[128,512]{1,0:T(8,128)S(1)}, f32[128,512]{1,0:T(8,128)S(1)}, u32[]{:S(2)}, u32[]{:S(2)}) %collective-permute-start.2) | collective-permute-done | bytes 262176 | tf_op jit(solution)/shard_map/ppermute | solution.py:69
  14.7 5.4 %collective-permute-done.4.rest_b = f32[128,512]{1,0:T(8,128)S(1)} collective-permute-done((f32[128,512]{1,0:T(8,128)S(1)}, f32[128,512]{1,0:T(8,128)S(1)}, u32[]{:S(2)}, u32[]{:S(2)}) %collective-permute-start.4) | collective-permute-done | bytes 262176 | tf_op jit(solution)/shard_map/ppermute | solution.py:69
  20.0 0.8 %shard_map.62 = (f32[264,512]{1,0:T(8,128)S(1)}, f32[32,2,128]{2,1,0:T(2,128)}) custom-call(f32[1,256,512]{2,1,0:T(8,128)S(1)} %get-tuple-element.27.keep, f32[1,256,512]{2,1,0:T(8,128)S(1)} %collective-permute-done.got, f32[128,512]{1,0:T(8,128)S(1)} %collective-permute-done.2.rest_a, f32[128,512]{1,0:T(8,128)S(1)} %collective-permute-done.4.rest_b, ...), custom_call_target="tpu_custom_call" | custom-call | bytes 1048576 | tf_op jit(solution)/shard_map/pallas_call | solution.py:389
  20.8 6.7 %all-to-all-start = ((f32[32,2,128]{2,1,0:T(2,128)}), f32[32,2,128]{2,1,0:T(2,128)S(1)}, u32[]{:S(2)}, u32[]{:S(2)}) async-start(f32[32,2,128]{2,1,0:T(2,128)} %get-tuple-element.41), calls=%async_computation | async-start | bytes 65536 | tf_op jit(solution)/shard_map/all_to_all | solution.py:393
  27.6 3.4 %shard_map.63 = (f32[2,128]{1,0:T(2,128)S(1)}, f32[264,512]{1,0:T(8,128)S(1)}, f32[264,512]{1,0:T(8,128)S(1)}, f32[264,512]{1,0:T(8,128)S(1)}, bf16[2,512,512]{2,1,0:T(8,128)(2,1)}) custom-call(f32[264,512]{1,0:T(8,128)S(1)} %get-tuple-element.34.half, ...), custom_call_target="tpu_custom_call", output_to_operand_aliasing={{3}: (0, {}), {2}: (1, {}), {1}: (2, {})} | custom-call | flops 2415919104 | bytes 1048576 | tf_op jit(solution)/shard_map/pallas_call | solution.py:394
  31.0 3.8 %all-to-all-done.sums = f32[32,2,128]{2,1,0:T(2,128)S(1)} async-done(((f32[32,2,128]{2,1,0:T(2,128)}), f32[32,2,128]{2,1,0:T(2,128)S(1)}, u32[]{:S(2)}, u32[]{:S(2)}) %all-to-all-start) | async-done | bytes 32800 | tf_op jit(solution)/shard_map/all_to_all | solution.py:393
  34.8 1.2 %shard_map.64 = (f32[384,512]{1,0:T(8,128)S(1)}, f32[1,128]{1,0:T(1,128)S(1)}, bf16[2,512,512]{2,1,0:T(8,128)(2,1)S(1)}) custom-call(f32[264,512]{1,0:T(8,128)S(1)} %get-tuple-element.36.stat, bf16[2,512,512]{2,1,0:T(8,128)(2,1)} %get-tuple-element.37.g_in, f32[264,512]{1,0:T(8,128)S(1)} %get-tuple-element.38.square, ...), custom_call_target="tpu_custom_call" | custom-call | flops 805306368 | bytes 1048576 | tf_op jit(solution)/shard_map/pallas_call | solution.py:404
  36.2 1.2 %shard_map.65.middle = bf16[2,512,512]{2,1,0:T(8,128)(2,1)S(1)} custom-call(bf16[2,512,512]{2,1,0:T(8,128)(2,1)S(1)} %get-tuple-element.42.g, f32[384,512]{1,0:T(8,128)S(1)} %get-tuple-element.43.packed), custom_call_target="tpu_custom_call" | custom-call | flops 805306368 | bytes 1048576 | tf_op jit(solution)/shard_map/pallas_call | solution.py:412
  37.4 1.0 %collective-permute-done.7.packed = f32[384,512]{1,0:T(8,128)S(1)} collective-permute-done((f32[384,512]{1,0:T(8,128)S(1)}, f32[384,512]{1,0:T(8,128)S(1)}, u32[]{:S(2)}, u32[]{:S(2)}) %collective-permute-start.7) | collective-permute-done | bytes 786464 | tf_op jit(solution)/shard_map/ppermute | solution.py:69
  39.7 1.4 %collective-permute-start.14 = (f32[264,512]{1,0:T(8,128)S(1)}, f32[264,512]{1,0:T(8,128)S(1)}, u32[]{:S(2)}, u32[]{:S(2)}) collective-permute-start(f32[264,512]{1,0:T(8,128)S(1)} %get-tuple-element.36.stat), channel_id=1, source_target_pairs={{8,0},{24,8},{0,16},{16,24},{9,1},{25,9},{1,17},{17,25},{10,2},{26... | collective-permute-start | bytes 1622024 | tf_op jit(solution)/shard_map/ppermute | solution.py:403
  41.1 10.0 %collective-permute-done.12.refs_1_ = f32[192,512]{1,0:T(8,128)S(1)} collective-permute-done((f32[192,512]{1,0:T(8,128)S(1)}, f32[192,512]{1,0:T(8,128)S(1)}, u32[]{:S(2)}, u32[]{:S(2)}) %collective-permute-start.12) | collective-permute-done | bytes 393248 | tf_op jit(solution)/shard_map/ppermute | solution.py:69
  51.1 6.4 %collective-permute-done.8.refs_3_ = f32[64,512]{1,0:T(8,128)S(1)} collective-permute-done((f32[64,512]{1,0:T(8,128)S(1)}, f32[64,512]{1,0:T(8,128)S(1)}, u32[]{:S(2)}, u32[]{:S(2)}) %collective-permute-start.8) | collective-permute-done | bytes 131104 | tf_op jit(solution)/shard_map/ppermute | solution.py:69
  57.5 1.2 %collective-permute-start.9 = (f32[64,512]{1,0:T(8,128)S(1)}, f32[64,512]{1,0:T(8,128)S(1)}, u32[]{:S(2)}, u32[]{:S(2)}) collective-permute-start(f32[64,512]{1,0:T(8,128)S(1)} %collective-permute-done.8.refs_3_), channel_id=1, source_target_pairs={{0,8},{8,0},{16,24},{24,16},{1,9},{9,1},{17,25},{25,17},{2,10},{10... | collective-permute-start | bytes 393224 | tf_op jit(solution)/shard_map/ppermute | solution.py:69
  58.7 0.8 %collective-permute-start.10 = (f32[16,1,128]{2,1,0:T(1,128)S(1)}, f32[16,1,128]{2,1,0:T(1,128)S(1)}, u32[]{:S(2)}, u32[]{:S(2)}) collective-permute-start(f32[16,1,128]{2,1,0:T(1,128)S(1)} %get-tuple-element.46), channel_id=1, source_target_pairs={{0,16},{8,24},{16,0},{24,8},{1,17},{9,25},{17,1},{25,9},{2,18},{10... | collective-permute-start | bytes 24584 | tf_op jit(solution)/shard_map/ppermute | solution.py:69
  59.5 2.8 %collective-permute-done.10 = f32[16,1,128]{2,1,0:T(1,128)S(1)} collective-permute-done((f32[16,1,128]{2,1,0:T(1,128)S(1)}, f32[16,1,128]{2,1,0:T(1,128)S(1)}, u32[]{:S(2)}, u32[]{:S(2)}) %collective-permute-start.10) | collective-permute-done | bytes 8224 | tf_op jit(solution)/shard_map/ppermute | solution.py:69
  63.0 3.8 %all-to-all-start.1 = ((f32[16,1,128]{2,1,0:T(1,128)}), f32[16,1,128]{2,1,0:T(1,128)S(1)}, u32[]{:S(2)}, u32[]{:S(2)}) async-start(f32[16,1,128]{2,1,0:T(1,128)} %add.19), calls=%async_computation.1 | async-start | bytes 16384 | tf_op jit(solution)/shard_map/all_to_all | solution.py:432
  66.8 1.2 %shard_map.70 = f32[512,512]{1,0:T(8,128)} custom-call(f32[264,512]{1,0:T(8,128)S(1)} %collective-permute-done.14.packed), custom_call_target="tpu_custom_call" | custom-call | bytes 1048576 | tf_op jit(solution)/shard_map/pallas_call | solution.py:433
  68.0 3.8 %all-to-all-done.1.refs_1_ = f32[16,1,128]{2,1,0:T(1,128)S(1)} async-done(((f32[16,1,128]{2,1,0:T(1,128)}), f32[16,1,128]{2,1,0:T(1,128)S(1)}, u32[]{:S(2)}, u32[]{:S(2)}) %all-to-all-start.1) | async-done | bytes 8224 | tf_op jit(solution)/shard_map/all_to_all | solution.py:432
  71.8 1.0 %shard_map.67 = (f32[1024,512]{1,0:T(8,128)}, f32[1,128]{1,0:T(1,128)S(1)}) custom-call(f32[256,512]{1,0:T(8,128)S(1)} %get-tuple-element.45.refs_0_, f32[16,1,128]{2,1,0:T(1,128)S(1)} %all-to-all-done.1.refs_1_, f32[1,128]{1,0:T(1,128)S(1)} %get-tuple-element.47.refs_2_, f32[4,128]{1,0:T(4,128)S(1)} %get-tuple-element.48.refs_3_.refs_5_.refs_2_), custom_call_target="tpu_custom_call" | custom-call | bytes 1048576 | tf_op jit(solution)/shard_map/pallas_call | solution.py:453
  72.8 1.3 %shard_map.68.refs_3_ = f32[1024,512]{1,0:T(8,128)} custom-call(f32[256,512]{1,0:T(8,128)S(1)} %collective-permute-done.11.refs_0_, f32[192,512]{1,0:T(8,128)S(1)} %collective-permute-done.12.refs_1_, f32[192,512]{1,0:T(8,128)S(1)} %collective-permute-done.13.refs_2_, f32[64,512]{1,0:T(8,128)S(1)} %collective-permute-done.8.refs_3_, ...), custom_call_target="tpu_custom_call", output_to_operand_aliasing={{}: (6, {})} | custom-call | bytes 1048576 | tf_op jit(solution)/shard_map/pallas_call | solution.py:441
  74.1 0.7 shard_map.69
  (29 shorter events, 4.3 us)
Async XLA Ops:
  0.6 7.0 %copy-start.1 = (s32[1,2]{1,0:T(1,128)S(1)}, s32[1,2]{1,0:T(1,128)}, u32[]{:S(2)}) copy-start(s32[1,2]{1,0:T(1,128)} %owners.5) | copy-start | bytes 28
  0.6 7.0 %copy-start = (f32[1,1,512,512]{3,2,1,0:T(8,128)S(1)}, f32[1,1,512,512]{3,2,1,0:T(8,128)}, u32[]{:S(2)}) copy-start(f32[1,1,512,512]{3,2,1,0:T(8,128)} %param.6) | copy-start | bytes 3145732
  2.2 2.6 %collective-permute-start.1 = (f32[1,128,512]{2,1,0:T(8,128)S(1)}, f32[1,128,512]{2,1,0:T(8,128)S(1)}, u32[]{:S(2)}, u32[]{:S(2)}) collective-permute-start(f32[1,128,512]{2,1,0:T(8,128)S(1)} %get-tuple-element.30), channel_id=1, source_target_pairs={{0,8},{8,0},{16,24},{24,16},{1,9},{9,1},{17,25},{25,17},{2,10},{10... | collective-permute-start | bytes 786440 | tf_op jit(solution)/shard_map/ppermute | solution.py:69
  2.8 4.7 %collective-permute-start.3 = (f32[1,128,512]{2,1,0:T(8,128)S(1)}, f32[1,128,512]{2,1,0:T(8,128)S(1)}, u32[]{:S(2)}, u32[]{:S(2)}) collective-permute-start(f32[1,128,512]{2,1,0:T(8,128)S(1)} %get-tuple-element.32), channel_id=1, source_target_pairs={{0,8},{8,0},{16,24},{24,16},{1,9},{9,1},{17,25},{25,17},{2,10},{10... | collective-permute-start | bytes 786440 | tf_op jit(solution)/shard_map/ppermute | solution.py:69
  4.3 15.7 %collective-permute-start = (f32[1,256,512]{2,1,0:T(8,128)S(1)}, f32[1,256,512]{2,1,0:T(8,128)S(1)}, u32[]{:S(2)}, u32[]{:S(2)}) collective-permute-start(f32[1,256,512]{2,1,0:T(8,128)S(1)} %get-tuple-element.28), channel_id=1, source_target_pairs={{0,8},{8,0},{16,24},{24,16},{1,9},{9,1},{17,25},{25,17},{2,10},{10... | collective-permute-start | bytes 1572872 | tf_op jit(solution)/shard_map/ppermute | solution.py:69
  4.9 9.8 %collective-permute-start.2 = (f32[128,512]{1,0:T(8,128)S(1)}, f32[128,512]{1,0:T(8,128)S(1)}, u32[]{:S(2)}, u32[]{:S(2)}) collective-permute-start(f32[128,512]{1,0:T(8,128)S(1)} %add_bitcast_fusion.1), channel_id=1, source_target_pairs={{0,16},{8,24},{16,0},{24,8},{1,17},{9,25},{17,1},{25,9},{2,18},{10... | collective-permute-start | bytes 786440 | tf_op jit(solution)/shard_map/ppermute | solution.py:69
  7.6 12.5 %collective-permute-start.4 = (f32[128,512]{1,0:T(8,128)S(1)}, f32[128,512]{1,0:T(8,128)S(1)}, u32[]{:S(2)}, u32[]{:S(2)}) collective-permute-start(f32[128,512]{1,0:T(8,128)S(1)} %add_bitcast_fusion), channel_id=1, source_target_pairs={{0,16},{8,24},{16,0},{24,8},{1,17},{9,25},{17,1},{25,9},{2,18},{10... | collective-permute-start | bytes 786440 | tf_op jit(solution)/shard_map/ppermute | solution.py:69
  8.3 19.3 %collective-permute-start.6 = (f32[264,512]{1,0:T(8,128)S(1)}, f32[264,512]{1,0:T(8,128)S(1)}, u32[]{:S(2)}, u32[]{:S(2)}) collective-permute-start(f32[264,512]{1,0:T(8,128)S(1)} %get-tuple-element.35), channel_id=1, source_target_pairs={{0,8},{8,24},{16,0},{24,16},{1,9},{9,25},{17,1},{25,17},{2,10},{10... | collective-permute-start | bytes 1622024 | tf_op jit(solution)/shard_map/ppermute | solution.py:388
  20.8 6.8 %collective-permute-start.5 = (f32[264,512]{1,0:T(8,128)S(1)}, f32[264,512]{1,0:T(8,128)S(1)}, u32[]{:S(2)}, u32[]{:S(2)}) collective-permute-start(f32[264,512]{1,0:T(8,128)S(1)} %get-tuple-element.34.half), channel_id=1, source_target_pairs={{0,8},{8,0},{16,24},{24,16},{1,9},{9,1},{17,25},{25,17},{2,10},{10... | collective-permute-start | bytes 1622024 | tf_op jit(solution)/shard_map/ppermute | solution.py:69
  20.8 13.9 %all-to-all-start = ((f32[32,2,128]{2,1,0:T(2,128)}), f32[32,2,128]{2,1,0:T(2,128)S(1)}, u32[]{:S(2)}, u32[]{:S(2)}) async-start(f32[32,2,128]{2,1,0:T(2,128)} %get-tuple-element.41), calls=%async_computation | async-start | bytes 65536 | tf_op jit(solution)/shard_map/all_to_all | solution.py:393
  36.0 2.4 %collective-permute-start.7 = (f32[384,512]{1,0:T(8,128)S(1)}, f32[384,512]{1,0:T(8,128)S(1)}, u32[]{:S(2)}, u32[]{:S(2)}) collective-permute-start(f32[384,512]{1,0:T(8,128)S(1)} %get-tuple-element.43.packed), channel_id=1, source_target_pairs={{0,8},{8,0},{16,24},{24,16},{1,9},{9,1},{17,25},{25,17},{2,10},{10... | collective-permute-start | bytes 2359304 | tf_op jit(solution)/shard_map/ppermute | solution.py:69
  39.1 12.1 %collective-permute-start.12 = (f32[192,512]{1,0:T(8,128)S(1)}, f32[192,512]{1,0:T(8,128)S(1)}, u32[]{:S(2)}, u32[]{:S(2)}) collective-permute-start(f32[192,512]{1,0:T(8,128)S(1)} %get-tuple-element.50), channel_id=1, source_target_pairs={{0,16},{8,24},{16,0},{24,8},{1,17},{9,25},{17,1},{25,9},{2,18},{10... | collective-permute-start | bytes 1179656 | tf_op jit(solution)/shard_map/ppermute | solution.py:69
  39.7 27.0 %collective-permute-start.14 = (f32[264,512]{1,0:T(8,128)S(1)}, f32[264,512]{1,0:T(8,128)S(1)}, u32[]{:S(2)}, u32[]{:S(2)}) collective-permute-start(f32[264,512]{1,0:T(8,128)S(1)} %get-tuple-element.36.stat), channel_id=1, source_target_pairs={{8,0},{24,8},{0,16},{16,24},{9,1},{25,9},{1,17},{17,25},{10,2},{26... | collective-permute-start | bytes 1622024 | tf_op jit(solution)/shard_map/ppermute | solution.py:403
  41.1 31.6 %collective-permute-start.11 = (f32[256,512]{1,0:T(8,128)S(1)}, f32[256,512]{1,0:T(8,128)S(1)}, u32[]{:S(2)}, u32[]{:S(2)}) collective-permute-start(f32[256,512]{1,0:T(8,128)S(1)} %get-tuple-element.45.refs_0_), channel_id=1, source_target_pairs={{0,8},{8,0},{16,24},{24,16},{1,9},{9,1},{17,25},{25,17},{2,10},{10... | collective-permute-start | bytes 1572872 | tf_op jit(solution)/shard_map/ppermute | solution.py:69
  51.1 21.7 %collective-permute-start.13 = (f32[192,512]{1,0:T(8,128)S(1)}, f32[192,512]{1,0:T(8,128)S(1)}, u32[]{:S(2)}, u32[]{:S(2)}) collective-permute-start(f32[192,512]{1,0:T(8,128)S(1)} %collective-permute-done.12.refs_1_), channel_id=1, source_target_pairs={{0,8},{8,0},{16,24},{24,16},{1,9},{9,1},{17,25},{25,17},{2,10},{10... | collective-permute-start | bytes 1179656 | tf_op jit(solution)/shard_map/ppermute | solution.py:69
  51.1 6.4 %collective-permute-start.8 = (f32[64,512]{1,0:T(8,128)S(1)}, f32[64,512]{1,0:T(8,128)S(1)}, u32[]{:S(2)}, u32[]{:S(2)}) collective-permute-start(f32[64,512]{1,0:T(8,128)S(1)} %get-tuple-element.44), channel_id=1, source_target_pairs={{0,16},{8,24},{16,0},{24,8},{1,17},{9,25},{17,1},{25,9},{2,18},{10... | collective-permute-start | bytes 393224 | tf_op jit(solution)/shard_map/ppermute | solution.py:69
  57.5 16.6 %collective-permute-start.9 = (f32[64,512]{1,0:T(8,128)S(1)}, f32[64,512]{1,0:T(8,128)S(1)}, u32[]{:S(2)}, u32[]{:S(2)}) collective-permute-start(f32[64,512]{1,0:T(8,128)S(1)} %collective-permute-done.8.refs_3_), channel_id=1, source_target_pairs={{0,8},{8,0},{16,24},{24,16},{1,9},{9,1},{17,25},{25,17},{2,10},{10... | collective-permute-start | bytes 393224 | tf_op jit(solution)/shard_map/ppermute | solution.py:69
  58.7 3.7 %collective-permute-start.10 = (f32[16,1,128]{2,1,0:T(1,128)S(1)}, f32[16,1,128]{2,1,0:T(1,128)S(1)}, u32[]{:S(2)}, u32[]{:S(2)}) collective-permute-start(f32[16,1,128]{2,1,0:T(1,128)S(1)} %get-tuple-element.46), channel_id=1, source_target_pairs={{0,16},{8,24},{16,0},{24,8},{1,17},{9,25},{17,1},{25,9},{2,18},{10... | collective-permute-start | bytes 24584 | tf_op jit(solution)/shard_map/ppermute | solution.py:69
  63.0 8.8 %all-to-all-start.1 = ((f32[16,1,128]{2,1,0:T(1,128)}), f32[16,1,128]{2,1,0:T(1,128)S(1)}, u32[]{:S(2)}, u32[]{:S(2)}) async-start(f32[16,1,128]{2,1,0:T(1,128)} %add.19), calls=%async_computation.1 | async-start | bytes 16384 | tf_op jit(solution)/shard_map/all_to_all | solution.py:432

commit v7 on v6

--- a/solution.py
+++ b/solution.py
@@ -12,7 +12,6 @@
 BLOCK = 512
 HALF = BLOCK // 2
 PACKED = HALF + 8
-CHUNK = 64
 MOST = HALF - 64
 
 decay_rate = 0.95
@@ -306,12 +305,11 @@
 def write_pieces(pieces, scale, out, scaled, sems):
     copies, base = [], 0
     for first, src in pieces:
-        for r in range(0, src.shape[0], CHUNK):
-            here = pl.ds(base + r, CHUNK)
-            scaled[here] = src[pl.ds(r, CHUNK)] * scale
-            start = pl.multiple_of(first + r, CHUNK)
-            copies.append(pltpu.make_async_copy(scaled.at[here], out.at[pl.ds(start, CHUNK)], sems.at[len(copies)]))
-            copies[-1].start()
+        here = pl.ds(base, src.shape[0])
+        scaled[here] = src[...] * scale
+        start = pl.multiple_of(first, 64)
+        copies.append(pltpu.make_async_copy(scaled.at[here], out.at[pl.ds(start, src.shape[0])], sems.at[len(copies)]))
+        copies[-1].start()
         base += src.shape[0]
     for copy in copies:
         copy.wait()
@@ -435,7 +433,7 @@
 
     def landing(found):
         count = sum(x.shape[0] for x in found)
-        return [pltpu.VMEM((count, BLOCK), f32), pltpu.SemaphoreType.DMA((count // CHUNK,))]
+        return [pltpu.VMEM((count, BLOCK), f32), pltpu.SemaphoreType.DMA((len(found),))]
 
     def place(placed, plan, *found):
         (placed,) = call(

time: 75.1 us -> 75.1 us (level)
  no operation moved by 1% of the time
where the time goes in v7:
time: 75.1 us; the launch traced here: 74.8 us
  waiting for transfers between devices  39.4 us (52%)
  starting transfers between devices  18.9 us (25%)
  Pallas kernels  15 us (20%)
  between operations  0.79 us (1%)
    ppermute x13, waiting for transfers between devices, flip(): lax.ppermute(x, 'rep', [(i, i ^ mask) for i in range(lax.axis_size('rep'))])  31.8 us
    ppermute x13, starting transfers between devices, flip(): lax.ppermute(x, 'rep', [(i, i ^ mask) for i in range(lax.axis_size('rep'))])  6.75 us
    all_to_all x1, starting transfers between devices, per_device(): sums = lax.all_to_all(sums, AXES, 0, 0)  6.74 us
    all_to_all x1, starting transfers between devices, per_device(): prec = lax.all_to_all(prec, AXES, 0, 0, axis_index_groups=groups)  3.83 us
    all_to_all x1, waiting for transfers between devices, per_device(): sums = lax.all_to_all(sums, AXES, 0, 0)  3.81 us
    all_to_all x1, waiting for transfers between devices, per_device(): prec = lax.all_to_all(prec, AXES, 0, 0, axis_index_groups=groups)  3.8 us
    pallas_call x1, Pallas kernels, per_device(): call(update_stat, [(2, 128)] + [(PACKED, BLOCK)] * 3 + [pltpu.HBM((2,) +...  3.35 us
    pallas_call x2, Pallas kernels, terms(): call(functools.partial(grad_terms, plan), [(len(chips), count, BLOCK) for...  3.04 us
  transfers between devices with their start and end apart: 17, of which 8 were waited for; matrix products, arithmetic and copies ran while one was open for 1% of the time, Pallas kernels for 14%

profile of v7, /device:TPU:0, one launch (start us, length us, event | category | flops | bytes accessed | tf_op | source)
XLA Modules:
  0.0 74.8 jit_solution(6598230073214072806)
XLA Ops:
  0.7 1.6 %shard_map.60 = (f32[1,128,512]{2,1,0:T(8,128)S(1)}, f32[1,128,512]{2,1,0:T(8,128)S(1)}, f32[1,128,512]{2,1,0:T(8,128)S(1)}, f32[1,128,512]{2,1,0:T(8,128)S(1)}) custom-call(bf16[256,1024]{1,0:T(8,128)(2,1)} %acts.3, bf16[256,512]{1,0:T(8,128)(2,1)} %grads.3, s32[1,2]{1,0:T(1,128)} %owners.5), custom_call_target="tpu_custom_call" | custom-call | flops 268435456 | bytes 1048576 | tf_op jit(solution)/shard_map/pallas_call | solution.py:351
  2.9 1.5 %shard_map.59 = (f32[1,256,512]{2,1,0:T(8,128)S(1)}, f32[1,256,512]{2,1,0:T(8,128)S(1)}) custom-call(bf16[256,1024]{1,0:T(8,128)(2,1)} %acts.3, bf16[256,512]{1,0:T(8,128)(2,1)} %grads.3, s32[1,2]{1,0:T(1,128)} %owners.5), custom_call_target="tpu_custom_call" | custom-call | flops 134217728 | bytes 1048576 | tf_op jit(solution)/shard_map/pallas_call | solution.py:351
  4.9 2.6 %collective-permute-start.2 = (f32[128,512]{1,0:T(8,128)S(1)}, f32[128,512]{1,0:T(8,128)S(1)}, u32[]{:S(2)}, u32[]{:S(2)}) collective-permute-start(f32[128,512]{1,0:T(8,128)S(1)} %add_bitcast_fusion.1), channel_id=1, source_target_pairs={{0,16},{8,24},{16,0},{24,8},{1,17},{9,25},{17,1},{25,9},{2,18},{10... | collective-permute-start | bytes 786440 | tf_op jit(solution)/shard_map/ppermute | solution.py:68
  8.4 6.2 %collective-permute-done.2.rest_a = f32[128,512]{1,0:T(8,128)S(1)} collective-permute-done((f32[128,512]{1,0:T(8,128)S(1)}, f32[128,512]{1,0:T(8,128)S(1)}, u32[]{:S(2)}, u32[]{:S(2)}) %collective-permute-start.2) | collective-permute-done | bytes 262176 | tf_op jit(solution)/shard_map/ppermute | solution.py:68
  14.7 5.4 %collective-permute-done.4.rest_b = f32[128,512]{1,0:T(8,128)S(1)} collective-permute-done((f32[128,512]{1,0:T(8,128)S(1)}, f32[128,512]{1,0:T(8,128)S(1)}, u32[]{:S(2)}, u32[]{:S(2)}) %collective-permute-start.4) | collective-permute-done | bytes 262176 | tf_op jit(solution)/shard_map/ppermute | solution.py:68
  20.0 0.8 %shard_map.62 = (f32[264,512]{1,0:T(8,128)S(1)}, f32[32,2,128]{2,1,0:T(2,128)}) custom-call(f32[1,256,512]{2,1,0:T(8,128)S(1)} %get-tuple-element.27.keep, f32[1,256,512]{2,1,0:T(8,128)S(1)} %collective-permute-done.got, f32[128,512]{1,0:T(8,128)S(1)} %collective-permute-done.2.rest_a, f32[128,512]{1,0:T(8,128)S(1)} %collective-permute-done.4.rest_b, ...), custom_call_target="tpu_custom_call" | custom-call | bytes 1048576 | tf_op jit(solution)/shard_map/pallas_call | solution.py:387
  20.8 6.7 %all-to-all-start = ((f32[32,2,128]{2,1,0:T(2,128)}), f32[32,2,128]{2,1,0:T(2,128)S(1)}, u32[]{:S(2)}, u32[]{:S(2)}) async-start(f32[32,2,128]{2,1,0:T(2,128)} %get-tuple-element.41), calls=%async_computation | async-start | bytes 65536 | tf_op jit(solution)/shard_map/all_to_all | solution.py:391
  27.6 3.4 %shard_map.63 = (f32[2,128]{1,0:T(2,128)S(1)}, f32[264,512]{1,0:T(8,128)S(1)}, f32[264,512]{1,0:T(8,128)S(1)}, f32[264,512]{1,0:T(8,128)S(1)}, bf16[2,512,512]{2,1,0:T(8,128)(2,1)}) custom-call(f32[264,512]{1,0:T(8,128)S(1)} %get-tuple-element.34.half, ...), custom_call_target="tpu_custom_call", output_to_operand_aliasing={{3}: (0, {}), {2}: (1, {}), {1}: (2, {})} | custom-call | flops 2415919104 | bytes 1048576 | tf_op jit(solution)/shard_map/pallas_call | solution.py:392
  31.0 3.8 %all-to-all-done.sums = f32[32,2,128]{2,1,0:T(2,128)S(1)} async-done(((f32[32,2,128]{2,1,0:T(2,128)}), f32[32,2,128]{2,1,0:T(2,128)S(1)}, u32[]{:S(2)}, u32[]{:S(2)}) %all-to-all-start) | async-done | bytes 32800 | tf_op jit(solution)/shard_map/all_to_all | solution.py:391
  34.8 1.2 %shard_map.64 = (f32[384,512]{1,0:T(8,128)S(1)}, f32[1,128]{1,0:T(1,128)S(1)}, bf16[2,512,512]{2,1,0:T(8,128)(2,1)S(1)}) custom-call(f32[264,512]{1,0:T(8,128)S(1)} %get-tuple-element.36.stat, bf16[2,512,512]{2,1,0:T(8,128)(2,1)} %get-tuple-element.37.g_in, f32[264,512]{1,0:T(8,128)S(1)} %get-tuple-element.38.square, ...), custom_call_target="tpu_custom_call" | custom-call | flops 805306368 | bytes 1048576 | tf_op jit(solution)/shard_map/pallas_call | solution.py:402
  36.2 1.2 %shard_map.65.middle = bf16[2,512,512]{2,1,0:T(8,128)(2,1)S(1)} custom-call(bf16[2,512,512]{2,1,0:T(8,128)(2,1)S(1)} %get-tuple-element.42.g, f32[384,512]{1,0:T(8,128)S(1)} %get-tuple-element.43.packed), custom_call_target="tpu_custom_call" | custom-call | flops 805306368 | bytes 1048576 | tf_op jit(solution)/shard_map/pallas_call | solution.py:410
  37.4 1.0 %collective-permute-done.7.packed = f32[384,512]{1,0:T(8,128)S(1)} collective-permute-done((f32[384,512]{1,0:T(8,128)S(1)}, f32[384,512]{1,0:T(8,128)S(1)}, u32[]{:S(2)}, u32[]{:S(2)}) %collective-permute-start.7) | collective-permute-done | bytes 786464 | tf_op jit(solution)/shard_map/ppermute | solution.py:68
  39.7 1.4 %collective-permute-start.14 = (f32[264,512]{1,0:T(8,128)S(1)}, f32[264,512]{1,0:T(8,128)S(1)}, u32[]{:S(2)}, u32[]{:S(2)}) collective-permute-start(f32[264,512]{1,0:T(8,128)S(1)} %get-tuple-element.36.stat), channel_id=1, source_target_pairs={{8,0},{24,8},{0,16},{16,24},{9,1},{25,9},{1,17},{17,25},{10,2},{26... | collective-permute-start | bytes 1622024 | tf_op jit(solution)/shard_map/ppermute | solution.py:401
  41.1 10.0 %collective-permute-done.12.refs_1_ = f32[192,512]{1,0:T(8,128)S(1)} collective-permute-done((f32[192,512]{1,0:T(8,128)S(1)}, f32[192,512]{1,0:T(8,128)S(1)}, u32[]{:S(2)}, u32[]{:S(2)}) %collective-permute-start.12) | collective-permute-done | bytes 393248 | tf_op jit(solution)/shard_map/ppermute | solution.py:68
  51.1 6.4 %collective-permute-done.8.refs_3_ = f32[64,512]{1,0:T(8,128)S(1)} collective-permute-done((f32[64,512]{1,0:T(8,128)S(1)}, f32[64,512]{1,0:T(8,128)S(1)}, u32[]{:S(2)}, u32[]{:S(2)}) %collective-permute-start.8) | collective-permute-done | bytes 131104 | tf_op jit(solution)/shard_map/ppermute | solution.py:68
  57.5 1.2 %collective-permute-start.9 = (f32[64,512]{1,0:T(8,128)S(1)}, f32[64,512]{1,0:T(8,128)S(1)}, u32[]{:S(2)}, u32[]{:S(2)}) collective-permute-start(f32[64,512]{1,0:T(8,128)S(1)} %collective-permute-done.8.refs_3_), channel_id=1, source_target_pairs={{0,8},{8,0},{16,24},{24,16},{1,9},{9,1},{17,25},{25,17},{2,10},{10... | collective-permute-start | bytes 393224 | tf_op jit(solution)/shard_map/ppermute | solution.py:68
  58.7 0.8 %collective-permute-start.10 = (f32[16,1,128]{2,1,0:T(1,128)S(1)}, f32[16,1,128]{2,1,0:T(1,128)S(1)}, u32[]{:S(2)}, u32[]{:S(2)}) collective-permute-start(f32[16,1,128]{2,1,0:T(1,128)S(1)} %get-tuple-element.46), channel_id=1, source_target_pairs={{0,16},{8,24},{16,0},{24,8},{1,17},{9,25},{17,1},{25,9},{2,18},{10... | collective-permute-start | bytes 24584 | tf_op jit(solution)/shard_map/ppermute | solution.py:68
  59.5 2.8 %collective-permute-done.10 = f32[16,1,128]{2,1,0:T(1,128)S(1)} collective-permute-done((f32[16,1,128]{2,1,0:T(1,128)S(1)}, f32[16,1,128]{2,1,0:T(1,128)S(1)}, u32[]{:S(2)}, u32[]{:S(2)}) %collective-permute-start.10) | collective-permute-done | bytes 8224 | tf_op jit(solution)/shard_map/ppermute | solution.py:68
  63.0 3.8 %all-to-all-start.1 = ((f32[16,1,128]{2,1,0:T(1,128)}), f32[16,1,128]{2,1,0:T(1,128)S(1)}, u32[]{:S(2)}, u32[]{:S(2)}) async-start(f32[16,1,128]{2,1,0:T(1,128)} %add.19), calls=%async_computation.1 | async-start | bytes 16384 | tf_op jit(solution)/shard_map/all_to_all | solution.py:430
  66.8 1.2 %shard_map.70 = f32[512,512]{1,0:T(8,128)} custom-call(f32[264,512]{1,0:T(8,128)S(1)} %collective-permute-done.14.packed), custom_call_target="tpu_custom_call" | custom-call | bytes 1048576 | tf_op jit(solution)/shard_map/pallas_call | solution.py:431
  68.0 3.8 %all-to-all-done.1.refs_1_ = f32[16,1,128]{2,1,0:T(1,128)S(1)} async-done(((f32[16,1,128]{2,1,0:T(1,128)}), f32[16,1,128]{2,1,0:T(1,128)S(1)}, u32[]{:S(2)}, u32[]{:S(2)}) %all-to-all-start.1) | async-done | bytes 8224 | tf_op jit(solution)/shard_map/all_to_all | solution.py:430
  71.8 1.0 %shard_map.67 = (f32[1024,512]{1,0:T(8,128)}, f32[1,128]{1,0:T(1,128)S(1)}) custom-call(f32[256,512]{1,0:T(8,128)S(1)} %get-tuple-element.45.refs_0_, f32[16,1,128]{2,1,0:T(1,128)S(1)} %all-to-all-done.1.refs_1_, f32[1,128]{1,0:T(1,128)S(1)} %get-tuple-element.47.refs_2_, f32[4,128]{1,0:T(4,128)S(1)} %get-tuple-element.48.refs_3_.refs_5_.refs_2_), custom_call_target="tpu_custom_call" | custom-call | bytes 1048576 | tf_op jit(solution)/shard_map/pallas_call | solution.py:451
  72.8 1.2 %shard_map.68.refs_3_ = f32[1024,512]{1,0:T(8,128)} custom-call(f32[256,512]{1,0:T(8,128)S(1)} %collective-permute-done.11.refs_0_, f32[192,512]{1,0:T(8,128)S(1)} %collective-permute-done.12.refs_1_, f32[192,512]{1,0:T(8,128)S(1)} %collective-permute-done.13.refs_2_, f32[64,512]{1,0:T(8,128)S(1)} %collective-permute-done.8.refs_3_, ...), custom_call_target="tpu_custom_call", output_to_operand_aliasing={{}: (6, {})} | custom-call | bytes 1048576 | tf_op jit(solution)/shard_map/pallas_call | solution.py:439
  74.1 0.7 shard_map.69
  (29 shorter events, 4.3 us)
Async XLA Ops:
  0.6 7.0 %copy-start.1 = (s32[1,2]{1,0:T(1,128)S(1)}, s32[1,2]{1,0:T(1,128)}, u32[]{:S(2)}) copy-start(s32[1,2]{1,0:T(1,128)} %owners.5) | copy-start | bytes 28
  0.6 7.0 %copy-start = (f32[1,1,512,512]{3,2,1,0:T(8,128)S(1)}, f32[1,1,512,512]{3,2,1,0:T(8,128)}, u32[]{:S(2)}) copy-start(f32[1,1,512,512]{3,2,1,0:T(8,128)} %param.6) | copy-start | bytes 3145732
  2.2 2.6 %collective-permute-start.1 = (f32[1,128,512]{2,1,0:T(8,128)S(1)}, f32[1,128,512]{2,1,0:T(8,128)S(1)}, u32[]{:S(2)}, u32[]{:S(2)}) collective-permute-start(f32[1,128,512]{2,1,0:T(8,128)S(1)} %get-tuple-element.30), channel_id=1, source_target_pairs={{0,8},{8,0},{16,24},{24,16},{1,9},{9,1},{17,25},{25,17},{2,10},{10... | collective-permute-start | bytes 786440 | tf_op jit(solution)/shard_map/ppermute | solution.py:68
  2.8 4.7 %collective-permute-start.3 = (f32[1,128,512]{2,1,0:T(8,128)S(1)}, f32[1,128,512]{2,1,0:T(8,128)S(1)}, u32[]{:S(2)}, u32[]{:S(2)}) collective-permute-start(f32[1,128,512]{2,1,0:T(8,128)S(1)} %get-tuple-element.32), channel_id=1, source_target_pairs={{0,8},{8,0},{16,24},{24,16},{1,9},{9,1},{17,25},{25,17},{2,10},{10... | collective-permute-start | bytes 786440 | tf_op jit(solution)/shard_map/ppermute | solution.py:68
  4.3 15.7 %collective-permute-start = (f32[1,256,512]{2,1,0:T(8,128)S(1)}, f32[1,256,512]{2,1,0:T(8,128)S(1)}, u32[]{:S(2)}, u32[]{:S(2)}) collective-permute-start(f32[1,256,512]{2,1,0:T(8,128)S(1)} %get-tuple-element.28), channel_id=1, source_target_pairs={{0,8},{8,0},{16,24},{24,16},{1,9},{9,1},{17,25},{25,17},{2,10},{10... | collective-permute-start | bytes 1572872 | tf_op jit(solution)/shard_map/ppermute | solution.py:68
  4.9 9.8 %collective-permute-start.2 = (f32[128,512]{1,0:T(8,128)S(1)}, f32[128,512]{1,0:T(8,128)S(1)}, u32[]{:S(2)}, u32[]{:S(2)}) collective-permute-start(f32[128,512]{1,0:T(8,128)S(1)} %add_bitcast_fusion.1), channel_id=1, source_target_pairs={{0,16},{8,24},{16,0},{24,8},{1,17},{9,25},{17,1},{25,9},{2,18},{10... | collective-permute-start | bytes 786440 | tf_op jit(solution)/shard_map/ppermute | solution.py:68
  7.6 12.5 %collective-permute-start.4 = (f32[128,512]{1,0:T(8,128)S(1)}, f32[128,512]{1,0:T(8,128)S(1)}, u32[]{:S(2)}, u32[]{:S(2)}) collective-permute-start(f32[128,512]{1,0:T(8,128)S(1)} %add_bitcast_fusion), channel_id=1, source_target_pairs={{0,16},{8,24},{16,0},{24,8},{1,17},{9,25},{17,1},{25,9},{2,18},{10... | collective-permute-start | bytes 786440 | tf_op jit(solution)/shard_map/ppermute | solution.py:68
  8.3 19.3 %collective-permute-start.6 = (f32[264,512]{1,0:T(8,128)S(1)}, f32[264,512]{1,0:T(8,128)S(1)}, u32[]{:S(2)}, u32[]{:S(2)}) collective-permute-start(f32[264,512]{1,0:T(8,128)S(1)} %get-tuple-element.35), channel_id=1, source_target_pairs={{0,8},{8,24},{16,0},{24,16},{1,9},{9,25},{17,1},{25,17},{2,10},{10... | collective-permute-start | bytes 1622024 | tf_op jit(solution)/shard_map/ppermute | solution.py:386
  20.8 6.8 %collective-permute-start.5 = (f32[264,512]{1,0:T(8,128)S(1)}, f32[264,512]{1,0:T(8,128)S(1)}, u32[]{:S(2)}, u32[]{:S(2)}) collective-permute-start(f32[264,512]{1,0:T(8,128)S(1)} %get-tuple-element.34.half), channel_id=1, source_target_pairs={{0,8},{8,0},{16,24},{24,16},{1,9},{9,1},{17,25},{25,17},{2,10},{10... | collective-permute-start | bytes 1622024 | tf_op jit(solution)/shard_map/ppermute | solution.py:68
  20.8 13.9 %all-to-all-start = ((f32[32,2,128]{2,1,0:T(2,128)}), f32[32,2,128]{2,1,0:T(2,128)S(1)}, u32[]{:S(2)}, u32[]{:S(2)}) async-start(f32[32,2,128]{2,1,0:T(2,128)} %get-tuple-element.41), calls=%async_computation | async-start | bytes 65536 | tf_op jit(solution)/shard_map/all_to_all | solution.py:391
  36.0 2.4 %collective-permute-start.7 = (f32[384,512]{1,0:T(8,128)S(1)}, f32[384,512]{1,0:T(8,128)S(1)}, u32[]{:S(2)}, u32[]{:S(2)}) collective-permute-start(f32[384,512]{1,0:T(8,128)S(1)} %get-tuple-element.43.packed), channel_id=1, source_target_pairs={{0,8},{8,0},{16,24},{24,16},{1,9},{9,1},{17,25},{25,17},{2,10},{10... | collective-permute-start | bytes 2359304 | tf_op jit(solution)/shard_map/ppermute | solution.py:68
  39.1 12.1 %collective-permute-start.12 = (f32[192,512]{1,0:T(8,128)S(1)}, f32[192,512]{1,0:T(8,128)S(1)}, u32[]{:S(2)}, u32[]{:S(2)}) collective-permute-start(f32[192,512]{1,0:T(8,128)S(1)} %get-tuple-element.50), channel_id=1, source_target_pairs={{0,16},{8,24},{16,0},{24,8},{1,17},{9,25},{17,1},{25,9},{2,18},{10... | collective-permute-start | bytes 1179656 | tf_op jit(solution)/shard_map/ppermute | solution.py:68
  39.7 27.0 %collective-permute-start.14 = (f32[264,512]{1,0:T(8,128)S(1)}, f32[264,512]{1,0:T(8,128)S(1)}, u32[]{:S(2)}, u32[]{:S(2)}) collective-permute-start(f32[264,512]{1,0:T(8,128)S(1)} %get-tuple-element.36.stat), channel_id=1, source_target_pairs={{8,0},{24,8},{0,16},{16,24},{9,1},{25,9},{1,17},{17,25},{10,2},{26... | collective-permute-start | bytes 1622024 | tf_op jit(solution)/shard_map/ppermute | solution.py:401
  41.1 31.6 %collective-permute-start.11 = (f32[256,512]{1,0:T(8,128)S(1)}, f32[256,512]{1,0:T(8,128)S(1)}, u32[]{:S(2)}, u32[]{:S(2)}) collective-permute-start(f32[256,512]{1,0:T(8,128)S(1)} %get-tuple-element.45.refs_0_), channel_id=1, source_target_pairs={{0,8},{8,0},{16,24},{24,16},{1,9},{9,1},{17,25},{25,17},{2,10},{10... | collective-permute-start | bytes 1572872 | tf_op jit(solution)/shard_map/ppermute | solution.py:68
  51.1 21.7 %collective-permute-start.13 = (f32[192,512]{1,0:T(8,128)S(1)}, f32[192,512]{1,0:T(8,128)S(1)}, u32[]{:S(2)}, u32[]{:S(2)}) collective-permute-start(f32[192,512]{1,0:T(8,128)S(1)} %collective-permute-done.12.refs_1_), channel_id=1, source_target_pairs={{0,8},{8,0},{16,24},{24,16},{1,9},{9,1},{17,25},{25,17},{2,10},{10... | collective-permute-start | bytes 1179656 | tf_op jit(solution)/shard_map/ppermute | solution.py:68
  51.1 6.4 %collective-permute-start.8 = (f32[64,512]{1,0:T(8,128)S(1)}, f32[64,512]{1,0:T(8,128)S(1)}, u32[]{:S(2)}, u32[]{:S(2)}) collective-permute-start(f32[64,512]{1,0:T(8,128)S(1)} %get-tuple-element.44), channel_id=1, source_target_pairs={{0,16},{8,24},{16,0},{24,8},{1,17},{9,25},{17,1},{25,9},{2,18},{10... | collective-permute-start | bytes 393224 | tf_op jit(solution)/shard_map/ppermute | solution.py:68
  57.5 16.6 %collective-permute-start.9 = (f32[64,512]{1,0:T(8,128)S(1)}, f32[64,512]{1,0:T(8,128)S(1)}, u32[]{:S(2)}, u32[]{:S(2)}) collective-permute-start(f32[64,512]{1,0:T(8,128)S(1)} %collective-permute-done.8.refs_3_), channel_id=1, source_target_pairs={{0,8},{8,0},{16,24},{24,16},{1,9},{9,1},{17,25},{25,17},{2,10},{10... | collective-permute-start | bytes 393224 | tf_op jit(solution)/shard_map/ppermute | solution.py:68
  58.7 3.7 %collective-permute-start.10 = (f32[16,1,128]{2,1,0:T(1,128)S(1)}, f32[16,1,128]{2,1,0:T(1,128)S(1)}, u32[]{:S(2)}, u32[]{:S(2)}) collective-permute-start(f32[16,1,128]{2,1,0:T(1,128)S(1)} %get-tuple-element.46), channel_id=1, source_target_pairs={{0,16},{8,24},{16,0},{24,8},{1,17},{9,25},{17,1},{25,9},{2,18},{10... | collective-permute-start | bytes 24584 | tf_op jit(solution)/shard_map/ppermute | solution.py:68
  63.0 8.8 %all-to-all-start.1 = ((f32[16,1,128]{2,1,0:T(1,128)}), f32[16,1,128]{2,1,0:T(1,128)S(1)}, u32[]{:S(2)}, u32[]{:S(2)}) async-start(f32[16,1,128]{2,1,0:T(1,128)} %add.19), calls=%async_computation.1 | async-start | bytes 16384 | tf_op jit(solution)/shard_map/all_to_all | solution.py:430

commit v8 on v6

--- a/solution.py
+++ b/solution.py
@@ -115,12 +115,15 @@
     return jnp.where(i <= j, u, ut), jnp.where(i > j, u, jnp.where(i < j, ut, diag))
 
 
-def pack_stat(pairs, stat, owners, out, trace, rows):
+def pack_stat(pairs, source, owners, out, trace, rows, stat, sem):
+    copy = pltpu.make_async_copy(source, stat, sem)
+    copy.start()
     chip, core = chip_core()
     for n in range(2 * pairs):
         half = core if n < pairs else 1 - core
         row = owners[0, lax.bitwise_xor(chip, jnp.int32(n % pairs))] * BLOCK + half * HALF
         rows[n : n + 1, :] = jnp.full((1, 128), row.astype(f32))
+    copy.wait()
     i, j = triangle()
     a, c = stat[LOW, LOW], stat[TOP, TOP]
     pack_into(out, a, stat[LOW, TOP], c)
@@ -131,7 +134,7 @@
     outs, (av, gv, ov, sems) = refs[: len(plan)], refs[len(plan) :]
     chip, core = chip_core()
     copies = [
-        pltpu.make_async_copy(src, dst, sems.at[k]) for k, (src, dst) in enumerate(((owners, ov), (acts, av), (grads, gv)))
+        pltpu.make_async_copy(src, dst, sems.at[k]) for k, (src, dst) in enumerate(((acts, av), (grads, gv), (owners, ov)))
     ]
     for copy in copies:
         copy.start()
@@ -383,8 +386,11 @@
         arrived = [(x[:quarter], x[quarter:]) for x in arrived]
     shuffle = [(s * pairs + p, 2 * p + 1 - s) for s in range(2) for p in range(pairs)]
     packed, trace, rows = call(
-        functools.partial(pack_stat, pairs), [(PACKED, BLOCK), (1, 128), (2 * pairs, 128)], [VMEM, SMEM]
-    )(statistics[0, 0], owner_blocks)
+        functools.partial(pack_stat, pairs),
+        [(PACKED, BLOCK), (1, 128), (2 * pairs, 128)],
+        [HBM, SMEM],
+        [pltpu.VMEM(square, f32), pltpu.SemaphoreType.DMA],
+    )(in_hbm(statistics[0, 0]), owner_blocks)
     old = lax.ppermute(packed, "rep", shuffle)
     half, sums = call(
         functools.partial(finish_half, devices), [(PACKED, BLOCK), (devices, 2, 128)], [VMEM] * 5

time: 75.1 us -> 75.1 us (level)
  waiting for transfers between devices: 39.4 us -> 38.2 us
  Pallas kernels: 15.1 us -> 16.2 us
    pallas_call x1, Pallas kernels: 0.6 us -> 1.83 us  [per_device(): call(functools.partial(pack_stat, pairs), [(PACKED, BLOCK), (1, 128), (2...]
    ppermute x13, waiting for transfers between devices: 31.8 us -> 30.6 us  [flip(): lax.ppermute(x, 'rep', [(i, i ^ mask) for i in range(lax.axis_size('rep'))])]
  transfers between devices with their start and end apart: 17 -> 17, of which waited for: 8 -> 8; matrix products, arithmetic and copies ran while one was open for 1% -> 1% of each run, Pallas kernels for 14% -> 16%
where the time goes in v8:
time: 75.1 us; the launch traced here: 74.7 us
  waiting for transfers between devices  38.2 us (51%)
  starting transfers between devices  18.9 us (25%)
  Pallas kernels  16.2 us (22%)
  between operations  0.78 us (1%)
    ppermute x13, waiting for transfers between devices, flip(): lax.ppermute(x, 'rep', [(i, i ^ mask) for i in range(lax.axis_size('rep'))])  30.6 us
    ppermute x13, starting transfers between devices, flip(): lax.ppermute(x, 'rep', [(i, i ^ mask) for i in range(lax.axis_size('rep'))])  6.76 us
    all_to_all x1, starting transfers between devices, per_device(): sums = lax.all_to_all(sums, AXES, 0, 0)  6.74 us
    all_to_all x1, starting transfers between devices, per_device(): prec = lax.all_to_all(prec, AXES, 0, 0, axis_index_groups=groups)  3.83 us
    all_to_all x1, waiting for transfers between devices, per_device(): sums = lax.all_to_all(sums, AXES, 0, 0)  3.81 us
    all_to_all x1, waiting for transfers between devices, per_device(): prec = lax.all_to_all(prec, AXES, 0, 0, axis_index_groups=groups)  3.8 us
    pallas_call x1, Pallas kernels, per_device(): call(update_stat, [(2, 128)] + [(PACKED, BLOCK)] * 3 + [pltpu.HBM((2,) +...  3.35 us
    pallas_call x2, Pallas kernels, terms(): call(functools.partial(grad_terms, plan), [(len(chips), count, BLOCK) for...  2.98 us
  transfers between devices with their start and end apart: 17, of which 8 were waited for; matrix products, arithmetic and copies ran while one was open for 1% of the time, Pallas kernels for 16%

profile of v8, /device:TPU:0, one launch (start us, length us, event | category | flops | bytes accessed | tf_op | source)
XLA Modules:
  0.0 74.7 jit_solution(9083621446196040427)
XLA Ops:
  0.6 1.5 %shard_map.60 = (f32[1,128,512]{2,1,0:T(8,128)S(1)}, f32[1,128,512]{2,1,0:T(8,128)S(1)}, f32[1,128,512]{2,1,0:T(8,128)S(1)}, f32[1,128,512]{2,1,0:T(8,128)S(1)}) custom-call(bf16[256,1024]{1,0:T(8,128)(2,1)} %acts.3, bf16[256,512]{1,0:T(8,128)(2,1)} %grads.3, s32[1,2]{1,0:T(1,128)} %owners.5), custom_call_target="tpu_custom_call" | custom-call | flops 268435456 | bytes 1048576 | tf_op jit(solution)/shard_map/pallas_call | solution.py:356
  2.8 1.5 %shard_map.59 = (f32[1,256,512]{2,1,0:T(8,128)S(1)}, f32[1,256,512]{2,1,0:T(8,128)S(1)}) custom-call(bf16[256,1024]{1,0:T(8,128)(2,1)} %acts.3, bf16[256,512]{1,0:T(8,128)(2,1)} %grads.3, s32[1,2]{1,0:T(1,128)} %owners.5), custom_call_target="tpu_custom_call" | custom-call | flops 134217728 | bytes 1048576 | tf_op jit(solution)/shard_map/pallas_call | solution.py:356
  4.8 2.6 %collective-permute-start.2 = (f32[128,512]{1,0:T(8,128)S(1)}, f32[128,512]{1,0:T(8,128)S(1)}, u32[]{:S(2)}, u32[]{:S(2)}) collective-permute-start(f32[128,512]{1,0:T(8,128)S(1)} %add_bitcast_fusion.1), channel_id=1, source_target_pairs={{0,16},{8,24},{16,0},{24,8},{1,17},{9,25},{17,1},{25,9},{2,18},{10... | collective-permute-start | bytes 786440 | tf_op jit(solution)/shard_map/ppermute | solution.py:69
  7.6 1.8 %shard_map.61 = (f32[264,512]{1,0:T(8,128)S(1)}, f32[1,128]{1,0:T(1,128)S(1)}, f32[4,128]{1,0:T(4,128)S(1)}) custom-call(f32[512,512]{1,0:T(8,128)} %bitcast.7, s32[1,2]{1,0:T(1,128)S(1)} %copy-done), custom_call_target="tpu_custom_call" | custom-call | bytes 1048576 | tf_op jit(solution)/shard_map/pallas_call | solution.py:388
  9.6 5.0 %collective-permute-done.2.rest_a = f32[128,512]{1,0:T(8,128)S(1)} collective-permute-done((f32[128,512]{1,0:T(8,128)S(1)}, f32[128,512]{1,0:T(8,128)S(1)}, u32[]{:S(2)}, u32[]{:S(2)}) %collective-permute-start.2) | collective-permute-done | bytes 262176 | tf_op jit(solution)/shard_map/ppermute | solution.py:69
  14.6 5.4 %collective-permute-done.4.rest_b = f32[128,512]{1,0:T(8,128)S(1)} collective-permute-done((f32[128,512]{1,0:T(8,128)S(1)}, f32[128,512]{1,0:T(8,128)S(1)}, u32[]{:S(2)}, u32[]{:S(2)}) %collective-permute-start.4) | collective-permute-done | bytes 262176 | tf_op jit(solution)/shard_map/ppermute | solution.py:69
  20.0 0.8 %shard_map.62 = (f32[264,512]{1,0:T(8,128)S(1)}, f32[32,2,128]{2,1,0:T(2,128)}) custom-call(f32[1,256,512]{2,1,0:T(8,128)S(1)} %get-tuple-element.27.keep, f32[1,256,512]{2,1,0:T(8,128)S(1)} %collective-permute-done.got, f32[128,512]{1,0:T(8,128)S(1)} %collective-permute-done.2.rest_a, f32[128,512]{1,0:T(8,128)S(1)} %collective-permute-done.4.rest_b, ...), custom_call_target="tpu_custom_call" | custom-call | bytes 1048576 | tf_op jit(solution)/shard_map/pallas_call | solution.py:395
  20.8 6.7 %all-to-all-start = ((f32[32,2,128]{2,1,0:T(2,128)}), f32[32,2,128]{2,1,0:T(2,128)S(1)}, u32[]{:S(2)}, u32[]{:S(2)}) async-start(f32[32,2,128]{2,1,0:T(2,128)} %get-tuple-element.41), calls=%async_computation | async-start | bytes 65536 | tf_op jit(solution)/shard_map/all_to_all | solution.py:399
  27.5 3.4 %shard_map.63 = (f32[2,128]{1,0:T(2,128)S(1)}, f32[264,512]{1,0:T(8,128)S(1)}, f32[264,512]{1,0:T(8,128)S(1)}, f32[264,512]{1,0:T(8,128)S(1)}, bf16[2,512,512]{2,1,0:T(8,128)(2,1)}) custom-call(f32[264,512]{1,0:T(8,128)S(1)} %get-tuple-element.34.half, ...), custom_call_target="tpu_custom_call", output_to_operand_aliasing={{3}: (0, {}), {2}: (1, {}), {1}: (2, {})} | custom-call | flops 2415919104 | bytes 1048576 | tf_op jit(solution)/shard_map/pallas_call | solution.py:400
  30.9 3.8 %all-to-all-done.sums = f32[32,2,128]{2,1,0:T(2,128)S(1)} async-done(((f32[32,2,128]{2,1,0:T(2,128)}), f32[32,2,128]{2,1,0:T(2,128)S(1)}, u32[]{:S(2)}, u32[]{:S(2)}) %all-to-all-start) | async-done | bytes 32800 | tf_op jit(solution)/shard_map/all_to_all | solution.py:399
  34.7 1.2 %shard_map.64 = (f32[384,512]{1,0:T(8,128)S(1)}, f32[1,128]{1,0:T(1,128)S(1)}, bf16[2,512,512]{2,1,0:T(8,128)(2,1)S(1)}) custom-call(f32[264,512]{1,0:T(8,128)S(1)} %get-tuple-element.36.stat, bf16[2,512,512]{2,1,0:T(8,128)(2,1)} %get-tuple-element.37.g_in, f32[264,512]{1,0:T(8,128)S(1)} %get-tuple-element.38.square, ...), custom_call_target="tpu_custom_call" | custom-call | flops 805306368 | bytes 1048576 | tf_op jit(solution)/shard_map/pallas_call | solution.py:410
  36.1 1.2 %shard_map.65.middle = bf16[2,512,512]{2,1,0:T(8,128)(2,1)S(1)} custom-call(bf16[2,512,512]{2,1,0:T(8,128)(2,1)S(1)} %get-tuple-element.42.g, f32[384,512]{1,0:T(8,128)S(1)} %get-tuple-element.43.packed), custom_call_target="tpu_custom_call" | custom-call | flops 805306368 | bytes 1048576 | tf_op jit(solution)/shard_map/pallas_call | solution.py:418
  37.3 1.0 %collective-permute-done.7.packed = f32[384,512]{1,0:T(8,128)S(1)} collective-permute-done((f32[384,512]{1,0:T(8,128)S(1)}, f32[384,512]{1,0:T(8,128)S(1)}, u32[]{:S(2)}, u32[]{:S(2)}) %collective-permute-start.7) | collective-permute-done | bytes 786464 | tf_op jit(solution)/shard_map/ppermute | solution.py:69
  39.7 1.4 %collective-permute-start.14 = (f32[264,512]{1,0:T(8,128)S(1)}, f32[264,512]{1,0:T(8,128)S(1)}, u32[]{:S(2)}, u32[]{:S(2)}) collective-permute-start(f32[264,512]{1,0:T(8,128)S(1)} %get-tuple-element.36.stat), channel_id=1, source_target_pairs={{8,0},{24,8},{0,16},{16,24},{9,1},{25,9},{1,17},{17,25},{10,2},{26... | collective-permute-start | bytes 1622024 | tf_op jit(solution)/shard_map/ppermute | solution.py:409
  41.1 10.0 %collective-permute-done.12.refs_1_ = f32[192,512]{1,0:T(8,128)S(1)} collective-permute-done((f32[192,512]{1,0:T(8,128)S(1)}, f32[192,512]{1,0:T(8,128)S(1)}, u32[]{:S(2)}, u32[]{:S(2)}) %collective-permute-start.12) | collective-permute-done | bytes 393248 | tf_op jit(solution)/shard_map/ppermute | solution.py:69
  51.0 6.4 %collective-permute-done.8.refs_3_ = f32[64,512]{1,0:T(8,128)S(1)} collective-permute-done((f32[64,512]{1,0:T(8,128)S(1)}, f32[64,512]{1,0:T(8,128)S(1)}, u32[]{:S(2)}, u32[]{:S(2)}) %collective-permute-start.8) | collective-permute-done | bytes 131104 | tf_op jit(solution)/shard_map/ppermute | solution.py:69
  57.4 1.2 %collective-permute-start.9 = (f32[64,512]{1,0:T(8,128)S(1)}, f32[64,512]{1,0:T(8,128)S(1)}, u32[]{:S(2)}, u32[]{:S(2)}) collective-permute-start(f32[64,512]{1,0:T(8,128)S(1)} %collective-permute-done.8.refs_3_), channel_id=1, source_target_pairs={{0,8},{8,0},{16,24},{24,16},{1,9},{9,1},{17,25},{25,17},{2,10},{10... | collective-permute-start | bytes 393224 | tf_op jit(solution)/shard_map/ppermute | solution.py:69
  58.6 0.8 %collective-permute-start.10 = (f32[16,1,128]{2,1,0:T(1,128)S(1)}, f32[16,1,128]{2,1,0:T(1,128)S(1)}, u32[]{:S(2)}, u32[]{:S(2)}) collective-permute-start(f32[16,1,128]{2,1,0:T(1,128)S(1)} %get-tuple-element.46), channel_id=1, source_target_pairs={{0,16},{8,24},{16,0},{24,8},{1,17},{9,25},{17,1},{25,9},{2,18},{10... | collective-permute-start | bytes 24584 | tf_op jit(solution)/shard_map/ppermute | solution.py:69
  59.4 2.8 %collective-permute-done.10 = f32[16,1,128]{2,1,0:T(1,128)S(1)} collective-permute-done((f32[16,1,128]{2,1,0:T(1,128)S(1)}, f32[16,1,128]{2,1,0:T(1,128)S(1)}, u32[]{:S(2)}, u32[]{:S(2)}) %collective-permute-start.10) | collective-permute-done | bytes 8224 | tf_op jit(solution)/shard_map/ppermute | solution.py:69
  62.9 3.8 %all-to-all-start.1 = ((f32[16,1,128]{2,1,0:T(1,128)}), f32[16,1,128]{2,1,0:T(1,128)S(1)}, u32[]{:S(2)}, u32[]{:S(2)}) async-start(f32[16,1,128]{2,1,0:T(1,128)} %add.19), calls=%async_computation.1 | async-start | bytes 16384 | tf_op jit(solution)/shard_map/all_to_all | solution.py:438
  66.7 1.2 %shard_map.70 = f32[512,512]{1,0:T(8,128)} custom-call(f32[264,512]{1,0:T(8,128)S(1)} %collective-permute-done.14.packed), custom_call_target="tpu_custom_call" | custom-call | bytes 1048576 | tf_op jit(solution)/shard_map/pallas_call | solution.py:439
  67.9 3.8 %all-to-all-done.1.refs_1_ = f32[16,1,128]{2,1,0:T(1,128)S(1)} async-done(((f32[16,1,128]{2,1,0:T(1,128)}), f32[16,1,128]{2,1,0:T(1,128)S(1)}, u32[]{:S(2)}, u32[]{:S(2)}) %all-to-all-start.1) | async-done | bytes 8224 | tf_op jit(solution)/shard_map/all_to_all | solution.py:438
  71.7 1.0 %shard_map.67 = (f32[1024,512]{1,0:T(8,128)}, f32[1,128]{1,0:T(1,128)S(1)}) custom-call(f32[256,512]{1,0:T(8,128)S(1)} %get-tuple-element.45.refs_0_, f32[16,1,128]{2,1,0:T(1,128)S(1)} %all-to-all-done.1.refs_1_, f32[1,128]{1,0:T(1,128)S(1)} %get-tuple-element.47.refs_2_, f32[4,128]{1,0:T(4,128)S(1)} %get-tuple-element.48.refs_3_.refs_5_.refs_2_), custom_call_target="tpu_custom_call" | custom-call | bytes 1048576 | tf_op jit(solution)/shard_map/pallas_call | solution.py:459
  72.7 1.3 %shard_map.68.refs_3_ = f32[1024,512]{1,0:T(8,128)} custom-call(f32[256,512]{1,0:T(8,128)S(1)} %collective-permute-done.11.refs_0_, f32[192,512]{1,0:T(8,128)S(1)} %collective-permute-done.12.refs_1_, f32[192,512]{1,0:T(8,128)S(1)} %collective-permute-done.13.refs_2_, f32[64,512]{1,0:T(8,128)S(1)} %collective-permute-done.8.refs_3_, ...), custom_call_target="tpu_custom_call", output_to_operand_aliasing={{}: (6, {})} | custom-call | bytes 1048576 | tf_op jit(solution)/shard_map/pallas_call | solution.py:447
  (27 shorter events, 4.4 us)
Async XLA Ops:
  0.6 7.0 %copy-start = (s32[1,2]{1,0:T(1,128)S(1)}, s32[1,2]{1,0:T(1,128)}, u32[]{:S(2)}) copy-start(s32[1,2]{1,0:T(1,128)} %owners.5) | copy-start | bytes 28
  2.2 2.6 %collective-permute-start.1 = (f32[1,128,512]{2,1,0:T(8,128)S(1)}, f32[1,128,512]{2,1,0:T(8,128)S(1)}, u32[]{:S(2)}, u32[]{:S(2)}) collective-permute-start(f32[1,128,512]{2,1,0:T(8,128)S(1)} %get-tuple-element.30), channel_id=1, source_target_pairs={{0,8},{8,0},{16,24},{24,16},{1,9},{9,1},{17,25},{25,17},{2,10},{10... | collective-permute-start | bytes 786440 | tf_op jit(solution)/shard_map/ppermute | solution.py:69
  2.7 4.7 %collective-permute-start.3 = (f32[1,128,512]{2,1,0:T(8,128)S(1)}, f32[1,128,512]{2,1,0:T(8,128)S(1)}, u32[]{:S(2)}, u32[]{:S(2)}) collective-permute-start(f32[1,128,512]{2,1,0:T(8,128)S(1)} %get-tuple-element.32), channel_id=1, source_target_pairs={{0,8},{8,0},{16,24},{24,16},{1,9},{9,1},{17,25},{25,17},{2,10},{10... | collective-permute-start | bytes 786440 | tf_op jit(solution)/shard_map/ppermute | solution.py:69
  4.3 15.7 %collective-permute-start = (f32[1,256,512]{2,1,0:T(8,128)S(1)}, f32[1,256,512]{2,1,0:T(8,128)S(1)}, u32[]{:S(2)}, u32[]{:S(2)}) collective-permute-start(f32[1,256,512]{2,1,0:T(8,128)S(1)} %get-tuple-element.28), channel_id=1, source_target_pairs={{0,8},{8,0},{16,24},{24,16},{1,9},{9,1},{17,25},{25,17},{2,10},{10... | collective-permute-start | bytes 1572872 | tf_op jit(solution)/shard_map/ppermute | solution.py:69
  4.8 9.8 %collective-permute-start.2 = (f32[128,512]{1,0:T(8,128)S(1)}, f32[128,512]{1,0:T(8,128)S(1)}, u32[]{:S(2)}, u32[]{:S(2)}) collective-permute-start(f32[128,512]{1,0:T(8,128)S(1)} %add_bitcast_fusion.1), channel_id=1, source_target_pairs={{0,16},{8,24},{16,0},{24,8},{1,17},{9,25},{17,1},{25,9},{2,18},{10... | collective-permute-start | bytes 786440 | tf_op jit(solution)/shard_map/ppermute | solution.py:69
  7.5 12.5 %collective-permute-start.4 = (f32[128,512]{1,0:T(8,128)S(1)}, f32[128,512]{1,0:T(8,128)S(1)}, u32[]{:S(2)}, u32[]{:S(2)}) collective-permute-start(f32[128,512]{1,0:T(8,128)S(1)} %add_bitcast_fusion), channel_id=1, source_target_pairs={{0,16},{8,24},{16,0},{24,8},{1,17},{9,25},{17,1},{25,9},{2,18},{10... | collective-permute-start | bytes 786440 | tf_op jit(solution)/shard_map/ppermute | solution.py:69
  9.4 18.1 %collective-permute-start.6 = (f32[264,512]{1,0:T(8,128)S(1)}, f32[264,512]{1,0:T(8,128)S(1)}, u32[]{:S(2)}, u32[]{:S(2)}) collective-permute-start(f32[264,512]{1,0:T(8,128)S(1)} %get-tuple-element.35), channel_id=1, source_target_pairs={{0,8},{8,24},{16,0},{24,16},{1,9},{9,25},{17,1},{25,17},{2,10},{10... | collective-permute-start | bytes 1622024 | tf_op jit(solution)/shard_map/ppermute | solution.py:394
  20.8 6.8 %collective-permute-start.5 = (f32[264,512]{1,0:T(8,128)S(1)}, f32[264,512]{1,0:T(8,128)S(1)}, u32[]{:S(2)}, u32[]{:S(2)}) collective-permute-start(f32[264,512]{1,0:T(8,128)S(1)} %get-tuple-element.34.half), channel_id=1, source_target_pairs={{0,8},{8,0},{16,24},{24,16},{1,9},{9,1},{17,25},{25,17},{2,10},{10... | collective-permute-start | bytes 1622024 | tf_op jit(solution)/shard_map/ppermute | solution.py:69
  20.8 13.9 %all-to-all-start = ((f32[32,2,128]{2,1,0:T(2,128)}), f32[32,2,128]{2,1,0:T(2,128)S(1)}, u32[]{:S(2)}, u32[]{:S(2)}) async-start(f32[32,2,128]{2,1,0:T(2,128)} %get-tuple-element.41), calls=%async_computation | async-start | bytes 65536 | tf_op jit(solution)/shard_map/all_to_all | solution.py:399
  35.9 2.4 %collective-permute-start.7 = (f32[384,512]{1,0:T(8,128)S(1)}, f32[384,512]{1,0:T(8,128)S(1)}, u32[]{:S(2)}, u32[]{:S(2)}) collective-permute-start(f32[384,512]{1,0:T(8,128)S(1)} %get-tuple-element.43.packed), channel_id=1, source_target_pairs={{0,8},{8,0},{16,24},{24,16},{1,9},{9,1},{17,25},{25,17},{2,10},{10... | collective-permute-start | bytes 2359304 | tf_op jit(solution)/shard_map/ppermute | solution.py:69
  39.0 12.1 %collective-permute-start.12 = (f32[192,512]{1,0:T(8,128)S(1)}, f32[192,512]{1,0:T(8,128)S(1)}, u32[]{:S(2)}, u32[]{:S(2)}) collective-permute-start(f32[192,512]{1,0:T(8,128)S(1)} %get-tuple-element.50), channel_id=1, source_target_pairs={{0,16},{8,24},{16,0},{24,8},{1,17},{9,25},{17,1},{25,9},{2,18},{10... | collective-permute-start | bytes 1179656 | tf_op jit(solution)/shard_map/ppermute | solution.py:69
  39.7 27.0 %collective-permute-start.14 = (f32[264,512]{1,0:T(8,128)S(1)}, f32[264,512]{1,0:T(8,128)S(1)}, u32[]{:S(2)}, u32[]{:S(2)}) collective-permute-start(f32[264,512]{1,0:T(8,128)S(1)} %get-tuple-element.36.stat), channel_id=1, source_target_pairs={{8,0},{24,8},{0,16},{16,24},{9,1},{25,9},{1,17},{17,25},{10,2},{26... | collective-permute-start | bytes 1622024 | tf_op jit(solution)/shard_map/ppermute | solution.py:409
  41.1 31.6 %collective-permute-start.11 = (f32[256,512]{1,0:T(8,128)S(1)}, f32[256,512]{1,0:T(8,128)S(1)}, u32[]{:S(2)}, u32[]{:S(2)}) collective-permute-start(f32[256,512]{1,0:T(8,128)S(1)} %get-tuple-element.45.refs_0_), channel_id=1, source_target_pairs={{0,8},{8,0},{16,24},{24,16},{1,9},{9,1},{17,25},{25,17},{2,10},{10... | collective-permute-start | bytes 1572872 | tf_op jit(solution)/shard_map/ppermute | solution.py:69
  51.0 21.7 %collective-permute-start.13 = (f32[192,512]{1,0:T(8,128)S(1)}, f32[192,512]{1,0:T(8,128)S(1)}, u32[]{:S(2)}, u32[]{:S(2)}) collective-permute-start(f32[192,512]{1,0:T(8,128)S(1)} %collective-permute-done.12.refs_1_), channel_id=1, source_target_pairs={{0,8},{8,0},{16,24},{24,16},{1,9},{9,1},{17,25},{25,17},{2,10},{10... | collective-permute-start | bytes 1179656 | tf_op jit(solution)/shard_map/ppermute | solution.py:69
  51.0 6.4 %collective-permute-start.8 = (f32[64,512]{1,0:T(8,128)S(1)}, f32[64,512]{1,0:T(8,128)S(1)}, u32[]{:S(2)}, u32[]{:S(2)}) collective-permute-start(f32[64,512]{1,0:T(8,128)S(1)} %get-tuple-element.44), channel_id=1, source_target_pairs={{0,16},{8,24},{16,0},{24,8},{1,17},{9,25},{17,1},{25,9},{2,18},{10... | collective-permute-start | bytes 393224 | tf_op jit(solution)/shard_map/ppermute | solution.py:69
  57.4 16.6 %collective-permute-start.9 = (f32[64,512]{1,0:T(8,128)S(1)}, f32[64,512]{1,0:T(8,128)S(1)}, u32[]{:S(2)}, u32[]{:S(2)}) collective-permute-start(f32[64,512]{1,0:T(8,128)S(1)} %collective-permute-done.8.refs_3_), channel_id=1, source_target_pairs={{0,8},{8,0},{16,24},{24,16},{1,9},{9,1},{17,25},{25,17},{2,10},{10... | collective-permute-start | bytes 393224 | tf_op jit(solution)/shard_map/ppermute | solution.py:69
  58.6 3.7 %collective-permute-start.10 = (f32[16,1,128]{2,1,0:T(1,128)S(1)}, f32[16,1,128]{2,1,0:T(1,128)S(1)}, u32[]{:S(2)}, u32[]{:S(2)}) collective-permute-start(f32[16,1,128]{2,1,0:T(1,128)S(1)} %get-tuple-element.46), channel_id=1, source_target_pairs={{0,16},{8,24},{16,0},{24,8},{1,17},{9,25},{17,1},{25,9},{2,18},{10... | collective-permute-start | bytes 24584 | tf_op jit(solution)/shard_map/ppermute | solution.py:69
  62.9 8.8 %all-to-all-start.1 = ((f32[16,1,128]{2,1,0:T(1,128)}), f32[16,1,128]{2,1,0:T(1,128)S(1)}, u32[]{:S(2)}, u32[]{:S(2)}) async-start(f32[16,1,128]{2,1,0:T(1,128)} %add.19), calls=%async_computation.1 | async-start | bytes 16384 | tf_op jit(solution)/shard_map/all_to_all | solution.py:438
